TPU v7x, 32 devices: a whole 2x2x4 slice. The times are simulated.
32 devices in a mesh: seq: 16 (over z, y, x), head: 2 (over core).
Axes of the slice: x: 2, y: 2, z: 4, core: 2. Of those that a mesh axis runs over, the one named last changes fastest.
Arguments:
- block_input: bfloat16 [2048, 2560], P('seq'), may hold values from -6 to 6
- first_gain: bfloat16 [2560], P('seq'), may hold values from 0.5 to 1.5
- gelu_weight: bfloat16 [2560, 2560], P('seq', 'head'), may hold values from -0.125 to 0.125
- scan_weight: bfloat16 [2560, 2560], P('seq', 'head'), may hold values from -0.125 to 0.125
- filter_taps: bfloat16 [4, 10, 256], P(None, 'head', 'seq'), may hold values from -3 to 3
- input_gate: bfloat16 [10, 256, 256], P('head', 'seq'), may hold values from -0.375 to 0.375
- input_bias: bfloat16 [10, 256], P('head', 'seq'), may hold values from -4 to 4
- decay_gate: bfloat16 [10, 256, 256], P('head', 'seq'), may hold values from -0.375 to 0.375
- decay_bias: bfloat16 [10, 256], P('head', 'seq'), may hold values from -4 to 4
- decay_param: bfloat16 [10, 256], P('head', 'seq'), may hold values from -11 to -3
- output_weight: bfloat16 [2560, 2560], P('head', 'seq'), may hold values from -0.125 to 0.125
- second_gain: bfloat16 [2560], P('seq'), may hold values from 0.5 to 1.5
- expand_gate: bfloat16 [2560, 7680], P('seq', 'head'), may hold values from -0.125 to 0.125
- expand_value: bfloat16 [2560, 7680], P('seq', 'head'), may hold values from -0.125 to 0.125
- contract_weight: bfloat16 [7680, 2560], P('head', 'seq'), may hold values from -0.0625 to 0.0625
- output_cotangent: bfloat16 [2048, 2560], P('seq'), may hold values from -6 to 6
Outputs:
- block_output: bfloat16 [2048, 2560], P('seq')
- input_gradient: float32 [2048, 2560], P('seq')
- first_gain_gradient: float32 [2560], P('seq')
- gelu_weight_gradient: float32 [2560, 2560], P('seq', 'head')
- scan_weight_gradient: float32 [2560, 2560], P('seq', 'head')
- filter_taps_gradient: float32 [4, 10, 256], P(None, 'head', 'seq')
- input_gate_gradient: float32 [10, 256, 256], P('head', 'seq')
- input_bias_gradient: float32 [10, 256], P('head', 'seq')
- decay_gate_gradient: float32 [10, 256, 256], P('head', 'seq')
- decay_bias_gradient: float32 [10, 256], P('head', 'seq')
- decay_param_gradient: float32 [10, 256], P('head', 'seq')
- output_weight_gradient: float32 [2560, 2560], P('head', 'seq')
- second_gain_gradient: float32 [2560], P('seq')
- expand_gate_gradient: float32 [2560, 7680], P('seq', 'head')
- expand_value_gradient: float32 [2560, 7680], P('seq', 'head')
- contract_weight_gradient: float32 [7680, 2560], P('head', 'seq')
All inputs are finite; a program needn't handle non-finite values.
Results may differ from a plain program's by a relative error of at most 0.017.
Values may be sent and summed in bfloat16 or wider, within the bound.
No kernel may reach another device: no remote copies, remote signals or barrier semaphores. Data moves between devices by JAX's collectives and lax.ppermute only.
A program may use at most 384 MiB of HBM per device.

v0:
```python
import jax
import jax.numpy as jnp
from jax import lax
from jax.sharding import PartitionSpec as P

EPSILON = 1e-06


def passed_along(value, axis, steps):
    count = lax.axis_size(axis)
    leading, last = (max(0, -steps), min(count, count - steps))
    return lax.ppermute(value, axis, [(source, source + steps) for source in range(leading, last)])


def carried_in(part, axis, combine, identity, reverse):
    count = lax.axis_size(axis)
    place = lax.axis_index(axis)
    ahead = count - 1 - place if reverse else place
    gathered = jax.tree.map(lambda a: lax.all_gather(a, axis), part)
    state = jax.tree.map(lambda a, e: jnp.zeros_like(a) + jnp.asarray(e, a.dtype), part, identity)

    def one(lap, state):
        source = count - 1 - lap if reverse else lap
        return combine(
            state, jax.tree.map(lambda a: lax.dynamic_index_in_dim(a, source, 0, False), gathered)
        )

    return lax.fori_loop(0, ahead, one, state)


def root_norm(values, gain_row):
    return (
        values * lax.rsqrt(jnp.mean(values * values, axis=-1, keepdims=True) + EPSILON) * gain_row
    )


def gating(pre_input, pre_decay, decay_param, filtered):
    input_open = jax.nn.sigmoid(pre_input)
    decay_open = jax.nn.sigmoid(pre_decay)
    log_decay = -8.0 * decay_open * jax.nn.softplus(decay_param)
    decay_rate = jnp.exp(log_decay)
    return (decay_rate, jnp.sqrt(-jnp.expm1(2.0 * log_decay)) * input_open * filtered)


def linked(earlier, latter):
    return (earlier[0] * latter[0], latter[0] * earlier[1] + latter[1])


def across(left_matrix, right_matrix):
    return lax.dot_general(
        left_matrix, right_matrix, (((0,), (0,)), ((), ())), preferred_element_type=jnp.float32
    )


def against(left_matrix, right_matrix):
    return lax.dot_general(
        left_matrix, right_matrix, (((1,), (1,)), ((), ())), preferred_element_type=jnp.float32
    )


def forward_dot(left_matrix, right_matrix):
    return jnp.dot(left_matrix, right_matrix, preferred_element_type=jnp.float32)


def shards(
    block_input,
    first_gain,
    gelu_weight,
    scan_weight,
    filter_taps,
    input_gate,
    input_bias,
    decay_gate,
    decay_bias,
    decay_param,
    output_weight,
    second_gain,
    expand_gate,
    expand_value,
    contract_weight,
    output_cotangent,
):
    (
        gain_first,
        weight_gelu,
        weight_scan,
        taps_whole,
        gate_input,
        bias_input,
        gate_decay,
        bias_decay,
        param_whole,
        weight_output,
    ) = (
        lax.all_gather(first_gain, "seq", axis=0, tiled=True),
        lax.all_gather(gelu_weight, "seq", axis=0, tiled=True),
        lax.all_gather(scan_weight, "seq", axis=0, tiled=True),
        lax.all_gather(filter_taps, "seq", axis=2, tiled=True),
        lax.all_gather(input_gate, "seq", axis=1, tiled=True),
        lax.all_gather(input_bias, "seq", axis=1, tiled=True),
        lax.all_gather(decay_gate, "seq", axis=1, tiled=True),
        lax.all_gather(decay_bias, "seq", axis=1, tiled=True),
        lax.all_gather(decay_param, "seq", axis=1, tiled=True),
        lax.all_gather(output_weight, "seq", axis=1, tiled=True),
    )
    token_count = block_input.shape[0]
    local_blocks = gate_input.shape[0]
    block_width = gate_input.shape[2]
    channels = local_blocks * block_width
    tap_count = taps_whole.shape[0]
    residual = block_input.astype(jnp.float32)
    normed_f, first_back = jax.vjp(root_norm, residual, gain_first.astype(jnp.float32))
    normed = normed_f.astype(jnp.bfloat16)
    gelu_pre = forward_dot(normed, weight_gelu)
    branch = forward_dot(normed, weight_scan)
    previous = passed_along(branch[token_count - tap_count + 1 :], "seq", 1)
    padded = jnp.concatenate([previous, branch], axis=0)
    tap_rows = taps_whole.astype(jnp.float32).reshape(tap_count, channels)
    filtered = jnp.zeros_like(branch)
    for offset in range(tap_count):
        filtered = (
            filtered
            + tap_rows[offset]
            * padded[tap_count - 1 - offset : tap_count - 1 - offset + token_count]
        )
    filtered_low = filtered.astype(jnp.bfloat16)
    shaped = filtered_low.reshape(token_count, local_blocks, block_width)
    pre_input = jnp.einsum(
        "thi,hij->thj", shaped, gate_input, preferred_element_type=jnp.float32
    ).reshape(token_count, channels) + bias_input.astype(jnp.float32).reshape(-1)
    pre_decay = jnp.einsum(
        "thi,hij->thj", shaped, gate_decay, preferred_element_type=jnp.float32
    ).reshape(token_count, channels) + bias_decay.astype(jnp.float32).reshape(-1)
    param_row = param_whole.astype(jnp.float32).reshape(-1)
    (decay_rate, update), gating_back = jax.vjp(gating, pre_input, pre_decay, param_row, filtered)
    local_prod, local_state = lax.associative_scan(linked, (decay_rate, update), axis=0)
    ones_row = jnp.ones((channels,), jnp.float32)
    zeros_row = jnp.zeros((channels,), jnp.float32)
    _, carry_state = carried_in(
        (local_prod[-1], local_state[-1]), "seq", linked, (ones_row, zeros_row), False
    )
    states = local_state + local_prod * carry_state
    gelu_out, gelu_back = jax.vjp(jax.nn.gelu, gelu_pre)
    merged = (states * gelu_out).astype(jnp.bfloat16)
    middle = residual + lax.psum(
        forward_dot(merged, weight_output).astype(jnp.bfloat16), "head"
    ).astype(jnp.float32)
    gain_second, weight_expand, weight_value, weight_contract = (
        lax.all_gather(second_gain, "seq", axis=0, tiled=True),
        lax.all_gather(expand_gate, "seq", axis=0, tiled=True),
        lax.all_gather(expand_value, "seq", axis=0, tiled=True),
        lax.all_gather(contract_weight, "seq", axis=1, tiled=True),
    )
    second_f, second_back = jax.vjp(root_norm, middle, gain_second.astype(jnp.float32))
    second = second_f.astype(jnp.bfloat16)
    gate_pre = forward_dot(second, weight_expand)
    value_pre = forward_dot(second, weight_value)
    gate_act, gate_back = jax.vjp(jax.nn.gelu, gate_pre)
    hidden = (gate_act * value_pre).astype(jnp.bfloat16)
    block_output = (
        middle
        + lax.psum(forward_dot(hidden, weight_contract).astype(jnp.bfloat16), "head").astype(
            jnp.float32
        )
    ).astype(jnp.bfloat16)
    gain_second, weight_expand, weight_value, weight_contract = (
        lax.all_gather(second_gain, "seq", axis=0, tiled=True),
        lax.all_gather(expand_gate, "seq", axis=0, tiled=True),
        lax.all_gather(expand_value, "seq", axis=0, tiled=True),
        lax.all_gather(contract_weight, "seq", axis=1, tiled=True),
    )
    cotangent = output_cotangent.astype(jnp.float32)
    hidden_grad = against(output_cotangent, weight_contract)
    gate_grad = gate_back(hidden_grad * value_pre)[0].astype(jnp.bfloat16)
    value_grad = (hidden_grad * gate_act).astype(jnp.bfloat16)
    second_grad = lax.psum(
        (against(gate_grad, weight_expand) + against(value_grad, weight_value)).astype(
            jnp.bfloat16
        ),
        "head",
    ).astype(jnp.float32)
    middle_part, second_gain_grad = second_back(second_grad)
    middle_grad = cotangent + middle_part
    expand_grad = across(second, gate_grad)
    value_wgrad = across(second, value_grad)
    contract_grad = across(hidden, output_cotangent)
    second_gain_gradient, expand_gate_gradient, expand_value_gradient, contract_weight_gradient = (
        lax.psum_scatter(second_gain_grad, "seq", scatter_dimension=0, tiled=True),
        lax.psum_scatter(expand_grad, "seq", scatter_dimension=0, tiled=True),
        lax.psum_scatter(value_wgrad, "seq", scatter_dimension=0, tiled=True),
        lax.psum_scatter(contract_grad, "seq", scatter_dimension=1, tiled=True),
    )
    (
        gain_first,
        weight_gelu,
        weight_scan,
        taps_whole,
        gate_input,
        bias_input,
        gate_decay,
        bias_decay,
        param_whole,
        weight_output,
    ) = (
        lax.all_gather(first_gain, "seq", axis=0, tiled=True),
        lax.all_gather(gelu_weight, "seq", axis=0, tiled=True),
        lax.all_gather(scan_weight, "seq", axis=0, tiled=True),
        lax.all_gather(filter_taps, "seq", axis=2, tiled=True),
        lax.all_gather(input_gate, "seq", axis=1, tiled=True),
        lax.all_gather(input_bias, "seq", axis=1, tiled=True),
        lax.all_gather(decay_gate, "seq", axis=1, tiled=True),
        lax.all_gather(decay_bias, "seq", axis=1, tiled=True),
        lax.all_gather(decay_param, "seq", axis=1, tiled=True),
        lax.all_gather(output_weight, "seq", axis=1, tiled=True),
    )
    tap_rows = taps_whole.astype(jnp.float32).reshape(tap_count, channels)
    middle_low = middle_grad.astype(jnp.bfloat16)
    merged_grad = against(middle_low, weight_output)
    output_wgrad = across(merged, middle_low)
    local_grad = merged_grad * gelu_out
    gelu_pre_grad = gelu_back(merged_grad * states)[0].astype(jnp.bfloat16)
    next_decay = jnp.concatenate([decay_rate[1:], jnp.ones((1, channels), jnp.float32)], axis=0)
    tail_prod, tail_state = lax.associative_scan(
        linked, (next_decay, local_grad), reverse=True, axis=0
    )
    first_decay = decay_rate[0]
    _, carry_grad = carried_in(
        (first_decay * tail_prod[0], first_decay * tail_state[0]),
        "seq",
        linked,
        (ones_row, zeros_row),
        True,
    )
    state_grad = tail_state + tail_prod * carry_grad
    previous_state = jnp.concatenate([carry_state[None], states[:-1]], axis=0)
    input_pre_grad, decay_pre_grad, param_grad, filtered_grad = gating_back(
        (state_grad * previous_state, state_grad)
    )
    input_low = input_pre_grad.astype(jnp.bfloat16).reshape(token_count, local_blocks, block_width)
    decay_low = decay_pre_grad.astype(jnp.bfloat16).reshape(token_count, local_blocks, block_width)
    input_wgrad = jnp.einsum("thi,thj->hij", shaped, input_low, preferred_element_type=jnp.float32)
    decay_wgrad = jnp.einsum("thi,thj->hij", shaped, decay_low, preferred_element_type=jnp.float32)
    filtered_grad = filtered_grad + (
        jnp.einsum("thj,hij->thi", input_low, gate_input, preferred_element_type=jnp.float32)
        + jnp.einsum("thj,hij->thi", decay_low, gate_decay, preferred_element_type=jnp.float32)
    ).reshape(token_count, channels)
    following = passed_along(filtered_grad[: tap_count - 1], "seq", -1)
    extended = jnp.concatenate([filtered_grad, following], axis=0)
    branch_grad = jnp.zeros_like(filtered_grad)
    tap_terms = []
    for offset in range(tap_count):
        branch_grad = branch_grad + tap_rows[offset] * extended[offset : offset + token_count]
        tap_terms.append(
            jnp.sum(
                filtered_grad
                * padded[tap_count - 1 - offset : tap_count - 1 - offset + token_count],
                axis=0,
            )
        )
    taps_grad = jnp.stack(tap_terms, axis=0).reshape(tap_count, local_blocks, block_width)
    branch_low = branch_grad.astype(jnp.bfloat16)
    gelu_wgrad = across(normed, gelu_pre_grad)
    scan_wgrad = across(normed, branch_low)
    normed_grad = lax.psum(
        (against(gelu_pre_grad, weight_gelu) + against(branch_low, weight_scan)).astype(
            jnp.bfloat16
        ),
        "head",
    ).astype(jnp.float32)
    input_part, first_gain_grad = first_back(normed_grad)
    input_gradient = middle_grad + input_part
    (
        first_gain_gradient,
        gelu_weight_gradient,
        scan_weight_gradient,
        filter_taps_gradient,
        input_gate_gradient,
        input_bias_gradient,
        decay_gate_gradient,
        decay_bias_gradient,
        decay_param_gradient,
        output_weight_gradient,
    ) = (
        lax.psum_scatter(first_gain_grad, "seq", scatter_dimension=0, tiled=True),
        lax.psum_scatter(gelu_wgrad, "seq", scatter_dimension=0, tiled=True),
        lax.psum_scatter(scan_wgrad, "seq", scatter_dimension=0, tiled=True),
        lax.psum_scatter(taps_grad, "seq", scatter_dimension=2, tiled=True),
        lax.psum_scatter(input_wgrad, "seq", scatter_dimension=1, tiled=True),
        lax.psum_scatter(
            jnp.sum(input_pre_grad, axis=0).reshape(local_blocks, block_width),
            "seq",
            scatter_dimension=1,
            tiled=True,
        ),
        lax.psum_scatter(decay_wgrad, "seq", scatter_dimension=1, tiled=True),
        lax.psum_scatter(
            jnp.sum(decay_pre_grad, axis=0).reshape(local_blocks, block_width),
            "seq",
            scatter_dimension=1,
            tiled=True,
        ),
        lax.psum_scatter(
            param_grad.reshape(local_blocks, block_width), "seq", scatter_dimension=1, tiled=True
        ),
        lax.psum_scatter(output_wgrad, "seq", scatter_dimension=1, tiled=True),
    )
    return (
        block_output,
        input_gradient,
        first_gain_gradient,
        gelu_weight_gradient,
        scan_weight_gradient,
        filter_taps_gradient,
        input_gate_gradient,
        input_bias_gradient,
        decay_gate_gradient,
        decay_bias_gradient,
        decay_param_gradient,
        output_weight_gradient,
        second_gain_gradient,
        expand_gate_gradient,
        expand_value_gradient,
        contract_weight_gradient,
    )


def solution(mesh):
    in_specs = (
        P("seq", None),
        P("seq"),
        P("seq", "head"),
        P("seq", "head"),
        P(None, "head", "seq"),
        P("head", "seq", None),
        P("head", "seq"),
        P("head", "seq", None),
        P("head", "seq"),
        P("head", "seq"),
        P("head", "seq"),
        P("seq"),
        P("seq", "head"),
        P("seq", "head"),
        P("head", "seq"),
        P("seq", None),
    )
    out_specs = (
        P("seq", None),
        P("seq", None),
        P("seq"),
        P("seq", "head"),
        P("seq", "head"),
        P(None, "head", "seq"),
        P("head", "seq", None),
        P("head", "seq"),
        P("head", "seq", None),
        P("head", "seq"),
        P("head", "seq"),
        P("head", "seq"),
        P("seq"),
        P("seq", "head"),
        P("seq", "head"),
        P("head", "seq"),
    )
    return jax.shard_map(shards, mesh=mesh, in_specs=in_specs, out_specs=out_specs, check_vma=False)
```

profile of v0, /device:TPU:5, one launch (start us, length us, event | category | flops | bytes accessed | tf_op | source)
XLA Modules:
  0.0 4502.4 jit_solution(17706490492475276257)
XLA Ops:
  13.2 61.4 %all-reduce.63 = (bf16[2560]{0:T(1024)(128)(2,1)S(1)}, bf16[2560]{0:T(1024)(128)(2,1)}) all-reduce(bf16[2560]{0:T(1024)(128)(2,1)S(1)} %dynamic-update-slice, bf16[2560]{0:T(1024)(128)(2,1)S(1)} %dynamic-update-slice.1), channel_id=1, replica_groups=mesh['seq'=16,'head'=2] {'seq'}, use_global_device_ids=true, to_apply=%add.58 | all-reduce | flops 5120 | bytes 20480
  75.3 32.0 all_gather.65
  107.8 35.4 all_gather.71
  143.2 40.6 all_gather.68
  183.8 29.1 all-gather.1
  213.6 31.3 all-gather
  244.8 29.6 all-gather.2
  385.5 26.8 all-gather.4
  420.3 29.5 all-gather.3
  450.5 5.8 multiply_convert_fusion.3
  456.4 6.1 convolution_convert_fusion.1
  467.2 5.5 slice.565
  479.0 74.9 %all-reduce.69.cloned.1.call-done = bf16[128,2560]{1,0:T(8,128)(2,1)} async-done(((bf16[128,2560]{1,0:T(8,128)(2,1)}), bf16[128,2560]{1,0:T(8,128)(2,1)}) %all-reduce.69.cloned.1.call-update) | async-done | bytes 655376 | tf_op jit(solution)/shard_map/psum | solution.py:145
  555.6 220.3 %all-gather.20.cloned.1.call-done = bf16[2560,3840]{1,0:T(8,128)(2,1)} async-done(((bf16[160,3840]{1,0:T(8,128)(2,1)}), bf16[2560,3840]{1,0:T(8,128)(2,1)}) %all-gather.20.cloned.1.call-update) | async-done | bytes 19660816 | tf_op jit(solution)/shard_map/all_gather | solution.py:150
  775.9 10.6 fusion.103
  786.5 209.6 %all-gather.22.cloned.1.call-done = bf16[2560,3840]{1,0:T(8,128)(2,1)} async-done(((bf16[160,3840]{1,0:T(8,128)(2,1)}), bf16[2560,3840]{1,0:T(8,128)(2,1)}) %all-gather.22.cloned.1.call-update) | async-done | bytes 19660816 | tf_op jit(solution)/shard_map/all_gather | solution.py:151
  996.1 10.6 fusion.104
  1006.7 209.7 %all-gather.24.cloned.1.call-done = bf16[3840,2560]{0,1:T(8,128)(2,1)} async-done(((bf16[3840,160]{0,1:T(8,128)(2,1)}), bf16[3840,2560]{0,1:T(8,128)(2,1)}) %all-gather.24.cloned.1.call-update) | async-done | bytes 19660816 | tf_op jit(solution)/shard_map/all_gather | solution.py:152
  1216.4 13.4 multiply_convert_fusion
  1229.8 14.4 fusion.105
  1244.2 11.4 fusion
  1255.7 14.3 convolution_convert_fusion
  1276.6 5.5 fusion.51
  1362.3 30.2 all-gather.5
  1392.5 29.0 all-gather.6
  1422.8 4.5 rev.9
  1427.2 5.9 rev.8
  1444.8 4.5 multiply_reduce_fusion.4
  1453.9 7.2 collective-permute-start.1
  1461.3 5.3 fusion.106
  1476.0 6.9 fusion.47
  1483.9 6.7 fusion.80
  1491.6 6.7 fusion.78
  1499.7 15.2 fusion.110
  1516.1 15.4 fusion.111
  1532.6 16.6 fusion.112
  1551.3 38.8 reduce-scatter.43.cloned.1.call-done
  1591.5 73.1 %reduce-scatter.41.cloned.1.call-done = f32[16,5]{1,0:T(8,128)} async-done(((f32[256,5]{1,0:T(8,128)}), f32[16,5]{1,0:T(8,128)}) %reduce-scatter.41.cloned.1.call-update) | async-done | bytes 336
  1665.9 73.0 %reduce-scatter.37.cloned.1.call-done = f32[16,20]{1,0:T(8,128)} async-done(((f32[256,20]{1,0:T(8,128)}), f32[16,20]{1,0:T(8,128)}) %reduce-scatter.37.cloned.1.call-update) | async-done | bytes 1296
  1740.4 34.0 all-reduce.73.cloned.1.call-done
  1776.4 60.6 %all-reduce.62 = (f32[2560]{0:T(1024)S(1)}, f32[2560]{0:T(1024)S(1)}) all-reduce(f32[2560]{0:T(1024)S(1)} %get-tuple-element.202, f32[2560]{0:T(1024)S(1)} %copy-done.74), channel_id=2, replica_groups=mesh['seq'=16,'head'=2] {'seq'}, use_global_device_ids=true, to_apply=%region_13.14.clone | all-reduce | flops 5120 | bytes 40960
  1842.2 77.6 %reduce-scatter.27.cloned.1.call-done = f32[5,16,256]{2,1,0:T(8,128)} async-done(((f32[5,256,256]{2,1,0:T(8,128)}), f32[5,16,256]{2,1,0:T(8,128)}) %reduce-scatter.27.cloned.1.call-update) | async-done | bytes 81936 | tf_op jit(solution)/shard_map/reduce_scatter | solution.py:295
  1919.8 286.5 %reduce-scatter.29.cloned.1.call-done = f32[1280,160]{0,1:T(8,128)} async-done(((f32[1280,2560]{0,1:T(8,128)}), f32[1280,160]{0,1:T(8,128)}) %reduce-scatter.29.cloned.1.call-update) | async-done | bytes 819216 | tf_op jit(solution)/shard_map/reduce_scatter | solution.py:305
  2206.3 280.4 %reduce-scatter.21.cloned.1.call-done = f32[160,1280]{1,0:T(8,128)} async-done(((f32[2560,1280]{1,0:T(8,128)}), f32[160,1280]{1,0:T(8,128)}) %reduce-scatter.21.cloned.1.call-update) | async-done | bytes 819216 | tf_op jit(solution)/shard_map/reduce_scatter | solution.py:285
  2486.6 280.4 %reduce-scatter.23.cloned.1.call-done = f32[160,1280]{1,0:T(8,128)} async-done(((f32[2560,1280]{1,0:T(8,128)}), f32[160,1280]{1,0:T(8,128)}) %reduce-scatter.23.cloned.1.call-update) | async-done | bytes 819216 | tf_op jit(solution)/shard_map/reduce_scatter | solution.py:286
  2767.0 579.6 %reduce-scatter.31.cloned.1.call-done = f32[160,3840]{1,0:T(8,128)} async-done(((f32[2560,3840]{1,0:T(8,128)}), f32[160,3840]{1,0:T(8,128)}) %reduce-scatter.31.cloned.1.call-update) | async-done | bytes 2457616 | tf_op jit(solution)/shard_map/reduce_scatter | solution.py:189
  3346.6 574.3 %reduce-scatter.33.cloned.1.call-done = f32[160,3840]{1,0:T(8,128)} async-done(((f32[2560,3840]{1,0:T(8,128)}), f32[160,3840]{1,0:T(8,128)}) %reduce-scatter.33.cloned.1.call-update) | async-done | bytes 2457616 | tf_op jit(solution)/shard_map/reduce_scatter | solution.py:190
  3921.0 574.4 %reduce-scatter.35.cloned.1.call-done = f32[3840,160]{0,1:T(8,128)} async-done(((f32[3840,2560]{0,1:T(8,128)}), f32[3840,160]{0,1:T(8,128)}) %reduce-scatter.35.cloned.1.call-update) | async-done | bytes 2457616 | tf_op jit(solution)/shard_map/reduce_scatter | solution.py:191
  (630 shorter events, 270.4 us)
Async XLA Ops:
  7.2 67.4 %copy-start = (bf16[128,2560]{1,0:T(8,128)(2,1)S(1)}, bf16[128,2560]{1,0:T(8,128)(2,1)}, u32[]{:S(2)}) copy-start(bf16[128,2560]{1,0:T(8,128)(2,1)} %param.20) | copy-start | bytes 1966084
  7.2 67.6 %copy-start.109 = (bf16[4,5,16]{2,0,1:T(4,128)(2,1)S(1)}, bf16[4,5,16]{2,0,1:T(4,128)(2,1)}, u32[]{:S(2)}) copy-start(bf16[4,5,16]{2,0,1:T(4,128)(2,1)} %param.24) | copy-start | bytes 1924
  7.2 267.2 %all-gather.14.cloned.1.call-start = ((), (), s32[]{:S(2)}) async-start(), calls=%async_computation.12 | async-start | bytes 6963200 | tf_op jit(solution)/shard_map/all_gather | solution.py:97
  7.9 442.6 %all-gather.16.cloned.1.call-start = ((), (), s32[]{:S(2)}) async-start(), calls=%async_computation.13 | async-start | bytes 6963200 | tf_op jit(solution)/shard_map/all_gather | solution.py:96
  8.7 99.1 %copy-start.80 = (bf16[5,16,256]{2,1,0:T(8,128)(2,1)S(1)}, bf16[5,16,256]{2,1,0:T(8,128)(2,1)}, u32[]{:S(2)}) copy-start(bf16[5,16,256]{2,1,0:T(8,128)(2,1)} %param.25) | copy-start | bytes 122884
  8.7 447.7 %all-gather.18.cloned.1.call-start = ((), (), s32[]{:S(2)}) async-start(), calls=%async_computation.14 | async-start | bytes 6963200 | tf_op jit(solution)/shard_map/all_gather | solution.py:104
  9.4 544.5 %all-reduce.69.cloned.1.call-start = ((), (), s32[]{:S(2)}) async-start(), calls=%async_computation.15 | async-start | bytes 1310720 | tf_op jit(solution)/shard_map/psum | solution.py:145
  74.6 68.6 %copy-start.81 = (bf16[5,16,256]{2,1,0:T(8,128)(2,1)S(1)}, bf16[5,16,256]{2,1,0:T(8,128)(2,1)}, u32[]{:S(2)}) copy-start(bf16[5,16,256]{2,1,0:T(8,128)(2,1)} %param.27) | copy-start | bytes 122884
  74.8 199.7 %copy-start.82 = (f32[128]{0:T(128)}, f32[128]{0:T(128)S(1)}, u32[]{:S(2)}) copy-start(f32[128]{0:T(128)S(1)} %fusion.76) | copy-start | bytes 1540
  75.3 108.5 %copy-start.112 = (bf16[5,16]{1,0:T(8,128)(2,1)S(1)}, bf16[5,16]{1,0:T(8,128)(2,1)}, u32[]{:S(2)}) copy-start(bf16[5,16]{1,0:T(8,128)(2,1)} %param.29) | copy-start | bytes 484
  107.4 106.2 %copy-start.113 = (bf16[5,16]{1,0:T(8,128)(2,1)S(1)}, bf16[5,16]{1,0:T(8,128)(2,1)}, u32[]{:S(2)}) copy-start(bf16[5,16]{1,0:T(8,128)(2,1)} %param.28) | copy-start | bytes 484
  107.4 137.4 %copy-start.114 = (bf16[5,16]{1,0:T(8,128)(2,1)S(1)}, bf16[5,16]{1,0:T(8,128)(2,1)}, u32[]{:S(2)}) copy-start(bf16[5,16]{1,0:T(8,128)(2,1)} %param.26) | copy-start | bytes 484
  143.2 146.8 %copy-start.17 = (bf16[5,256,256]{2,1,0:T(8,128)(2,1)}, bf16[5,256,256]{2,1,0:T(8,128)(2,1)S(1)}, u32[]{:S(2)}) copy-start(bf16[5,256,256]{2,1,0:T(8,128)(2,1)S(1)} %all_gather.71) | copy-start | bytes 1966084
  183.8 110.8 %copy-start.19 = (bf16[5,256,256]{2,1,0:T(8,128)(2,1)}, bf16[5,256,256]{2,1,0:T(8,128)(2,1)S(1)}, u32[]{:S(2)}) copy-start(bf16[5,256,256]{2,1,0:T(8,128)(2,1)S(1)} %all_gather.68) | copy-start | bytes 1966084
  278.4 8.4 collective-permute-start
  284.3 13.1 copy-start.53
  294.6 1141.0 %copy-start.5 = (f32[128,1280]{1,0:T(8,128)}, f32[128,1280]{1,0:T(8,128)S(1)}, u32[]{:S(2)}) copy-start(f32[128,1280]{1,0:T(8,128)S(1)} %copy.100) | copy-start | bytes 1966084
  297.4 1138.3 %copy-start.6 = (f32[128,1280]{1,0:T(8,128)}, f32[128,1280]{1,0:T(8,128)S(1)}, u32[]{:S(2)}) copy-start(f32[128,1280]{1,0:T(8,128)S(1)} %copy.95) | copy-start | bytes 1966084
  299.0 165.5 %copy-start.11 = (f32[128,1280]{1,0:T(8,128)}, f32[128,1280]{1,0:T(8,128)S(1)}, u32[]{:S(2)}) copy-start(f32[128,1280]{1,0:T(8,128)S(1)} %get-tuple-element.251) | copy-start | bytes 1966084
  380.1 32.3 copy-start.86
  381.9 34.9 copy-start.36
  414.1 36.5 copy-start.83
  462.5 313.4 %all-gather.20.cloned.1.call-start = ((), (), s32[]{:S(2)}) async-start(), calls=%async_computation.16 | async-start | bytes 20889600 | tf_op jit(solution)/shard_map/all_gather | solution.py:150
  463.1 533.0 %all-gather.22.cloned.1.call-start = ((), (), s32[]{:S(2)}) async-start(), calls=%async_computation.17 | async-start | bytes 20889600 | tf_op jit(solution)/shard_map/all_gather | solution.py:151
  463.6 752.8 %all-gather.24.cloned.1.call-start = ((), (), s32[]{:S(2)}) async-start(), calls=%async_computation.18 | async-start | bytes 20889600 | tf_op jit(solution)/shard_map/all_gather | solution.py:152
  464.4 809.7 %all-reduce.71.cloned.1.call-start = ((), (), s32[]{:S(2)}) async-start(), calls=%async_computation.19 | async-start | bytes 1310720 | tf_op jit(solution)/shard_map/psum | solution.py:176
  555.4 721.2 %copy-start.106 = (f32[128]{0:T(128)}, f32[128]{0:T(128)S(1)}, u32[]{:S(2)}) copy-start(f32[128]{0:T(128)S(1)} %fusion.77) | copy-start | bytes 1540
  555.6 440.5 %copy-start.1 = (bf16[128,2560]{1,0:T(8,128)(2,1)}, bf16[128,2560]{1,0:T(8,128)(2,1)S(1)}, u32[]{:S(2)}) copy-start(bf16[128,2560]{1,0:T(8,128)(2,1)S(1)} %multiply_convert_fusion.2) | copy-start | bytes 1966084
  1255.7 294.3 %reduce-scatter.39.cloned.1.call-start = ((), (), s32[]{:S(2)}) async-start(), calls=%async_computation.29 | async-start | bytes 139264
  1296.9 37.6 copy-start.39
  1440.1 150.0 %reduce-scatter.43.cloned.1.call-start = ((), (), s32[]{:S(2)}) async-start(), calls=%async_computation.31 | async-start | bytes 139264
  1444.7 219.9 %reduce-scatter.41.cloned.1.call-start = ((), (), s32[]{:S(2)}) async-start(), calls=%async_computation.30 | async-start | bytes 139264
  1444.7 23.0 slice-start
  1450.1 288.9 %reduce-scatter.37.cloned.1.call-start = ((), (), s32[]{:S(2)}) async-start(), calls=%async_computation.28 | async-start | bytes 139264
  1453.9 12.7 collective-permute-start.1
  1461.2 313.3 %all-reduce.73.cloned.1.call-start = ((), (), s32[]{:S(2)}) async-start(), calls=%async_computation.32 | async-start | bytes 2621440 | tf_op jit(solution)/shard_map/psum | solution.py:162
  1470.8 371.3 %reduce-scatter.25.cloned.1.call-start = ((), (), s32[]{:S(2)}) async-start(), calls=%async_computation.22 | async-start | bytes 1392640 | tf_op jit(solution)/shard_map/reduce_scatter | solution.py:288
  1473.3 446.5 %reduce-scatter.27.cloned.1.call-start = ((), (), s32[]{:S(2)}) async-start(), calls=%async_computation.23 | async-start | bytes 1392640 | tf_op jit(solution)/shard_map/reduce_scatter | solution.py:295
  1475.9 730.3 %reduce-scatter.29.cloned.1.call-start = ((), (), s32[]{:S(2)}) async-start(), calls=%async_computation.24 | async-start | bytes 13926400 | tf_op jit(solution)/shard_map/reduce_scatter | solution.py:305
  1483.0 1003.7 %reduce-scatter.21.cloned.1.call-start = ((), (), s32[]{:S(2)}) async-start(), calls=%async_computation.20 | async-start | bytes 13926400 | tf_op jit(solution)/shard_map/reduce_scatter | solution.py:285
  1490.6 1276.4 %reduce-scatter.23.cloned.1.call-start = ((), (), s32[]{:S(2)}) async-start(), calls=%async_computation.21 | async-start | bytes 13926400 | tf_op jit(solution)/shard_map/reduce_scatter | solution.py:286
  1498.3 1848.3 %reduce-scatter.31.cloned.1.call-start = ((), (), s32[]{:S(2)}) async-start(), calls=%async_computation.25 | async-start | bytes 41779200 | tf_op jit(solution)/shard_map/reduce_scatter | solution.py:189
  1515.0 2406.0 %reduce-scatter.33.cloned.1.call-start = ((), (), s32[]{:S(2)}) async-start(), calls=%async_computation.26 | async-start | bytes 41779200 | tf_op jit(solution)/shard_map/reduce_scatter | solution.py:190
  1531.5 2963.8 %reduce-scatter.35.cloned.1.call-start = ((), (), s32[]{:S(2)}) async-start(), calls=%async_computation.27 | async-start | bytes 41779200 | tf_op jit(solution)/shard_map/reduce_scatter | solution.py:191
  1549.2 227.2 %copy-start.74 = (f32[2560]{0:T(1024)S(1)}, f32[2560]{0:T(1024)}, u32[]{:S(2)}) copy-start(f32[2560]{0:T(1024)} %get-tuple-element.194) | copy-start | bytes 30724
  1549.2 289.0 %copy-start.116 = (f32[128]{0:T(128)S(1)}, f32[128]{0:T(128)}, u32[]{:S(2)}) copy-start(f32[128]{0:T(128)} %copy-done.115) | copy-start | bytes 1540
  1549.2 289.0 %copy-start.16 = (bf16[128,2560]{1,0:T(8,128)(2,1)S(1)}, bf16[128,2560]{1,0:T(8,128)(2,1)}, u32[]{:S(2)}) copy-start(bf16[128,2560]{1,0:T(8,128)(2,1)} %all-reduce.71.cloned.1.call-done) | copy-start | bytes 1966084
  1774.5 63.8 %copy-start.38 = (bf16[128,2560]{1,0:T(8,128)(2,1)S(1)}, bf16[128,2560]{1,0:T(8,128)(2,1)}, u32[]{:S(2)}) copy-start(bf16[128,2560]{1,0:T(8,128)(2,1)} %get-tuple-element.229) | copy-start | bytes 1966084
  (94 other events, 465.5 us)
Sparse Core Ops, SparseCore 0:
  10.7 101.6 all-gather.13
  115.1 106.2 all-gather.15
  224.1 96.6 all-gather.17
  462.6 91.2 all-reduce.68
  556.9 218.9 all-gather.19
  779.0 217.0 all-gather.21
  999.3 217.0 all-gather.23
  1255.8 18.2 all-reduce.70
  1440.2 75.4 reduce-scatter.38
  1517.9 72.1 reduce-scatter.42
  1592.4 72.1 reduce-scatter.40
  1666.8 72.1 reduce-scatter.36
  1741.9 32.5 all-reduce.72
  1777.3 64.8 reduce-scatter.24
  1845.0 74.7 reduce-scatter.26
  1922.7 283.5 reduce-scatter.28
  2209.1 277.4 reduce-scatter.20
  2489.5 277.4 reduce-scatter.22
  2774.7 571.8 reduce-scatter.30
  3354.2 566.7 reduce-scatter.32
  3928.7 566.6 reduce-scatter.34
where the time goes:
time: 4520 us; the launch traced here: 4500 us
  waiting for transfers between devices  3600 us (80%)
  blocking collectives  436 us (10%)
  local copies, waits for them, and re-layouts  191 us (4%)
  matrix products  180 us (4%)
  other arithmetic  66.7 us (1%)
    reduce_scatter x1, waiting for transfers between devices, shards(): lax.psum_scatter(expand_grad, 'seq', scatter_dimension=0, tiled=True)  580 us
    reduce_scatter x1, waiting for transfers between devices, shards(): lax.psum_scatter(contract_grad, 'seq', scatter_dimension=1, tiled=True)  574 us
    reduce_scatter x1, waiting for transfers between devices, shards(): lax.psum_scatter(value_wgrad, 'seq', scatter_dimension=0, tiled=True)  574 us
    reduce_scatter x1, waiting for transfers between devices, shards(): lax.psum_scatter(output_wgrad, 'seq', scatter_dimension=1, tiled=True)  286 us
    reduce_scatter x1, waiting for transfers between devices, shards(): lax.psum_scatter(scan_wgrad, 'seq', scatter_dimension=0, tiled=True)  280 us
    reduce_scatter x1, waiting for transfers between devices, shards(): lax.psum_scatter(gelu_wgrad, 'seq', scatter_dimension=0, tiled=True)  280 us
    all_gather x1, waiting for transfers between devices, shards(): lax.all_gather(expand_gate, 'seq', axis=0, tiled=True)  220 us
    all_gather x1, waiting for transfers between devices, shards(): lax.all_gather(contract_weight, 'seq', axis=1, tiled=True)  210 us
  transfers between devices with their start and end apart: 23, of which 18 were waited for; matrix products, arithmetic and copies ran while one was open for 6% of the time, Pallas kernels for 0%

commit v1 on v0

v1 whole, which is shorter than its diff:
```python
import functools

import jax
import jax.numpy as jnp
from jax import lax
from jax.experimental import pallas as pl
from jax.experimental.pallas import tpu as pltpu
from jax.sharding import PartitionSpec as P

BF16 = jnp.bfloat16
F32 = jnp.float32
EPSILON = 1e-06
BOTH = ("seq", "head")
LANES = 128
CHUNK = 128
GELU_A = 0.7978845608028654
GELU_B = 0.044715
VMEM_BYTES = 56 * 1024 * 1024


def xor_send(value, mask_first, mask_second=None, allowed=None):
    count = lax.axis_size("seq")
    masks = (mask_first, mask_first if mask_second is None else mask_second)
    pairs = [
        (chip * 2 + core, (chip ^ masks[core]) * 2 + core)
        for chip in range(count)
        for core in range(2)
        if allowed is None or allowed(chip, chip ^ masks[core])
    ]
    return lax.ppermute(value, BOTH, pairs)


def core_swap(value):
    return lax.ppermute(value, "head", [(0, 1), (1, 0)])


def gathered(rows):
    count = lax.axis_size("seq")
    columns = [rows] + [xor_send(rows, 4 * g) for g in range(1, count // 4)]
    own = []
    for block in columns:
        near = xor_send(block, 2, 1)
        own.append(
            jnp.concatenate([block, xor_send(block, 1, 2), near, xor_send(near, 1, 2)], axis=0)
        )
    other = [core_swap(group) for group in own]
    return jnp.concatenate(own + other, axis=0)


def scattered(partial):
    count = lax.axis_size("seq")
    blocks = partial.reshape(count // 4, 4, -1, partial.shape[-1])
    arriving = []
    own = None
    for g in list(range(1, count // 4)) + [0]:
        near = blocks[g, 2] + xor_send(blocks[g, 3].astype(BF16), 1, 2).astype(F32)
        here = blocks[g, 0] + xor_send(blocks[g, 1].astype(BF16), 1, 2).astype(F32)
        here = here + xor_send(near.astype(BF16), 2, 1).astype(F32)
        if g:
            arriving.append(xor_send(here.astype(BF16), 4 * g))
        else:
            own = here
    for more in arriving:
        own = own + more.astype(F32)
    return own


def exchanged(pieces, allowed):
    count = lax.axis_size("seq")
    return jnp.stack([pieces[0]] + [xor_send(pieces[j], j, None, allowed) for j in range(1, count)])


def params(**more):
    return pltpu.CompilerParams(vmem_limit_bytes=VMEM_BYTES, **more)


def picked_body(index, source, target):
    target[...] = source[...]


def picked(blocks, index):
    shape = blocks.shape[1:]
    zeros = (0,) * len(shape)
    return pl.pallas_call(
        picked_body,
        out_shape=jax.ShapeDtypeStruct((index.shape[0],) + shape, blocks.dtype),
        grid_spec=pltpu.PrefetchScalarGridSpec(
            num_scalar_prefetch=1,
            grid=(index.shape[0],),
            in_specs=[pl.BlockSpec((1,) + shape, lambda j, at: (at[j],) + zeros)],
            out_specs=pl.BlockSpec((1,) + shape, lambda j, at: (j,) + zeros),
        ),
        compiler_params=params(),
    )(index, blocks)


def gelu_parts(w):
    inner = jnp.tanh(GELU_A * (w + GELU_B * w * w * w))
    return 0.5 * w * (1.0 + inner), inner


def gelu_slope(w, inner):
    return 0.5 * (1.0 + inner) + 0.5 * w * (1.0 - inner * inner) * GELU_A * (
        1.0 + 3.0 * GELU_B * w * w
    )


def rate_parts(ga, soft_row):
    log_rate = -8.0 * ga * soft_row
    twice = 2.0 * log_rate
    near = -twice * (
        1.0 + twice * (0.5 + twice * (1.0 / 6 + twice * (1.0 / 24 + twice * (1.0 / 120))))
    )
    rate = jnp.exp(log_rate)
    far = 1.0 - jnp.exp(twice)
    return rate, jnp.sqrt(jnp.where(twice > -0.1, near, far))


def filter_kernel(slot, yv, rows, y, vp, c, cb, *, th, taps):
    total = y.shape[0]
    vp[0:8, :] = jnp.zeros((8, LANES), F32)

    def order(b, carry):
        block = yv[pl.ds(pl.multiple_of(slot[b] * th, th), th), :]
        y[pl.ds(pl.multiple_of(b * th, th), th), :] = block[:, :LANES]
        vp[pl.ds(pl.multiple_of(b * th + 8, 8), th), :] = block[:, LANES:]
        return carry

    lax.fori_loop(0, total // th, order, 0)

    def chunk(i, carry):
        start = pl.multiple_of(i * CHUNK, CHUNK)
        window = vp[pl.ds(start, CHUNK + 8), :]
        out = rows[0:1, :] * window[8 : 8 + CHUNK]
        for k in range(1, taps):
            out = out + rows[k : k + 1, :] * window[8 - k : 8 - k + CHUNK]
        c[pl.ds(start, CHUNK), :] = out
        cb[pl.ds(start, CHUNK), :] = out.astype(BF16)
        return carry

    lax.fori_loop(0, total // CHUNK, chunk, 0)


def state_kernel(slot, cbo, cbx, near, far, c, y, rows, gi, ga, hp, ob, a, p, *, th):
    total = y.shape[0]
    length = total // 8
    bias_i, bias_a, soft = rows[0:1, :], rows[1:2, :], rows[2:3, :]

    def chunk(i, carry):
        at = pl.ds(pl.multiple_of(i * CHUNK, CHUNK), CHUNK)
        pre = jnp.dot(cbo[at, :], near[...], preferred_element_type=F32) + jnp.dot(
            cbx[at, :], far[...], preferred_element_type=F32
        )
        open_i = jax.nn.sigmoid(pre[:, :LANES] + bias_i)
        open_a = jax.nn.sigmoid(pre[:, LANES:] + bias_a)
        rate, scale = rate_parts(open_a, soft)
        gi[at, :] = open_i
        ga[at, :] = open_a
        a[at, :] = rate
        hp[pl.ds(pl.multiple_of(i * CHUNK + 8, 8), CHUNK), :] = scale * open_i * c[at, :]
        return carry

    lax.fori_loop(0, total // CHUNK, chunk, 0)

    def step(t, carry):
        h, q = carry
        at = pl.ds(t, 8, stride=length)
        rate = a[at, :]
        h = rate * h + hp[pl.ds(t + 8, 8, stride=length), :]
        q = q * rate
        hp[pl.ds(t + 8, 8, stride=length), :] = h
        p[at, :] = q
        return h, q

    last, product = lax.fori_loop(
        0,
        length,
        step,
        (jnp.zeros((8, LANES), F32), jnp.ones((8, LANES), F32)),
        unroll=8,
    )
    hp[0:8, :] = jnp.zeros((8, LANES), F32)
    entering = [jnp.zeros((1, LANES), F32)]
    for j in range(7):
        entering.append(last[j : j + 1] + product[j : j + 1] * entering[-1])

    per = length // th
    for j in range(8):
        enter = entering[j]

        def finish(i, carry, j=j, enter=enter):
            b = j * per + i
            at = pl.ds(pl.multiple_of(b * th, th), th)
            ahead = pl.ds(pl.multiple_of(b * th + 8, 8), th)
            h = hp[ahead, :] + p[at, :] * enter
            hp[ahead, :] = h
            out, _ = gelu_parts(y[at, :])
            ob[pl.ds(pl.multiple_of(slot[b] * th, th), th), :] = (h * out).astype(BF16)
            return carry

        lax.fori_loop(0, per, finish, 0)


def adjoint_kernel(
    slot, dob, y, hp, gi, ga, c, rows, dy, dpp, dc, sums, lam, a, q, *, th
):
    total = y.shape[0]
    length = total // 8
    soft = rows[2:3, :]

    def order(b, carry):
        at = pl.ds(pl.multiple_of(b * th, th), th)
        there = pl.ds(pl.multiple_of(slot[b] * th, th), th)
        block = dob[there, :]
        w = y[at, :]
        out, inner = gelu_parts(w)
        lam[at, :] = block * out
        h = hp[pl.ds(pl.multiple_of(b * th + 8, 8), th), :]
        dy[there, :] = (block * h * gelu_slope(w, inner)).astype(BF16)
        a[at, :] = jnp.exp(-8.0 * ga[at, :] * soft)
        return carry

    lax.fori_loop(0, total // th, order, 0)

    def step(i, carry):
        later, product = carry
        at = pl.ds(length - 1 - i, 8, stride=length)
        here = lam[at, :] + later
        lam[at, :] = here
        q[at, :] = product
        rate = a[at, :]
        return rate * here, product * rate

    first, product = lax.fori_loop(
        0,
        length,
        step,
        (jnp.zeros((8, LANES), F32), jnp.ones((8, LANES), F32)),
        unroll=8,
    )
    entering = [jnp.zeros((1, LANES), F32)]
    for j in range(7, 0, -1):
        entering.append(first[j : j + 1] + product[j : j + 1] * entering[-1])
    entering = entering[::-1]

    per = length // th
    carry = (jnp.zeros((1, LANES), F32),) * 3
    for j in range(8):
        enter = entering[j]

        def finish(i, carry, j=j, enter=enter):
            b = j * per + i
            start = pl.multiple_of(b * th, th)
            at = pl.ds(start, th)
            state_grad = lam[at, :] + q[at, :] * enter
            before = hp[pl.ds(start, th + 8), :][7 : 7 + th]
            open_i, open_a, filtered = gi[at, :], ga[at, :], c[at, :]
            rate, scale = rate_parts(open_a, soft)
            dla = state_grad * before * rate - state_grad * open_i * filtered * rate * rate / scale
            dpi = state_grad * scale * filtered * open_i * (1.0 - open_i)
            slope = -8.0 * open_a * dla
            dpa = soft * slope * (1.0 - open_a)
            dpp[at, :LANES] = dpi.astype(BF16)
            dpp[at, LANES:] = dpa.astype(BF16)
            dc[at, :] = state_grad * scale * open_i
            return (
                carry[0] + jnp.sum(dpi, axis=0, keepdims=True),
                carry[1] + jnp.sum(dpa, axis=0, keepdims=True),
                carry[2] + jnp.sum(slope, axis=0, keepdims=True),
            )

        carry = lax.fori_loop(0, per, finish, carry)
    sums[...] = jnp.zeros_like(sums)
    for row in range(3):
        sums[row : row + 1, :] = carry[row]


def unfilter_kernel(
    slot, dpo, dpx, near, far, dc, vp, rows, dv, sums, dcp, *, th, taps
):
    total = dc.shape[0]
    last = (((1,), (1,)), ((), ()))
    dcp[total : total + 8, :] = jnp.zeros((8, LANES), F32)

    def chunk(i, carry):
        start = pl.multiple_of(i * CHUNK, CHUNK)
        at = pl.ds(start, CHUNK)
        whole = (
            dc[at, :]
            + lax.dot_general(dpo[at, :], near[...], last, preferred_element_type=F32)
            + lax.dot_general(dpx[at, :], far[...], last, preferred_element_type=F32)
        )
        dcp[at, :] = whole
        window = vp[pl.ds(start, CHUNK + 8), :]
        return tuple(
            carry[k] + jnp.sum(whole * window[8 - k : 8 - k + CHUNK], axis=0, keepdims=True)
            for k in range(taps)
        )

    carry = lax.fori_loop(
        0, total // CHUNK, chunk, tuple(jnp.zeros((1, LANES), F32) for _ in range(taps))
    )
    sums[...] = jnp.zeros_like(sums)
    for k in range(taps):
        sums[k : k + 1, :] = carry[k]

    def order(b, carry):
        window = dcp[pl.ds(pl.multiple_of(b * th, th), th + 8), :]
        out = rows[0:1, :] * window[0:th]
        for k in range(1, taps):
            out = out + rows[k : k + 1, :] * window[k : k + th]
        dv[pl.ds(pl.multiple_of(slot[b] * th, th), th), :] = out.astype(BF16)
        return carry

    lax.fori_loop(0, total // th, order, 0)


def on_chip(kernel, slot, inputs, outs, scratch=()):
    vmem = pl.BlockSpec(memory_space=pltpu.VMEM)
    return pl.pallas_call(
        kernel,
        out_shape=[jax.ShapeDtypeStruct(shape, dtype) for shape, dtype in outs],
        in_specs=[pl.BlockSpec(memory_space=pltpu.SMEM)] + [vmem] * len(inputs),
        out_specs=[vmem] * len(outs),
        scratch_shapes=[pltpu.VMEM(shape, dtype) for shape, dtype in scratch],
        compiler_params=params(),
    )(slot, *inputs)


def dot(left, right, over):
    return lax.dot_general(left, right, (over, ((), ())), preferred_element_type=F32)


def shards(
    block_input,
    first_gain,
    gelu_weight,
    scan_weight,
    filter_taps,
    input_gate,
    input_bias,
    decay_gate,
    decay_bias,
    decay_param,
    output_weight,
    second_gain,
    expand_gate,
    expand_value,
    contract_weight,
    output_cotangent,
):
    count = lax.axis_size("seq")
    chip = lax.axis_index("seq")
    core = lax.axis_index("head")
    slots = jnp.arange(count, dtype=jnp.int32)
    here = chip ^ slots
    th = block_input.shape[0] // 2
    width = block_input.shape[1]
    part = gelu_weight.shape[0]
    taps = filter_taps.shape[0]
    local_blocks, gate_rows, block_width = input_gate.shape
    blocks = 2 * local_blocks
    assert block_width == 2 * LANES and width == part * count
    mine = count * th
    total = 2 * mine

    chip_of = [b * count // blocks for b in range(blocks)]
    assert count >= blocks
    block_of = [chip_of.index(s) if s in chip_of else 0 for s in range(count)]
    gate_chips = frozenset(chip_of)
    hidden = expand_gate.shape[1]
    lanes = LANES * -(-hidden // (count * LANES))
    hidden_chips = hidden // lanes
    assert hidden_chips * lanes == hidden

    number = jnp.arange(2 * count, dtype=jnp.int32)
    relative = chip ^ (number // 2)
    turned = (relative & ~3) | ((relative & 1) << 1) | ((relative >> 1) & 1)
    slot = jnp.where(number % 2 == 0, relative, turned) + jnp.where(
        number % 2 == core, 0, count
    )
    slot = slot.astype(jnp.int32)

    x = lax.dynamic_slice_in_dim(block_input, core * th, th, 0).astype(F32)
    s1 = lax.rsqrt(jnp.mean(x * x, axis=-1, keepdims=True) + EPSILON)
    first = gathered((x * s1).astype(BF16))

    extra = max(16, gate_rows)
    gain1 = first_gain.astype(F32)[:, None]
    mats = jnp.stack(
        [
            (gelu_weight.astype(F32) * gain1).astype(BF16),
            (scan_weight.astype(F32) * gain1).astype(BF16),
            output_weight.T,
        ],
        axis=1,
    ).reshape(part, 3, local_blocks, 2, LANES)
    mats = mats.transpose(3, 2, 0, 1, 4).reshape(2, local_blocks, part, 3 * LANES)
    small = jnp.concatenate(
        [
            filter_taps.transpose(1, 0, 2),
            input_bias[:, None],
            decay_bias[:, None],
            decay_param[:, None],
        ],
        axis=1,
    )
    small = jnp.pad(
        small, ((0, 0), (0, extra - small.shape[1]), (0, LANES - small.shape[2]))
    )
    gates = jnp.stack([input_gate, decay_gate], axis=2).reshape(
        local_blocks, gate_rows, 2, 2, LANES
    )
    gates = jnp.pad(gates, ((0, 0), (0, extra - gate_rows), (0, 0), (0, 0), (0, 0)))
    gates = gates.transpose(3, 0, 1, 2, 4).reshape(2, local_blocks, extra, 2 * LANES)
    gates = jnp.concatenate([gates, jnp.broadcast_to(small, (2,) + small.shape)], axis=-1)
    mats = jnp.concatenate([mats, gates], axis=2)
    kept = lax.dynamic_index_in_dim(mats, core, 0, False)
    given = core_swap(lax.dynamic_index_in_dim(mats, 1 - core, 0, False))
    mats = jnp.concatenate(
        [jnp.where(core == 0, kept, given), jnp.where(core == 0, given, kept)], axis=0
    )
    mats = picked(mats, jnp.asarray(block_of, jnp.int32)[here])
    mats = exchanged(mats, lambda source, target: target in gate_chips)
    mats = picked(mats, here)
    weights = mats[:, :part].reshape(width, 3 * LANES)
    weight_yv, weight_out = weights[:, : 2 * LANES], weights[:, 2 * LANES :]
    gates = mats[:, part : part + gate_rows, : 2 * LANES].reshape(block_width, 2 * LANES)
    small = mats[:, part : part + taps + 3, 2 * LANES : 2 * LANES + gate_rows]
    small = small.transpose(1, 0, 2).reshape(taps + 3, block_width)
    small = lax.dynamic_slice_in_dim(small, core * LANES, LANES, 1).astype(F32)
    tap_rows = jnp.pad(small[:taps], ((0, 8 - taps), (0, 0)))
    param_row = small[taps + 2 :]
    gate_rows_of = jnp.pad(
        jnp.concatenate([small[taps : taps + 2], jax.nn.softplus(param_row)], axis=0),
        ((0, 5), (0, 0)),
    )
    weights_other = core_swap(weights)
    gates_other = core_swap(gates)
    own_half = lambda a: lax.dynamic_slice_in_dim(a, core * LANES, LANES, 0)
    far_half = lambda a: lax.dynamic_slice_in_dim(a, (1 - core) * LANES, LANES, 0)

    gain2 = second_gain.astype(F32)[:, None]
    wide = jnp.stack(
        [
            (expand_gate.astype(F32) * gain2).astype(BF16),
            (expand_value.astype(F32) * gain2).astype(BF16),
            contract_weight.T,
        ],
        axis=1,
    ).reshape(part, 3, hidden_chips, lanes)
    wide = wide.transpose(2, 0, 1, 3).reshape(hidden_chips, part, 3 * lanes)
    wide = picked(wide, jnp.minimum(here, hidden_chips - 1).astype(jnp.int32))
    wide = exchanged(wide, lambda source, target: target < hidden_chips)
    wide = picked(wide, here).reshape(width, 3 * lanes)
    wide_other = core_swap(wide)
    cotangent = lax.dynamic_slice_in_dim(output_cotangent, core * th, th, 0)
    given_out = gathered(cotangent)

    yv = dot(first, weight_yv, ((1,), (0,)))
    token_f32, token_bf16 = ((total, LANES), F32), ((total, LANES), BF16)
    padded = ((total + 8, LANES), F32)
    y, vp, c, cb = on_chip(
        functools.partial(filter_kernel, th=th, taps=taps),
        slot,
        [yv, tap_rows],
        [token_f32, padded, token_f32, token_bf16],
    )
    cb_other = core_swap(cb)
    gate_near, gate_far = own_half(gates), far_half(gates)
    gi, ga, hp, ob = on_chip(
        functools.partial(state_kernel, th=th),
        slot,
        [cb, cb_other, gate_near, gate_far, c, y, gate_rows_of],
        [token_f32, token_f32, padded, token_bf16],
        [token_f32, token_f32],
    )
    merged = jnp.concatenate([ob[:mine], core_swap(ob[mine:])], axis=1)
    out_both = jnp.concatenate([weight_out, weights_other[:, 2 * LANES :]], axis=1)
    r = x + scattered(dot(merged, out_both, ((1,), (1,))))

    s2 = lax.rsqrt(jnp.mean(r * r, axis=-1, keepdims=True) + EPSILON)
    second = gathered((r * s2).astype(BF16))
    weight_ge, weight_c = wide[:, : 2 * lanes], wide[:, 2 * lanes :]
    ge = dot(second, weight_ge, ((1,), (0,)))
    dz = dot(given_out, weight_c, ((1,), (0,)))
    g, e = ge[:, :lanes], ge[:, lanes:]
    act, inner = gelu_parts(g)
    zb = (act * e).astype(BF16)
    dgate = (dz * e * gelu_slope(g, inner)).astype(BF16)
    dvalue = (dz * act).astype(BF16)
    dge = jnp.concatenate([dgate, dvalue], axis=1)
    dge_both = jnp.concatenate([dge[:mine], core_swap(dge[mine:])], axis=1)
    ge_both = jnp.concatenate([weight_ge, wide_other[:, : 2 * lanes]], axis=1)
    back2 = scattered(dot(dge_both, ge_both, ((1,), (1,))))
    dr = (
        cotangent.astype(F32)
        + s2 * back2
        - r * (s2 * s2 * s2) * jnp.mean(back2 * r, axis=-1, keepdims=True)
    )
    zb_both = jnp.concatenate([zb[:mine], core_swap(zb[mine:])], axis=1)
    c_both = jnp.concatenate([weight_c, wide_other[:, 2 * lanes :]], axis=1)
    out_half = (r + scattered(dot(zb_both, c_both, ((1,), (1,))))).astype(BF16)

    wide_grad = jnp.concatenate(
        [dot(second, dge, ((0,), (0,))), dot(given_out, zb, ((0,), (0,)))], axis=1
    ).astype(BF16)
    wide_grad = picked(wide_grad.reshape(count, part, 3 * lanes), here)
    wide_grad = exchanged(wide_grad, lambda source, target: source < hidden_chips)
    wide_grad = picked(wide_grad, here)[:hidden_chips].astype(F32)
    wide_grad = wide_grad.transpose(1, 0, 2).reshape(part, hidden_chips, 3, lanes)
    gate_hat, value_hat, contract_t = (wide_grad[:, :, i].reshape(part, hidden) for i in range(3))
    gain2_part = jnp.sum(
        gate_hat * expand_gate.astype(F32) + value_hat * expand_value.astype(F32), axis=1
    )

    dq = gathered(dr.astype(BF16))
    dob = dot(dq, weight_out, ((1,), (0,)))
    dy, dpp, dc, sums = on_chip(
        functools.partial(adjoint_kernel, th=th),
        slot,
        [dob, y, hp, gi, ga, c, gate_rows_of],
        [token_bf16, ((total, 2 * LANES), BF16), token_f32, ((8, LANES), F32)],
        [token_f32, token_f32, token_f32],
    )
    dpp_other = core_swap(dpp)
    dv, tap_sums = on_chip(
        functools.partial(unfilter_kernel, th=th, taps=taps),
        slot,
        [dpp, dpp_other, gate_near, own_half(gates_other), dc, vp, tap_rows],
        [token_bf16, ((8, LANES), F32)],
        [padded],
    )
    dyv = jnp.concatenate([dy, dv], axis=1)
    dyv_both = jnp.concatenate([dyv[:mine], core_swap(dyv[mine:])], axis=1)
    yv_both = jnp.concatenate([weight_yv, weights_other[:, : 2 * LANES]], axis=1)
    back1 = scattered(dot(dyv_both, yv_both, ((1,), (1,))))
    in_half = dr + s1 * back1 - x * (s1 * s1 * s1) * jnp.mean(back1 * x, axis=-1, keepdims=True)

    yv_grad = dot(first, dyv, ((0,), (0,)))
    out_grad = dot(dq, ob, ((0,), (0,)))
    weight_grad = jnp.concatenate([yv_grad, out_grad], axis=1).astype(BF16)
    weight_grad = weight_grad.reshape(count, part, 3 * LANES)
    own_grad, far_grad = dot(cb, dpp, ((0,), (0,))), dot(cb_other, dpp, ((0,), (0,)))
    gate_grad = jnp.concatenate(
        [jnp.where(core == 0, own_grad, far_grad), jnp.where(core == 0, far_grad, own_grad)], axis=0
    )
    gate_grad = jnp.pad(
        gate_grad.reshape(count, gate_rows, 2 * LANES), ((0, 0), (0, extra - gate_rows), (0, 0))
    )
    small_grad = jnp.concatenate(
        [tap_sums[:taps], sums[:2], sums[2:3] * jax.nn.sigmoid(param_row)], axis=0
    )
    small_grad = jnp.concatenate(
        [
            jnp.where(core == 0, small_grad, 0.0),
            jnp.where(core == 0, 0.0, small_grad),
        ],
        axis=1,
    )
    small_grad = small_grad.reshape(taps + 3, count, gate_rows).transpose(1, 0, 2)
    small_grad = jnp.pad(
        small_grad, ((0, 0), (0, extra - taps - 3), (0, LANES - gate_rows))
    )
    gate_grad = jnp.concatenate([gate_grad, small_grad], axis=-1).astype(BF16)
    weight_grad = jnp.concatenate([weight_grad, gate_grad], axis=1)
    weight_grad = picked(weight_grad, here)
    weight_grad = exchanged(weight_grad, lambda source, target: source in gate_chips)
    weight_grad = picked(weight_grad, (jnp.asarray(chip_of, jnp.int32) ^ chip).astype(jnp.int32))
    kept = lax.dynamic_slice_in_dim(weight_grad, core * local_blocks, local_blocks, 0)
    given = lax.dynamic_slice_in_dim(weight_grad, (1 - core) * local_blocks, local_blocks, 0)
    given = core_swap(given)
    halves = jnp.stack(
        [jnp.where(core == 0, kept, given), jnp.where(core == 0, given, kept)], axis=0
    ).astype(F32)
    mats_grad = halves[:, :, :part].reshape(2, local_blocks, part, 3, LANES)
    mats_grad = mats_grad.transpose(3, 2, 1, 0, 4).reshape(3, part, local_blocks * block_width)
    gates_grad = halves[:, :, part : part + gate_rows, : 2 * LANES]
    gates_grad = gates_grad.reshape(2, local_blocks, gate_rows, 2, LANES)
    gates_grad = gates_grad.transpose(3, 1, 2, 0, 4).reshape(
        2, local_blocks, gate_rows, block_width
    )
    small_sum = halves[0, :, part:, 2 * LANES :] + halves[1, :, part:, 2 * LANES :]
    small_sum = small_sum[:, : taps + 3, :gate_rows].transpose(1, 0, 2)
    gain1_part = jnp.sum(
        mats_grad[0] * gelu_weight.astype(F32) + mats_grad[1] * scan_weight.astype(F32), axis=1
    )

    gain_parts = jnp.stack([gain1_part, gain2_part])
    gain_grads = gain_parts + core_swap(gain_parts)

    def both_halves(half):
        swapped = core_swap(half)
        return jnp.concatenate(
            [jnp.where(core == 0, half, swapped), jnp.where(core == 0, swapped, half)], axis=0
        )

    return (
        both_halves(out_half),
        both_halves(in_half),
        gain_grads[0],
        mats_grad[0] * gain1,
        mats_grad[1] * gain1,
        small_sum[:taps],
        gates_grad[0],
        small_sum[taps],
        gates_grad[1],
        small_sum[taps + 1],
        small_sum[taps + 2],
        mats_grad[2].T,
        gain_grads[1],
        gate_hat * gain2,
        value_hat * gain2,
        contract_t.T,
    )


def solution(mesh):
    in_specs = (
        P("seq", None),
        P("seq"),
        P("seq", "head"),
        P("seq", "head"),
        P(None, "head", "seq"),
        P("head", "seq", None),
        P("head", "seq"),
        P("head", "seq", None),
        P("head", "seq"),
        P("head", "seq"),
        P("head", "seq"),
        P("seq"),
        P("seq", "head"),
        P("seq", "head"),
        P("head", "seq"),
        P("seq", None),
    )
    out_specs = (
        P("seq", None),
        P("seq", None),
        P("seq"),
        P("seq", "head"),
        P("seq", "head"),
        P(None, "head", "seq"),
        P("head", "seq", None),
        P("head", "seq"),
        P("head", "seq", None),
        P("head", "seq"),
        P("head", "seq"),
        P("head", "seq"),
        P("seq"),
        P("seq", "head"),
        P("seq", "head"),
        P("head", "seq"),
    )
    return jax.shard_map(shards, mesh=mesh, in_specs=in_specs, out_specs=out_specs, check_vma=False)
```

time: 4520 us -> 1560 us (0.35)
  waiting for transfers between devices: 3600 us -> 439 us
  starting transfers between devices: 12.3 us -> 606 us
  blocking collectives: 436 us -> 0 us
  Pallas kernels: 0 us -> 115 us
  matrix products: 180 us -> 81.7 us
    reduce_scatter x8 -> x0, waiting for transfers between devices: 2650 us -> none  [the longest x1 580 us: shards(): lax.psum_scatter(expand_grad, 'seq', scatter_dimension=0, tiled=True)]
    all_gather x6 -> x0, waiting for transfers between devices: 640 us -> none  [the longest x1 220 us: shards(): lax.all_gather(expand_gate, 'seq', axis=0, tiled=True)]
    ppermute x2 -> x210, starting transfers between devices: 10.8 us -> 606 us  [the longest x180 542 us: xor_send(): return lax.ppermute(value, BOTH, pairs)]
    ppermute x2 -> x210, waiting for transfers between devices: 2.39 us -> 439 us  [the longest x180 431 us: xor_send(): return lax.ppermute(value, BOTH, pairs)]
    all_gather x10 -> x0, blocking collectives: 314 us -> none  [the longest x4 116 us: carried_in(): gathered = jax.tree.map(lambda a: lax.all_gather(a, axis), part)]
    unnamed x25 -> x0, waiting for transfers between devices: 189 us -> none
    unnamed x2 -> x0, blocking collectives: 122 us -> none
    pallas_call x0 -> x12, Pallas kernels: none -> 115 us  [the longest x8 81.1 us: picked(): pl.pallas_call(picked_body, out_shape=jax.ShapeDtypeStruct((index.shape[0...]
  transfers between devices with their start and end apart: 23 -> 210, of which waited for: 18 -> 87; matrix products, arithmetic and copies ran while one was open for 6% -> 20% of each run, Pallas kernels for 0% -> 5%
where the time goes in v1:
time: 1560 us; the launch traced here: 1550 us
  starting transfers between devices  606 us (39%)
  waiting for transfers between devices  439 us (28%)
  local copies, waits for them, and re-layouts  221 us (14%)
  Pallas kernels  115 us (7%)
  matrix products  81.7 us (5%)
  other arithmetic  79.5 us (5%)
    ppermute x180, starting transfers between devices, xor_send(): return lax.ppermute(value, BOTH, pairs)  542 us
    ppermute x180, waiting for transfers between devices, xor_send(): return lax.ppermute(value, BOTH, pairs)  431 us
    dot_general x14, matrix products, dot(): lax.dot_general(left, right, (over, ((), ())), preferred_element_type=F32)  81.7 us
    pallas_call x8, Pallas kernels, picked(): pl.pallas_call(picked_body, out_shape=jax.ShapeDtypeStruct((index.shape[0...  81.1 us
    unnamed x297, local copies, waits for them, and re-layouts  77.9 us
    ppermute x30, starting transfers between devices, core_swap(): return lax.ppermute(value, 'head', [(0, 1), (1, 0)])  63.6 us
    pallas_call x4, Pallas kernels, on_chip(): pl.pallas_call(kernel, out_shape=[jax.ShapeDtypeStruct(shape, dtype) for...  33.8 us
  transfers between devices with their start and end apart: 210, of which 87 were waited for; matrix products, arithmetic and copies ran while one was open for 20% of the time, Pallas kernels for 5%

profile of v1, /device:TPU:5, one launch (start us, length us, event | category | flops | bytes accessed | tf_op | source)
XLA Modules:
  0.0 1546.7 jit_solution(1661831218099376921)
XLA Ops:
  28.7 10.8 reshape.224.source
  39.6 10.8 shard_map.301
  54.6 8.5 collective-permute-start.73
  140.1 10.2 collective-permute-done.79
  164.0 10.2 collective-permute-done.81
  189.4 14.7 collective-permute-start.85
  222.8 10.8 shard_map.302
  300.6 10.2 shard_map.297
  316.6 15.1 collective-permute-start.21
  347.7 8.7 collective-permute-start.24
  356.4 8.5 collective-permute-start.25
  366.9 8.8 collective-permute-start.26
  376.5 16.6 %collective-permute-start.28 = (bf16[176,384]{1,0:T(8,128)(2,1)S(1)}, bf16[176,384]{1,0:T(8,128)(2,1)S(1)}, u32[]{:S(2)}, u32[]{:S(2)}) collective-permute-start(bf16[176,384]{1,0:T(8,128)(2,1)S(1)} %get-tuple-element.185), channel_id=1, source_target_pairs={{0,18},{1,19},{2,16},{3,17},{4,22},{5,23},{10,24},{11,25},{14,28},... | collective-permute-start | bytes 405512 | tf_op jit(solution)/shard_map/ppermute | solution.py:30
  395.1 13.6 collective-permute-start.29
  428.2 11.9 collective-permute-start.32
  440.2 13.0 collective-permute-start.33
  456.2 21.8 %collective-permute-start.34 = (bf16[176,384]{1,0:T(8,128)(2,1)S(1)}, bf16[176,384]{1,0:T(8,128)(2,1)S(1)}, u32[]{:S(2)}, u32[]{:S(2)}) collective-permute-start(bf16[176,384]{1,0:T(8,128)(2,1)S(1)} %get-tuple-element.179), channel_id=1, source_target_pairs={{2,28},{3,29},{6,24},{7,25},{8,22},{9,23},{12,18},{13,19},{14,16},... | collective-permute-start | bytes 405512 | tf_op jit(solution)/shard_map/ppermute | solution.py:30
  479.4 10.2 shard_map.298
  528.3 10.6 collective-permute-done.14
  577.3 8.2 fusion.173.yv
  594.0 10.7 shard_map.300
  670.1 18.3 %collective-permute-done.48 = bf16[64,2560]{1,0:T(8,128)(2,1)S(1)} collective-permute-done((bf16[64,2560]{1,0:T(8,128)(2,1)S(1)}, bf16[64,2560]{1,0:T(8,128)(2,1)S(1)}, u32[]{:S(2)}, u32[]{:S(2)}) %collective-permute-start.48) | collective-permute-done | bytes 327712 | tf_op jit(solution)/shard_map/ppermute | solution.py:30
  703.5 11.3 collective-permute-done.60
  717.7 8.8 collective-permute-done.55
  774.5 9.5 multiply_convert_fusion
  784.0 8.1 convolution_convert_fusion.1
  800.8 10.8 shard_map.307
  886.2 11.2 collective-permute-done.201
  909.5 12.2 collective-permute-done.203
  936.7 14.3 collective-permute-start.207
  951.0 9.0 collective-permute-done.207
  962.0 10.8 shard_map.308
  978.6 12.3 reshape.235
  990.9 16.4 %fusion.180 = (f32[160,15,1,256]{3,2,0,1:T(1,128)S(1)}, f32[160,15,1,256]{3,2,0,1:T(1,128)S(1)}, f32[160,15,1,256]{3,2,0,1:T(1,128)S(1)}) fusion(f32[160,15,3,256]{3,2,0,1:T(4,128)} %reshape.235), kind=kLoop, calls=%fused_computation.564 | loop fusion | bytes 14745600 | tf_op jit(solution)/shard_map/slice | solution.py:512
  1035.3 9.4 fusion
  1054.2 9.4 collective-permute-start.137
  1135.1 21.2 %collective-permute-start.135 = (bf16[64,2560]{1,0:T(8,128)(2,1)}, bf16[64,2560]{1,0:T(8,128)(2,1)}, u32[]{:S(2)}, u32[]{:S(2)}) collective-permute-start(bf16[64,2560]{1,0:T(8,128)(2,1)} %get-tuple-element.72), channel_id=1, source_target_pairs={{0,16},{1,17},{2,18},{3,19},{4,20},{5,21},{6,22},{7,23},{8,24},{9,... | collective-permute-start | bytes 983048 | tf_op jit(solution)/shard_map/ppermute | solution.py:30
  1159.6 16.1 %collective-permute-done.135 = bf16[64,2560]{1,0:T(8,128)(2,1)} collective-permute-done((bf16[64,2560]{1,0:T(8,128)(2,1)}, bf16[64,2560]{1,0:T(8,128)(2,1)}, u32[]{:S(2)}, u32[]{:S(2)}) %collective-permute-start.135) | collective-permute-done | bytes 327712 | tf_op jit(solution)/shard_map/ppermute | solution.py:30
  1195.5 16.2 %collective-permute-done.147 = bf16[64,2560]{1,0:T(8,128)(2,1)S(1)} collective-permute-done((bf16[64,2560]{1,0:T(8,128)(2,1)S(1)}, bf16[64,2560]{1,0:T(8,128)(2,1)S(1)}, u32[]{:S(2)}, u32[]{:S(2)}) %collective-permute-start.147) | collective-permute-done | bytes 327712 | tf_op jit(solution)/shard_map/ppermute | solution.py:30
  1216.1 8.8 collective-permute-done.142
  1265.3 11.9 shard_map.303
  1308.0 10.2 shard_map.305
  1361.5 9.0 collective-permute-done.183
  1373.3 18.3 %collective-permute-done.186 = bf16[176,384]{1,0:T(8,128)(2,1)S(1)} collective-permute-done((bf16[176,384]{1,0:T(8,128)(2,1)S(1)}, bf16[176,384]{1,0:T(8,128)(2,1)S(1)}, u32[]{:S(2)}, u32[]{:S(2)}) %collective-permute-start.186) | collective-permute-done | bytes 135200 | tf_op jit(solution)/shard_map/ppermute | solution.py:30
  1401.6 8.5 collective-permute-done.188
  1427.7 12.1 collective-permute-start.193
  1508.7 12.8 collective-permute-done.168
  1521.5 15.5 %collective-permute-done.172 = bf16[64,2560]{1,0:T(8,128)(2,1)S(1)} collective-permute-done((bf16[64,2560]{1,0:T(8,128)(2,1)S(1)}, bf16[64,2560]{1,0:T(8,128)(2,1)S(1)}, u32[]{:S(2)}, u32[]{:S(2)}) %collective-permute-start.172) | collective-permute-done | bytes 327712 | tf_op jit(solution)/shard_map/ppermute | solution.py:30
  (868 shorter events, 966.6 us)
Async XLA Ops:
  5.0 502.1 %collective-permute-start.11 = (bf16[64,2560]{1,0:T(8,128)(2,1)}, bf16[64,2560]{1,0:T(8,128)(2,1)}, u32[]{:S(2)}, u32[]{:S(2)}) collective-permute-start(bf16[64,2560]{1,0:T(8,128)(2,1)} %get-tuple-element.58), channel_id=1, source_target_pairs={{0,24},{1,25},{2,26},{3,27},{4,28},{5,29},{6,30},{7,31},{8,16},{9,... | collective-permute-start | bytes 983048 | tf_op jit(solution)/shard_map/ppermute | solution.py:30
  8.3 489.2 %collective-permute-start.7 = (bf16[64,2560]{1,0:T(8,128)(2,1)}, bf16[64,2560]{1,0:T(8,128)(2,1)}, u32[]{:S(2)}, u32[]{:S(2)}) collective-permute-start(bf16[64,2560]{1,0:T(8,128)(2,1)} %get-tuple-element.58), channel_id=1, source_target_pairs={{0,16},{1,17},{2,18},{3,19},{4,20},{5,21},{6,22},{7,23},{8,24},{9,... | collective-permute-start | bytes 983048 | tf_op jit(solution)/shard_map/ppermute | solution.py:30
  8.3 247.1 %collective-permute-start.3 = (bf16[64,2560]{1,0:T(8,128)(2,1)}, bf16[64,2560]{1,0:T(8,128)(2,1)}, u32[]{:S(2)}, u32[]{:S(2)}) collective-permute-start(bf16[64,2560]{1,0:T(8,128)(2,1)} %get-tuple-element.58), channel_id=1, source_target_pairs={{0,8},{1,9},{2,10},{3,11},{4,12},{5,13},{6,14},{7,15},{8,0},{9,1},... | collective-permute-start | bytes 983048 | tf_op jit(solution)/shard_map/ppermute | solution.py:30
  54.6 38.0 %collective-permute-start.73 = (bf16[160,768]{1,0:T(8,128)(2,1)}, bf16[160,768]{1,0:T(8,128)(2,1)}, u32[]{:S(2)}, u32[]{:S(2)}) collective-permute-start(bf16[160,768]{1,0:T(8,128)(2,1)} %get-tuple-element.154), channel_id=1, source_target_pairs={{0,4},{1,5},{2,6},{3,7},{4,0},{5,1},{6,2},{7,3},{8,12},{9,13},{10,... | collective-permute-start | bytes 737288 | tf_op jit(solution)/shard_map/ppermute | solution.py:30
  124.7 25.7 %collective-permute-start.79 = (bf16[160,768]{1,0:T(8,128)(2,1)S(1)}, bf16[160,768]{1,0:T(8,128)(2,1)S(1)}, u32[]{:S(2)}, u32[]{:S(2)}) collective-permute-start(bf16[160,768]{1,0:T(8,128)(2,1)S(1)} %copy-done.61), channel_id=1, source_target_pairs={{0,16},{1,17},{2,18},{3,19},{4,20},{5,21},{6,22},{7,23},{8,24},{9,... | collective-permute-start | bytes 737288 | tf_op jit(solution)/shard_map/ppermute | solution.py:30
  213.2 26.3 %collective-permute-start = (bf16[64,2560]{1,0:T(8,128)(2,1)}, bf16[64,2560]{1,0:T(8,128)(2,1)S(1)}, u32[]{:S(2)}, u32[]{:S(2)}) collective-permute-start(bf16[64,2560]{1,0:T(8,128)(2,1)} %get-tuple-element.58), channel_id=1, source_target_pairs={{0,2},{1,5},{2,0},{3,7},{4,6},{5,1},{6,4},{7,3},{8,10},{9,13},{10,... | collective-permute-start | bytes 983048 | tf_op jit(solution)/shard_map/ppermute | solution.py:30
  239.5 285.7 %collective-permute-start.116 = (bf16[64,2560]{1,0:T(8,128)(2,1)}, bf16[64,2560]{1,0:T(8,128)(2,1)}, u32[]{:S(2)}, u32[]{:S(2)}) collective-permute-start(bf16[64,2560]{1,0:T(8,128)(2,1)} %get-tuple-element.52), channel_id=1, source_target_pairs={{0,24},{1,25},{2,26},{3,27},{4,28},{5,29},{6,30},{7,31},{8,16},{9,... | collective-permute-start | bytes 983048 | tf_op jit(solution)/shard_map/ppermute | solution.py:30
  255.4 26.5 %collective-permute-start.108 = (bf16[64,2560]{1,0:T(8,128)(2,1)}, bf16[64,2560]{1,0:T(8,128)(2,1)S(1)}, u32[]{:S(2)}, u32[]{:S(2)}) collective-permute-start(bf16[64,2560]{1,0:T(8,128)(2,1)} %get-tuple-element.52), channel_id=1, source_target_pairs={{0,8},{1,9},{2,10},{3,11},{4,12},{5,13},{6,14},{7,15},{8,0},{9,1},... | collective-permute-start | bytes 983048 | tf_op jit(solution)/shard_map/ppermute | solution.py:30
  299.2 202.9 %collective-permute-start.6 = (bf16[64,2560]{1,0:T(8,128)(2,1)}, bf16[64,2560]{1,0:T(8,128)(2,1)}, u32[]{:S(2)}, u32[]{:S(2)}) collective-permute-start(bf16[64,2560]{1,0:T(8,128)(2,1)} %collective-permute-done.5), channel_id=1, source_target_pairs={{0,2},{1,5},{2,0},{3,7},{4,6},{5,1},{6,4},{7,3},{8,10},{9,13},{10,... | collective-permute-start | bytes 983048 | tf_op jit(solution)/shard_map/ppermute | solution.py:30
  507.1 187.6 %collective-permute-start.88 = (bf16[2560,768]{1,0:T(8,128)(2,1)S(1)}, bf16[2560,768]{1,0:T(8,128)(2,1)}, u32[]{:S(2)}, u32[]{:S(2)}) collective-permute-start(bf16[2560,768]{1,0:T(8,128)(2,1)S(1)} %bitcast.666), channel_id=1, source_target_pairs={{0,1},{1,0},{2,3},{3,2},{4,5},{5,4},{6,7},{7,6},{8,9},{9,8},{10,11... | collective-permute-start | bytes 11796488 | tf_op jit(solution)/shard_map/ppermute | solution.py:34
  525.3 32.6 %collective-permute-start.117 = (bf16[64,2560]{1,0:T(8,128)(2,1)}, bf16[64,2560]{1,0:T(8,128)(2,1)S(1)}, u32[]{:S(2)}, u32[]{:S(2)}) collective-permute-start(bf16[64,2560]{1,0:T(8,128)(2,1)} %collective-permute-done.116), channel_id=1, source_target_pairs={{0,2},{1,5},{2,0},{3,7},{4,6},{5,1},{6,4},{7,3},{8,10},{9,13},{10,... | collective-permute-start | bytes 983048 | tf_op jit(solution)/shard_map/ppermute | solution.py:30
  565.0 50.9 %collective-permute-start.120 = (bf16[256,2560]{1,0:T(8,128)(2,1)}, bf16[256,2560]{1,0:T(8,128)(2,1)}, u32[]{:S(2)}, u32[]{:S(2)}) collective-permute-start(bf16[256,2560]{1,0:T(8,128)(2,1)} %pad_maximum_fusion.12), channel_id=1, source_target_pairs={{0,1},{1,0},{2,3},{3,2},{4,5},{5,4},{6,7},{7,6},{8,9},{9,8},{10,11... | collective-permute-start | bytes 3932168 | tf_op jit(solution)/shard_map/ppermute | solution.py:34
  573.2 33.4 %collective-permute-start.37 = (bf16[2560,384]{1,0:T(8,128)(2,1)S(1)}, bf16[2560,384]{1,0:T(8,128)(2,1)}, u32[]{:S(2)}, u32[]{:S(2)}) collective-permute-start(bf16[2560,384]{1,0:T(8,128)(2,1)S(1)} %bitcast.677), channel_id=1, source_target_pairs={{0,1},{1,0},{2,3},{3,2},{4,5},{5,4},{6,7},{7,6},{8,9},{9,8},{10,11... | collective-permute-start | bytes 5898248 | tf_op jit(solution)/shard_map/ppermute | solution.py:34
  590.6 25.7 %collective-permute-start.121 = (bf16[256,2560]{1,0:T(8,128)(2,1)}, bf16[256,2560]{1,0:T(8,128)(2,1)}, u32[]{:S(2)}, u32[]{:S(2)}) collective-permute-start(bf16[256,2560]{1,0:T(8,128)(2,1)} %pad_maximum_fusion.13), channel_id=1, source_target_pairs={{0,1},{1,0},{2,3},{3,2},{4,5},{5,4},{6,7},{7,6},{8,9},{9,8},{10,11... | collective-permute-start | bytes 3932168 | tf_op jit(solution)/shard_map/ppermute | solution.py:34
  620.7 33.2 %collective-permute-start.122 = (bf16[256,2560]{1,0:T(8,128)(2,1)S(1)}, bf16[256,2560]{1,0:T(8,128)(2,1)S(1)}, u32[]{:S(2)}, u32[]{:S(2)}) collective-permute-start(bf16[256,2560]{1,0:T(8,128)(2,1)S(1)} %copy-done.41), channel_id=1, source_target_pairs={{0,1},{1,0},{2,3},{3,2},{4,5},{5,4},{6,7},{7,6},{8,9},{9,8},{10,11... | collective-permute-start | bytes 3932168 | tf_op jit(solution)/shard_map/ppermute | solution.py:34
  647.0 44.0 %collective-permute-start.123 = (bf16[256,2560]{1,0:T(8,128)(2,1)S(1)}, bf16[256,2560]{1,0:T(8,128)(2,1)S(1)}, u32[]{:S(2)}, u32[]{:S(2)}) collective-permute-start(bf16[256,2560]{1,0:T(8,128)(2,1)S(1)} %copy-done.42), channel_id=1, source_target_pairs={{0,1},{1,0},{2,3},{3,2},{4,5},{5,4},{6,7},{7,6},{8,9},{9,8},{10,11... | collective-permute-start | bytes 3932168 | tf_op jit(solution)/shard_map/ppermute | solution.py:34
  661.6 26.7 %collective-permute-start.48 = (bf16[64,2560]{1,0:T(8,128)(2,1)S(1)}, bf16[64,2560]{1,0:T(8,128)(2,1)S(1)}, u32[]{:S(2)}, u32[]{:S(2)}) collective-permute-start(bf16[64,2560]{1,0:T(8,128)(2,1)S(1)} %get-tuple-element.86), channel_id=1, source_target_pairs={{0,16},{1,17},{2,18},{3,19},{4,20},{5,21},{6,22},{7,23},{8,24},{9,... | collective-permute-start | bytes 983048 | tf_op jit(solution)/shard_map/ppermute | solution.py:30
  702.0 33.9 %collective-permute-start.66 = (bf16[64,2560]{1,0:T(8,128)(2,1)S(1)}, bf16[64,2560]{1,0:T(8,128)(2,1)S(1)}, u32[]{:S(2)}, u32[]{:S(2)}) collective-permute-start(bf16[64,2560]{1,0:T(8,128)(2,1)S(1)} %collective-permute-done.64), channel_id=1, source_target_pairs={{0,4},{1,3},{2,6},{3,1},{4,0},{5,7},{6,2},{7,5},{8,12},{9,11},{10,... | collective-permute-start | bytes 983048 | tf_op jit(solution)/shard_map/ppermute | solution.py:30
  714.8 27.7 %collective-permute-start.65 = (bf16[64,2560]{1,0:T(8,128)(2,1)S(1)}, bf16[64,2560]{1,0:T(8,128)(2,1)S(1)}, u32[]{:S(2)}, u32[]{:S(2)}) collective-permute-start(bf16[64,2560]{1,0:T(8,128)(2,1)S(1)} %collective-permute-done.64), channel_id=1, source_target_pairs={{0,2},{1,5},{2,0},{3,7},{4,6},{5,1},{6,4},{7,3},{8,10},{9,13},{10,... | collective-permute-start | bytes 983048 | tf_op jit(solution)/shard_map/ppermute | solution.py:30
  716.0 26.9 %collective-permute-start.62 = (bf16[64,2560]{1,0:T(8,128)(2,1)S(1)}, bf16[64,2560]{1,0:T(8,128)(2,1)S(1)}, u32[]{:S(2)}, u32[]{:S(2)}) collective-permute-start(bf16[64,2560]{1,0:T(8,128)(2,1)S(1)} %collective-permute-done.60), channel_id=1, source_target_pairs={{0,4},{1,3},{2,6},{3,1},{4,0},{5,7},{6,2},{7,5},{8,12},{9,11},{10,... | collective-permute-start | bytes 983048 | tf_op jit(solution)/shard_map/ppermute | solution.py:30
  717.2 33.9 %collective-permute-start.61 = (bf16[64,2560]{1,0:T(8,128)(2,1)S(1)}, bf16[64,2560]{1,0:T(8,128)(2,1)S(1)}, u32[]{:S(2)}, u32[]{:S(2)}) collective-permute-start(bf16[64,2560]{1,0:T(8,128)(2,1)S(1)} %collective-permute-done.60), channel_id=1, source_target_pairs={{0,2},{1,5},{2,0},{3,7},{4,6},{5,1},{6,4},{7,3},{8,10},{9,13},{10,... | collective-permute-start | bytes 983048 | tf_op jit(solution)/shard_map/ppermute | solution.py:30
  828.4 192.3 %collective-permute-start.87 = (bf16[1024,256]{0,1:T(8,128)(2,1)}, bf16[1024,256]{0,1:T(8,128)(2,1)}, u32[]{:S(2)}, u32[]{:S(2)}) collective-permute-start(bf16[1024,256]{0,1:T(8,128)(2,1)} %get-tuple-element.206), channel_id=1, source_target_pairs={{0,1},{1,0},{2,3},{3,2},{4,5},{5,4},{6,7},{7,6},{8,9},{9,8},{10,11... | collective-permute-start | bytes 1572872 | tf_op jit(solution)/shard_map/ppermute | solution.py:34
  828.8 205.3 %collective-permute-start.124 = (bf16[1024,512]{0,1:T(8,128)(2,1)}, bf16[1024,512]{0,1:T(8,128)(2,1)}, u32[]{:S(2)}, u32[]{:S(2)}) collective-permute-start(bf16[1024,512]{0,1:T(8,128)(2,1)} %get-tuple-element.196), channel_id=1, source_target_pairs={{0,1},{1,0},{2,3},{3,2},{4,5},{5,4},{6,7},{7,6},{8,9},{9,8},{10,11... | collective-permute-start | bytes 3145736 | tf_op jit(solution)/shard_map/ppermute | solution.py:34
  828.9 131.1 %collective-permute-start.208 = (bf16[160,768]{1,0:T(8,128)(2,1)S(1)}, bf16[160,768]{1,0:T(8,128)(2,1)S(1)}, u32[]{:S(2)}, u32[]{:S(2)}) collective-permute-start(bf16[160,768]{1,0:T(8,128)(2,1)S(1)} %get-tuple-element.125), channel_id=1, source_target_pairs={{0,30},{1,31},{2,28},{3,29},{4,26},{5,27},{6,24},{7,25},{8,22},{9,... | collective-permute-start | bytes 737288 | tf_op jit(solution)/shard_map/ppermute | solution.py:30
  1032.6 31.1 %collective-permute-start.97 = (bf16[64,2560]{1,0:T(8,128)(2,1)}, bf16[64,2560]{1,0:T(8,128)(2,1)}, u32[]{:S(2)}, u32[]{:S(2)}) collective-permute-start(bf16[64,2560]{1,0:T(8,128)(2,1)} %get-tuple-element.111), channel_id=1, source_target_pairs={{0,2},{1,5},{2,0},{3,7},{4,6},{5,1},{6,4},{7,3},{8,10},{9,13},{10,... | collective-permute-start | bytes 983048 | tf_op jit(solution)/shard_map/ppermute | solution.py:30
  1033.8 29.9 %collective-permute-start.93 = (bf16[64,2560]{1,0:T(8,128)(2,1)}, bf16[64,2560]{1,0:T(8,128)(2,1)}, u32[]{:S(2)}, u32[]{:S(2)}) collective-permute-start(bf16[64,2560]{1,0:T(8,128)(2,1)} %get-tuple-element.113), channel_id=1, source_target_pairs={{0,2},{1,5},{2,0},{3,7},{4,6},{5,1},{6,4},{7,3},{8,10},{9,13},{10,... | collective-permute-start | bytes 983048 | tf_op jit(solution)/shard_map/ppermute | solution.py:30
  1034.0 31.1 %collective-permute-start.90 = (bf16[64,2560]{1,0:T(8,128)(2,1)}, bf16[64,2560]{1,0:T(8,128)(2,1)}, u32[]{:S(2)}, u32[]{:S(2)}) collective-permute-start(bf16[64,2560]{1,0:T(8,128)(2,1)} %get-tuple-element.115), channel_id=1, source_target_pairs={{0,2},{1,5},{2,0},{3,7},{4,6},{5,1},{6,4},{7,3},{8,10},{9,13},{10,... | collective-permute-start | bytes 983048 | tf_op jit(solution)/shard_map/ppermute | solution.py:30
  1122.3 37.3 %collective-permute-start.99 = (bf16[64,2560]{1,0:T(8,128)(2,1)S(1)}, bf16[64,2560]{1,0:T(8,128)(2,1)S(1)}, u32[]{:S(2)}, u32[]{:S(2)}) collective-permute-start(bf16[64,2560]{1,0:T(8,128)(2,1)S(1)} %get-tuple-element.79), channel_id=1, source_target_pairs={{0,16},{1,17},{2,18},{3,19},{4,20},{5,21},{6,22},{7,23},{8,24},{9,... | collective-permute-start | bytes 983048 | tf_op jit(solution)/shard_map/ppermute | solution.py:30
  1125.1 34.5 %collective-permute-start.127 = (bf16[64,2560]{1,0:T(8,128)(2,1)S(1)}, bf16[64,2560]{1,0:T(8,128)(2,1)S(1)}, u32[]{:S(2)}, u32[]{:S(2)}) collective-permute-start(bf16[64,2560]{1,0:T(8,128)(2,1)S(1)} %get-tuple-element.66), channel_id=1, source_target_pairs={{0,4},{1,3},{2,6},{3,1},{4,0},{5,7},{6,2},{7,5},{8,12},{9,11},{10,... | collective-permute-start | bytes 983048 | tf_op jit(solution)/shard_map/ppermute | solution.py:30
  1126.5 33.1 %collective-permute-start.131 = (bf16[64,2560]{1,0:T(8,128)(2,1)}, bf16[64,2560]{1,0:T(8,128)(2,1)}, u32[]{:S(2)}, u32[]{:S(2)}) collective-permute-start(bf16[64,2560]{1,0:T(8,128)(2,1)} %get-tuple-element.70), channel_id=1, source_target_pairs={{0,8},{1,9},{2,10},{3,11},{4,12},{5,13},{6,14},{7,15},{8,0},{9,1},... | collective-permute-start | bytes 983048 | tf_op jit(solution)/shard_map/ppermute | solution.py:30
  1132.1 27.5 %collective-permute-start.139 = (bf16[64,2560]{1,0:T(8,128)(2,1)}, bf16[64,2560]{1,0:T(8,128)(2,1)}, u32[]{:S(2)}, u32[]{:S(2)}) collective-permute-start(bf16[64,2560]{1,0:T(8,128)(2,1)} %get-tuple-element.71), channel_id=1, source_target_pairs={{0,24},{1,25},{2,26},{3,27},{4,28},{5,29},{6,30},{7,31},{8,16},{9,... | collective-permute-start | bytes 983048 | tf_op jit(solution)/shard_map/ppermute | solution.py:30
  1135.1 40.5 %collective-permute-start.135 = (bf16[64,2560]{1,0:T(8,128)(2,1)}, bf16[64,2560]{1,0:T(8,128)(2,1)}, u32[]{:S(2)}, u32[]{:S(2)}) collective-permute-start(bf16[64,2560]{1,0:T(8,128)(2,1)} %get-tuple-element.72), channel_id=1, source_target_pairs={{0,16},{1,17},{2,18},{3,19},{4,20},{5,21},{6,22},{7,23},{8,24},{9,... | collective-permute-start | bytes 983048 | tf_op jit(solution)/shard_map/ppermute | solution.py:30
  1184.4 27.3 %collective-permute-start.147 = (bf16[64,2560]{1,0:T(8,128)(2,1)S(1)}, bf16[64,2560]{1,0:T(8,128)(2,1)S(1)}, u32[]{:S(2)}, u32[]{:S(2)}) collective-permute-start(bf16[64,2560]{1,0:T(8,128)(2,1)S(1)} %get-tuple-element.47), channel_id=1, source_target_pairs={{0,16},{1,17},{2,18},{3,19},{4,20},{5,21},{6,22},{7,23},{8,24},{9,... | collective-permute-start | bytes 983048 | tf_op jit(solution)/shard_map/ppermute | solution.py:30
  1184.4 30.2 %collective-permute-start.143 = (bf16[64,2560]{1,0:T(8,128)(2,1)S(1)}, bf16[64,2560]{1,0:T(8,128)(2,1)S(1)}, u32[]{:S(2)}, u32[]{:S(2)}) collective-permute-start(bf16[64,2560]{1,0:T(8,128)(2,1)S(1)} %get-tuple-element.47), channel_id=1, source_target_pairs={{0,8},{1,9},{2,10},{3,11},{4,12},{5,13},{6,14},{7,15},{8,0},{9,1},... | collective-permute-start | bytes 983048 | tf_op jit(solution)/shard_map/ppermute | solution.py:30
  1185.6 27.5 %collective-permute-start.141 = (bf16[64,2560]{1,0:T(8,128)(2,1)S(1)}, bf16[64,2560]{1,0:T(8,128)(2,1)S(1)}, u32[]{:S(2)}, u32[]{:S(2)}) collective-permute-start(bf16[64,2560]{1,0:T(8,128)(2,1)S(1)} %get-tuple-element.47), channel_id=1, source_target_pairs={{0,4},{1,3},{2,6},{3,1},{4,0},{5,7},{6,2},{7,5},{8,12},{9,11},{10,... | collective-permute-start | bytes 983048 | tf_op jit(solution)/shard_map/ppermute | solution.py:30
  1187.0 27.5 %collective-permute-start.140 = (bf16[64,2560]{1,0:T(8,128)(2,1)S(1)}, bf16[64,2560]{1,0:T(8,128)(2,1)S(1)}, u32[]{:S(2)}, u32[]{:S(2)}) collective-permute-start(bf16[64,2560]{1,0:T(8,128)(2,1)S(1)} %get-tuple-element.47), channel_id=1, source_target_pairs={{0,2},{1,5},{2,0},{3,7},{4,6},{5,1},{6,4},{7,3},{8,10},{9,13},{10,... | collective-permute-start | bytes 983048 | tf_op jit(solution)/shard_map/ppermute | solution.py:30
  1193.3 40.1 %collective-permute-start.153 = (bf16[64,2560]{1,0:T(8,128)(2,1)S(1)}, bf16[64,2560]{1,0:T(8,128)(2,1)S(1)}, u32[]{:S(2)}, u32[]{:S(2)}) collective-permute-start(bf16[64,2560]{1,0:T(8,128)(2,1)S(1)} %collective-permute-done.151), channel_id=1, source_target_pairs={{0,4},{1,3},{2,6},{3,1},{4,0},{5,7},{6,2},{7,5},{8,12},{9,11},{10,... | collective-permute-start | bytes 983048 | tf_op jit(solution)/shard_map/ppermute | solution.py:30
  1211.7 27.9 %collective-permute-start.152 = (bf16[64,2560]{1,0:T(8,128)(2,1)S(1)}, bf16[64,2560]{1,0:T(8,128)(2,1)S(1)}, u32[]{:S(2)}, u32[]{:S(2)}) collective-permute-start(bf16[64,2560]{1,0:T(8,128)(2,1)S(1)} %collective-permute-done.151), channel_id=1, source_target_pairs={{0,2},{1,5},{2,0},{3,7},{4,6},{5,1},{6,4},{7,3},{8,10},{9,13},{10,... | collective-permute-start | bytes 983048 | tf_op jit(solution)/shard_map/ppermute | solution.py:30
  1213.1 26.7 %collective-permute-start.149 = (bf16[64,2560]{1,0:T(8,128)(2,1)S(1)}, bf16[64,2560]{1,0:T(8,128)(2,1)S(1)}, u32[]{:S(2)}, u32[]{:S(2)}) collective-permute-start(bf16[64,2560]{1,0:T(8,128)(2,1)S(1)} %collective-permute-done.147), channel_id=1, source_target_pairs={{0,4},{1,3},{2,6},{3,1},{4,0},{5,7},{6,2},{7,5},{8,12},{9,11},{10,... | collective-permute-start | bytes 983048 | tf_op jit(solution)/shard_map/ppermute | solution.py:30
  1214.6 33.3 %collective-permute-start.148 = (bf16[64,2560]{1,0:T(8,128)(2,1)S(1)}, bf16[64,2560]{1,0:T(8,128)(2,1)S(1)}, u32[]{:S(2)}, u32[]{:S(2)}) collective-permute-start(bf16[64,2560]{1,0:T(8,128)(2,1)S(1)} %collective-permute-done.147), channel_id=1, source_target_pairs={{0,2},{1,5},{2,0},{3,7},{4,6},{5,1},{6,4},{7,3},{8,10},{9,13},{10,... | collective-permute-start | bytes 983048 | tf_op jit(solution)/shard_map/ppermute | solution.py:30
  1322.2 117.6 %collective-permute-start.161 = (bf16[1024,256]{1,0:T(8,128)(2,1)S(1)}, bf16[1024,256]{1,0:T(8,128)(2,1)}, u32[]{:S(2)}, u32[]{:S(2)}) collective-permute-start(bf16[1024,256]{1,0:T(8,128)(2,1)S(1)} %get-tuple-element.204), channel_id=1, source_target_pairs={{0,1},{1,0},{2,3},{3,2},{4,5},{5,4},{6,7},{7,6},{8,9},{9,8},{10,11... | collective-permute-start | bytes 1572872 | tf_op jit(solution)/shard_map/ppermute | solution.py:34
  1322.3 95.5 %collective-permute-start.192 = (bf16[176,384]{1,0:T(8,128)(2,1)S(1)}, bf16[176,384]{1,0:T(8,128)(2,1)S(1)}, u32[]{:S(2)}, u32[]{:S(2)}) collective-permute-start(bf16[176,384]{1,0:T(8,128)(2,1)S(1)} %get-tuple-element.163), channel_id=1, source_target_pairs={{0,30},{1,31},{2,28},{3,29},{6,24},{7,25},{8,22},{9,23},{12,18},{1... | collective-permute-start | bytes 405512 | tf_op jit(solution)/shard_map/ppermute | solution.py:30
  1327.7 90.0 %collective-permute-start.191 = (bf16[176,384]{1,0:T(8,128)(2,1)S(1)}, bf16[176,384]{1,0:T(8,128)(2,1)S(1)}, u32[]{:S(2)}, u32[]{:S(2)}) collective-permute-start(bf16[176,384]{1,0:T(8,128)(2,1)S(1)} %get-tuple-element.164), channel_id=1, source_target_pairs={{0,28},{1,29},{2,30},{3,31},{6,26},{7,27},{8,20},{9,21},{12,16},{1... | collective-permute-start | bytes 405512 | tf_op jit(solution)/shard_map/ppermute | solution.py:30
  1334.0 83.6 %collective-permute-start.190 = (bf16[176,384]{1,0:T(8,128)(2,1)S(1)}, bf16[176,384]{1,0:T(8,128)(2,1)S(1)}, u32[]{:S(2)}, u32[]{:S(2)}) collective-permute-start(bf16[176,384]{1,0:T(8,128)(2,1)S(1)} %get-tuple-element.165), channel_id=1, source_target_pairs={{0,26},{1,27},{2,24},{3,25},{6,28},{7,29},{8,18},{9,19},{12,22},{1... | collective-permute-start | bytes 405512 | tf_op jit(solution)/shard_map/ppermute | solution.py:30
  1427.7 27.9 %collective-permute-start.193 = (bf16[5,176,384]{2,1,0:T(8,128)(2,1)S(1)}, bf16[5,176,384]{2,1,0:T(8,128)(2,1)S(1)}, u32[]{:S(2)}, u32[]{:S(2)}) collective-permute-start(bf16[5,176,384]{2,1,0:T(8,128)(2,1)S(1)} %constant_dynamic-slice_fusion), channel_id=1, source_target_pairs={{0,1},{1,0},{2,3},{3,2},{4,5},{5,4},{6,7},{7,6},{8,9},{9,8},{10,11... | collective-permute-start | bytes 2027528 | tf_op jit(solution)/shard_map/ppermute | solution.py:34
  1452.7 30.9 %collective-permute-start.173 = (bf16[64,2560]{1,0:T(8,128)(2,1)}, bf16[64,2560]{1,0:T(8,128)(2,1)}, u32[]{:S(2)}, u32[]{:S(2)}) collective-permute-start(bf16[64,2560]{1,0:T(8,128)(2,1)} %get-tuple-element.94), channel_id=1, source_target_pairs={{0,2},{1,5},{2,0},{3,7},{4,6},{5,1},{6,4},{7,3},{8,10},{9,13},{10,... | collective-permute-start | bytes 983048 | tf_op jit(solution)/shard_map/ppermute | solution.py:30
  1505.9 31.1 %collective-permute-start.172 = (bf16[64,2560]{1,0:T(8,128)(2,1)S(1)}, bf16[64,2560]{1,0:T(8,128)(2,1)S(1)}, u32[]{:S(2)}, u32[]{:S(2)}) collective-permute-start(bf16[64,2560]{1,0:T(8,128)(2,1)S(1)} %get-tuple-element.65), channel_id=1, source_target_pairs={{0,16},{1,17},{2,18},{3,19},{4,20},{5,21},{6,22},{7,23},{8,24},{9,... | collective-permute-start | bytes 983048 | tf_op jit(solution)/shard_map/ppermute | solution.py:30
  1508.6 35.9 %collective-permute-start.209 = (f32[2,160]{1,0:T(2,128)S(1)}, f32[2,160]{1,0:T(2,128)S(1)}, u32[]{:S(2)}, u32[]{:S(2)}) collective-permute-start(f32[2,160]{1,0:T(2,128)S(1)} %pad_maximum_fusion.24), channel_id=1, source_target_pairs={{0,1},{1,0},{2,3},{3,2},{4,5},{5,4},{6,7},{7,6},{8,9},{9,8},{10,11... | collective-permute-start | bytes 3848 | tf_op jit(solution)/shard_map/ppermute | solution.py:34
  (243 other events, 4295.4 us)

commit v2 on v1

--- a/solution.py
+++ b/solution.py
@@ -39,59 +39,215 @@
     columns = [rows] + [xor_send(rows, 4 * g) for g in range(1, count // 4)]
     own = []
     for block in columns:
-        near = xor_send(block, 2, 1)
-        own.append(
-            jnp.concatenate([block, xor_send(block, 1, 2), near, xor_send(near, 1, 2)], axis=0)
-        )
-    other = [core_swap(group) for group in own]
-    return jnp.concatenate(own + other, axis=0)
-
-
-def scattered(partial):
-    count = lax.axis_size("seq")
-    blocks = partial.reshape(count // 4, 4, -1, partial.shape[-1])
+        pair = jnp.concatenate([block, xor_send(block, 2, 1)], axis=0)
+        own.append(jnp.concatenate([pair, xor_send(pair, 1, 2)], axis=0))
+    return own + [core_swap(group) for group in own]
+
+
+def scattered(*products):
+    count = lax.axis_size("seq") // 4
+    rows = products[0][0][0].shape[0] // 4
+    parts = len(products)
+
+    def sent(arrays, *masks):
+        moved = xor_send(jnp.concatenate([a.astype(BF16) for a in arrays]), *masks)
+        return [a.astype(F32) for a in jnp.split(moved, parts)]
+
+    own = None
     arriving = []
-    own = None
-    for g in list(range(1, count // 4)) + [0]:
-        near = blocks[g, 2] + xor_send(blocks[g, 3].astype(BF16), 1, 2).astype(F32)
-        here = blocks[g, 0] + xor_send(blocks[g, 1].astype(BF16), 1, 2).astype(F32)
-        here = here + xor_send(near.astype(BF16), 2, 1).astype(F32)
+    for g in list(range(1, count)) + [0]:
+        sums = [dot(groups[g], right, ((1,), (1,))).astype(BF16) for groups, right in products]
+        more = sent([a[2 * rows :] for a in sums], 1, 2)
+        sums = [a[: 2 * rows].astype(F32) + b for a, b in zip(sums, more)]
+        more = sent([a[rows:] for a in sums], 2, 1)
+        sums = [a[:rows] + b for a, b in zip(sums, more)]
         if g:
-            arriving.append(xor_send(here.astype(BF16), 4 * g))
+            arriving.append(sent(sums, 4 * g))
         else:
-            own = here
+            own = sums
     for more in arriving:
-        own = own + more.astype(F32)
+        own = [a + b for a, b in zip(own, more)]
     return own
 
 
-def exchanged(pieces, allowed):
-    count = lax.axis_size("seq")
-    return jnp.stack([pieces[0]] + [xor_send(pieces[j], j, None, allowed) for j in range(1, count)])
+def grouped(rows):
+    half = rows.shape[0] // 2
+    both = jnp.concatenate([rows[:half], core_swap(rows[half:])], axis=1)
+    return list(both.reshape(lax.axis_size("seq") // 4, -1, both.shape[1]))
+
+
+def after(value, *others):
+    return lax.optimization_barrier((value,) + others)[0]
+
+
+def all_to_all(pieces):
+    return lax.all_to_all(pieces, "seq", 0, 0, tiled=True)
 
 
 def params(**more):
     return pltpu.CompilerParams(vmem_limit_bytes=VMEM_BYTES, **more)
 
 
-def picked_body(index, source, target):
-    target[...] = source[...]
-
-
-def picked(blocks, index):
-    shape = blocks.shape[1:]
-    zeros = (0,) * len(shape)
+def pack_wide(gain, gate, value, contract, out, *, chips):
+    lanes = gate.shape[1]
+    live = pl.program_id(0) < chips
+    scale = jnp.where(live, gain[...], 0.0)
+    out[0, :, :lanes] = (gate[...].astype(F32) * scale).astype(BF16)
+    out[0, :, lanes : 2 * lanes] = (value[...].astype(F32) * scale).astype(BF16)
+    out[0, :, 2 * lanes :] = jnp.where(live, contract[...].astype(F32), 0.0).astype(BF16)
+
+
+def packed_wide(gain, gate, value, contract, count, lanes):
+    part, hidden = gate.shape
+    chips = hidden // lanes
+    column = pl.BlockSpec((part, lanes), lambda j: (0, jnp.minimum(j, chips - 1)))
     return pl.pallas_call(
-        picked_body,
-        out_shape=jax.ShapeDtypeStruct((index.shape[0],) + shape, blocks.dtype),
-        grid_spec=pltpu.PrefetchScalarGridSpec(
-            num_scalar_prefetch=1,
-            grid=(index.shape[0],),
-            in_specs=[pl.BlockSpec((1,) + shape, lambda j, at: (at[j],) + zeros)],
-            out_specs=pl.BlockSpec((1,) + shape, lambda j, at: (j,) + zeros),
-        ),
+        functools.partial(pack_wide, chips=chips),
+        out_shape=jax.ShapeDtypeStruct((count, part, 3 * lanes), BF16),
+        grid=(count,),
+        in_specs=[
+            pl.BlockSpec((part, 1), lambda j: (0, 0)),
+            column,
+            column,
+            column,
+        ],
+        out_specs=pl.BlockSpec((1, part, 3 * lanes), lambda j: (j, 0, 0)),
         compiler_params=params(),
-    )(index, blocks)
+    )(gain, gate, value, contract)
+
+
+def unpack_wide(grads, gain, gate, value, gate_out, value_out, contract_out, sums):
+    lanes = gate.shape[1]
+    gate_hat = grads[0, :, :lanes].astype(F32)
+    value_hat = grads[0, :, lanes : 2 * lanes].astype(F32)
+    gate_out[...] = gate_hat * gain[...]
+    value_out[...] = value_hat * gain[...]
+    contract_out[...] = grads[0, :, 2 * lanes :].astype(F32)
+    both = gate_hat * gate[...].astype(F32) + value_hat * value[...].astype(F32)
+
+    @pl.when(pl.program_id(0) == 0)
+    def _():
+        sums[...] = jnp.zeros_like(sums)
+
+    total = both[:, :LANES]
+    for start in range(LANES, lanes, LANES):
+        total = total + both[:, start : start + LANES]
+    sums[...] += total
+
+
+def unpacked_wide(grads, gain, gate, value, lanes):
+    part, hidden = gate.shape
+    column = pl.BlockSpec((part, lanes), lambda j: (0, j))
+    return pl.pallas_call(
+        unpack_wide,
+        out_shape=[
+            jax.ShapeDtypeStruct((part, hidden), F32),
+            jax.ShapeDtypeStruct((part, hidden), F32),
+            jax.ShapeDtypeStruct((part, hidden), F32),
+            jax.ShapeDtypeStruct((part, LANES), F32),
+        ],
+        grid=(hidden // lanes,),
+        in_specs=[
+            pl.BlockSpec((1, part, 3 * lanes), lambda j: (j, 0, 0)),
+            pl.BlockSpec((part, 1), lambda j: (0, 0)),
+            column,
+            column,
+        ],
+        out_specs=[
+            column,
+            column,
+            column,
+            pl.BlockSpec((part, LANES), lambda j: (0, 0)),
+        ],
+        compiler_params=params(),
+    )(grads, gain, gate, value)
+
+
+def pack_narrow(gain, gelu, scan, output, in_gate, de_gate, small, out):
+    extra = small.shape[1]
+    out[0, 0, :extra, :LANES] = in_gate[0]
+    out[0, 0, :extra, LANES : 2 * LANES] = de_gate[0]
+    out[0, 0, :extra, 2 * LANES :] = small[0]
+    out[0, 0, extra:, :LANES] = (gelu[...].astype(F32) * gain[...]).astype(BF16)
+    out[0, 0, extra:, LANES : 2 * LANES] = (scan[...].astype(F32) * gain[...]).astype(BF16)
+    out[0, 0, extra:, 2 * LANES :] = output[...]
+
+
+def packed_narrow(gain, gelu, scan, output, in_gate, de_gate, small):
+    part = gelu.shape[0]
+    local_blocks, extra = small.shape[:2]
+    column = pl.BlockSpec((part, LANES), lambda h, b: (0, 2 * b + h))
+    gate = pl.BlockSpec((1, extra, LANES), lambda h, b: (b, 0, h))
+    return pl.pallas_call(
+        pack_narrow,
+        out_shape=jax.ShapeDtypeStruct((2, local_blocks, extra + part, 3 * LANES), BF16),
+        grid=(2, local_blocks),
+        in_specs=[
+            pl.BlockSpec((part, 1), lambda h, b: (0, 0)),
+            column,
+            column,
+            column,
+            gate,
+            gate,
+            pl.BlockSpec((1, extra, LANES), lambda h, b: (b, 0, 0)),
+        ],
+        out_specs=pl.BlockSpec((1, 1, extra + part, 3 * LANES), lambda h, b: (h, b, 0, 0)),
+        compiler_params=params(),
+    )(gain, gelu, scan, output, in_gate, de_gate, small)
+
+
+def unpack_narrow(
+    grads, gain, gelu, scan, gelu_out, scan_out, output_out, in_out, de_out, sums, *, extra
+):
+    gelu_hat = grads[0, 0, extra:, :LANES].astype(F32)
+    scan_hat = grads[0, 0, extra:, LANES : 2 * LANES].astype(F32)
+    gelu_out[...] = gelu_hat * gain[...]
+    scan_out[...] = scan_hat * gain[...]
+    output_out[...] = grads[0, 0, extra:, 2 * LANES :].astype(F32)
+    rows = in_out.shape[1]
+    in_out[0] = grads[0, 0, :extra, :LANES].astype(F32)[:rows]
+    de_out[0] = grads[0, 0, :extra, LANES : 2 * LANES].astype(F32)[:rows]
+
+    @pl.when((pl.program_id(0) == 0) & (pl.program_id(1) == 0))
+    def _():
+        sums[...] = jnp.zeros_like(sums)
+
+    sums[...] += gelu_hat * gelu[...].astype(F32) + scan_hat * scan[...].astype(F32)
+
+
+def unpacked_narrow(grads, gain, gelu, scan, gate_rows):
+    part, width = gelu.shape
+    local_blocks = grads.shape[1]
+    extra = grads.shape[2] - part
+    column = pl.BlockSpec((part, LANES), lambda h, b: (0, 2 * b + h))
+    gate = pl.BlockSpec((1, gate_rows, LANES), lambda h, b: (b, 0, h))
+    return pl.pallas_call(
+        functools.partial(unpack_narrow, extra=extra),
+        out_shape=[
+            jax.ShapeDtypeStruct((part, width), F32),
+            jax.ShapeDtypeStruct((part, width), F32),
+            jax.ShapeDtypeStruct((part, width), F32),
+            jax.ShapeDtypeStruct((local_blocks, gate_rows, 2 * LANES), F32),
+            jax.ShapeDtypeStruct((local_blocks, gate_rows, 2 * LANES), F32),
+            jax.ShapeDtypeStruct((part, LANES), F32),
+        ],
+        grid=(2, local_blocks),
+        in_specs=[
+            pl.BlockSpec((1, 1, extra + part, 3 * LANES), lambda h, b: (h, b, 0, 0)),
+            pl.BlockSpec((part, 1), lambda h, b: (0, 0)),
+            column,
+            column,
+        ],
+        out_specs=[
+            column,
+            column,
+            column,
+            gate,
+            gate,
+            pl.BlockSpec((part, LANES), lambda h, b: (0, 0)),
+        ],
+        compiler_params=params(),
+    )(grads, gain, gelu, scan)
 
 
 def gelu_parts(w):
@@ -313,6 +469,21 @@
         return carry
 
     lax.fori_loop(0, total // th, order, 0)
+
+
+def feed_kernel(slot, ge, dz, zb, dge, *, th):
+    lanes = dz.shape[1]
+
+    def block(b, carry):
+        at = pl.ds(pl.multiple_of(b * th, th), th)
+        g, e, d = ge[at, :lanes], ge[at, lanes:], dz[at, :]
+        act, inner = gelu_parts(g)
+        zb[at, :] = (act * e).astype(BF16)
+        dge[at, :lanes] = (d * e * gelu_slope(g, inner)).astype(BF16)
+        dge[at, lanes:] = (d * act).astype(BF16)
+        return carry
+
+    lax.fori_loop(0, dz.shape[0] // th, block, 0)
 
 
 def on_chip(kernel, slot, inputs, outs, scratch=()):
@@ -352,8 +523,6 @@
     count = lax.axis_size("seq")
     chip = lax.axis_index("seq")
     core = lax.axis_index("head")
-    slots = jnp.arange(count, dtype=jnp.int32)
-    here = chip ^ slots
     th = block_input.shape[0] // 2
     width = block_input.shape[1]
     part = gelu_weight.shape[0]
@@ -374,28 +543,23 @@
     assert hidden_chips * lanes == hidden
 
     number = jnp.arange(2 * count, dtype=jnp.int32)
+    turn = lambda a: (a & ~3) | ((a & 1) << 1) | ((a >> 1) & 1)
     relative = chip ^ (number // 2)
-    turned = (relative & ~3) | ((relative & 1) << 1) | ((relative >> 1) & 1)
-    slot = jnp.where(number % 2 == 0, relative, turned) + jnp.where(
+    slot = jnp.where(number % 2 == 0, turn(relative), relative) + jnp.where(
         number % 2 == core, 0, count
     )
     slot = slot.astype(jnp.int32)
-
     x = lax.dynamic_slice_in_dim(block_input, core * th, th, 0).astype(F32)
     s1 = lax.rsqrt(jnp.mean(x * x, axis=-1, keepdims=True) + EPSILON)
-    first = gathered((x * s1).astype(BF16))
+    cotangent = lax.dynamic_slice_in_dim(output_cotangent, core * th, th, 0)
+    both = gathered(jnp.concatenate([(x * s1).astype(BF16), cotangent], axis=0))
+    both = [piece.reshape(4, 2, th, width) for piece in both]
+    first = [piece[:, 0].reshape(4 * th, width) for piece in both]
+    given_out = jnp.concatenate([piece[:, 1].reshape(4 * th, width) for piece in both])
 
     extra = max(16, gate_rows)
+    more_rows = ((0, 0), (0, extra - gate_rows), (0, 0))
     gain1 = first_gain.astype(F32)[:, None]
-    mats = jnp.stack(
-        [
-            (gelu_weight.astype(F32) * gain1).astype(BF16),
-            (scan_weight.astype(F32) * gain1).astype(BF16),
-            output_weight.T,
-        ],
-        axis=1,
-    ).reshape(part, 3, local_blocks, 2, LANES)
-    mats = mats.transpose(3, 2, 0, 1, 4).reshape(2, local_blocks, part, 3 * LANES)
     small = jnp.concatenate(
         [
             filter_taps.transpose(1, 0, 2),
@@ -408,25 +572,32 @@
     small = jnp.pad(
         small, ((0, 0), (0, extra - small.shape[1]), (0, LANES - small.shape[2]))
     )
-    gates = jnp.stack([input_gate, decay_gate], axis=2).reshape(
-        local_blocks, gate_rows, 2, 2, LANES
-    )
-    gates = jnp.pad(gates, ((0, 0), (0, extra - gate_rows), (0, 0), (0, 0), (0, 0)))
-    gates = gates.transpose(3, 0, 1, 2, 4).reshape(2, local_blocks, extra, 2 * LANES)
-    gates = jnp.concatenate([gates, jnp.broadcast_to(small, (2,) + small.shape)], axis=-1)
-    mats = jnp.concatenate([mats, gates], axis=2)
+    mats = packed_narrow(
+        gain1,
+        gelu_weight,
+        scan_weight,
+        output_weight.T,
+        jnp.pad(input_gate, more_rows),
+        jnp.pad(decay_gate, more_rows),
+        small,
+    )
     kept = lax.dynamic_index_in_dim(mats, core, 0, False)
     given = core_swap(lax.dynamic_index_in_dim(mats, 1 - core, 0, False))
-    mats = jnp.concatenate(
-        [jnp.where(core == 0, kept, given), jnp.where(core == 0, given, kept)], axis=0
-    )
-    mats = picked(mats, jnp.asarray(block_of, jnp.int32)[here])
-    mats = exchanged(mats, lambda source, target: target in gate_chips)
-    mats = picked(mats, here)
-    weights = mats[:, :part].reshape(width, 3 * LANES)
+    halves = [jnp.where(core == 0, kept, given), jnp.where(core == 0, given, kept)]
+    nothing = jnp.zeros_like(kept[0])
+    mats = jnp.stack(
+        [
+            halves[block_of[c] // local_blocks][block_of[c] % local_blocks]
+            if c in gate_chips
+            else nothing
+            for c in range(count)
+        ]
+    )
+    mats = all_to_all(mats)
+    weights = mats[:, extra:].reshape(width, 3 * LANES)
     weight_yv, weight_out = weights[:, : 2 * LANES], weights[:, 2 * LANES :]
-    gates = mats[:, part : part + gate_rows, : 2 * LANES].reshape(block_width, 2 * LANES)
-    small = mats[:, part : part + taps + 3, 2 * LANES : 2 * LANES + gate_rows]
+    gates = mats[:, :gate_rows, : 2 * LANES].reshape(block_width, 2 * LANES)
+    small = mats[:, : taps + 3, 2 * LANES : 2 * LANES + gate_rows]
     small = small.transpose(1, 0, 2).reshape(taps + 3, block_width)
     small = lax.dynamic_slice_in_dim(small, core * LANES, LANES, 1).astype(F32)
     tap_rows = jnp.pad(small[:taps], ((0, 8 - taps), (0, 0)))
@@ -441,23 +612,10 @@
     far_half = lambda a: lax.dynamic_slice_in_dim(a, (1 - core) * LANES, LANES, 0)
 
     gain2 = second_gain.astype(F32)[:, None]
-    wide = jnp.stack(
-        [
-            (expand_gate.astype(F32) * gain2).astype(BF16),
-            (expand_value.astype(F32) * gain2).astype(BF16),
-            contract_weight.T,
-        ],
-        axis=1,
-    ).reshape(part, 3, hidden_chips, lanes)
-    wide = wide.transpose(2, 0, 1, 3).reshape(hidden_chips, part, 3 * lanes)
-    wide = picked(wide, jnp.minimum(here, hidden_chips - 1).astype(jnp.int32))
-    wide = exchanged(wide, lambda source, target: target < hidden_chips)
-    wide = picked(wide, here).reshape(width, 3 * lanes)
-    wide_other = core_swap(wide)
-    cotangent = lax.dynamic_slice_in_dim(output_cotangent, core * th, th, 0)
-    given_out = gathered(cotangent)
-
-    yv = dot(first, weight_yv, ((1,), (0,)))
+    wide = packed_wide(gain2, expand_gate, expand_value, contract_weight.T, count, lanes)
+    wide = all_to_all(after(wide, *first)).reshape(width, 3 * lanes)
+
+    yv = jnp.concatenate([dot(piece, weight_yv, ((1,), (0,))) for piece in first])
     token_f32, token_bf16 = ((total, LANES), F32), ((total, LANES), BF16)
     padded = ((total + 8, LANES), F32)
     y, vp, c, cb = on_chip(
@@ -475,47 +633,50 @@
         [token_f32, token_f32, padded, token_bf16],
         [token_f32, token_f32],
     )
-    merged = jnp.concatenate([ob[:mine], core_swap(ob[mine:])], axis=1)
     out_both = jnp.concatenate([weight_out, weights_other[:, 2 * LANES :]], axis=1)
-    r = x + scattered(dot(merged, out_both, ((1,), (1,))))
+    weight_ge, weight_c = wide[:, : 2 * lanes], wide[:, 2 * lanes :]
+    dz = dot(given_out, weight_c, ((1,), (0,)))
+    merged = grouped(after(ob, wide))
+    merged[0] = after(merged[0], dz)
+    r = x + scattered((merged, out_both))[0]
 
     s2 = lax.rsqrt(jnp.mean(r * r, axis=-1, keepdims=True) + EPSILON)
     second = gathered((r * s2).astype(BF16))
-    weight_ge, weight_c = wide[:, : 2 * lanes], wide[:, 2 * lanes :]
-    ge = dot(second, weight_ge, ((1,), (0,)))
-    dz = dot(given_out, weight_c, ((1,), (0,)))
-    g, e = ge[:, :lanes], ge[:, lanes:]
-    act, inner = gelu_parts(g)
-    zb = (act * e).astype(BF16)
-    dgate = (dz * e * gelu_slope(g, inner)).astype(BF16)
-    dvalue = (dz * act).astype(BF16)
-    dge = jnp.concatenate([dgate, dvalue], axis=1)
-    dge_both = jnp.concatenate([dge[:mine], core_swap(dge[mine:])], axis=1)
-    ge_both = jnp.concatenate([weight_ge, wide_other[:, : 2 * lanes]], axis=1)
-    back2 = scattered(dot(dge_both, ge_both, ((1,), (1,))))
+    second = jnp.concatenate(second)
+    zb, dge = on_chip(
+        functools.partial(feed_kernel, th=th),
+        slot,
+        [dot(second, weight_ge, ((1,), (0,))), dz],
+        [((total, lanes), BF16), ((total, 2 * lanes), BF16)],
+    )
+    ge_both = jnp.concatenate([weight_ge, core_swap(weight_ge)], axis=1)
+    c_both = jnp.concatenate([weight_c, core_swap(weight_c)], axis=1)
+    (back2,) = scattered((grouped(dge), ge_both))
     dr = (
         cotangent.astype(F32)
         + s2 * back2
         - r * (s2 * s2 * s2) * jnp.mean(back2 * r, axis=-1, keepdims=True)
     )
-    zb_both = jnp.concatenate([zb[:mine], core_swap(zb[mine:])], axis=1)
-    c_both = jnp.concatenate([weight_c, wide_other[:, 2 * lanes :]], axis=1)
-    out_half = (r + scattered(dot(zb_both, c_both, ((1,), (1,))))).astype(BF16)
+    dq = gathered(dr.astype(BF16))
 
     wide_grad = jnp.concatenate(
-        [dot(second, dge, ((0,), (0,))), dot(given_out, zb, ((0,), (0,)))], axis=1
-    ).astype(BF16)
-    wide_grad = picked(wide_grad.reshape(count, part, 3 * lanes), here)
-    wide_grad = exchanged(wide_grad, lambda source, target: source < hidden_chips)
-    wide_grad = picked(wide_grad, here)[:hidden_chips].astype(F32)
-    wide_grad = wide_grad.transpose(1, 0, 2).reshape(part, hidden_chips, 3, lanes)
-    gate_hat, value_hat, contract_t = (wide_grad[:, :, i].reshape(part, hidden) for i in range(3))
-    gain2_part = jnp.sum(
-        gate_hat * expand_gate.astype(F32) + value_hat * expand_value.astype(F32), axis=1
-    )
-
-    dq = gathered(dr.astype(BF16))
-    dob = dot(dq, weight_out, ((1,), (0,)))
+        lax.optimization_barrier(
+            (
+                dot(second, dge, ((0,), (0,))).astype(BF16),
+                dot(given_out, zb, ((0,), (0,))).astype(BF16),
+            )
+        ),
+        axis=1,
+    )
+    *dq, wide_grad = lax.optimization_barrier((*dq, wide_grad))
+    (out_sum,) = scattered((grouped(after(zb, back2)), c_both))
+    out_half = (r + out_sum).astype(BF16)
+    wide_grad = all_to_all(wide_grad.reshape(count, part, 3 * lanes))
+    gate_grad_out, value_grad_out, contract_grad_out, gain2_part = unpacked_wide(
+        wide_grad, gain2, expand_gate, expand_value, lanes
+    )
+
+    dob = jnp.concatenate([dot(piece, weight_out, ((1,), (0,))) for piece in dq])
     dy, dpp, dc, sums = on_chip(
         functools.partial(adjoint_kernel, th=th),
         slot,
@@ -532,14 +693,15 @@
         [padded],
     )
     dyv = jnp.concatenate([dy, dv], axis=1)
-    dyv_both = jnp.concatenate([dyv[:mine], core_swap(dyv[mine:])], axis=1)
-    yv_both = jnp.concatenate([weight_yv, weights_other[:, : 2 * LANES]], axis=1)
-    back1 = scattered(dot(dyv_both, yv_both, ((1,), (1,))))
-    in_half = dr + s1 * back1 - x * (s1 * s1 * s1) * jnp.mean(back1 * x, axis=-1, keepdims=True)
-
-    yv_grad = dot(first, dyv, ((0,), (0,)))
-    out_grad = dot(dq, ob, ((0,), (0,)))
-    weight_grad = jnp.concatenate([yv_grad, out_grad], axis=1).astype(BF16)
+    weight_grad = jnp.concatenate(
+        lax.optimization_barrier(
+            (
+                dot(jnp.concatenate(first), dyv, ((0,), (0,))).astype(BF16),
+                dot(jnp.concatenate(dq), ob, ((0,), (0,))).astype(BF16),
+            )
+        ),
+        axis=1,
+    )
     weight_grad = weight_grad.reshape(count, part, 3 * LANES)
     own_grad, far_grad = dot(cb, dpp, ((0,), (0,))), dot(cb_other, dpp, ((0,), (0,)))
     gate_grad = jnp.concatenate(
@@ -563,30 +725,30 @@
         small_grad, ((0, 0), (0, extra - taps - 3), (0, LANES - gate_rows))
     )
     gate_grad = jnp.concatenate([gate_grad, small_grad], axis=-1).astype(BF16)
-    weight_grad = jnp.concatenate([weight_grad, gate_grad], axis=1)
-    weight_grad = picked(weight_grad, here)
-    weight_grad = exchanged(weight_grad, lambda source, target: source in gate_chips)
-    weight_grad = picked(weight_grad, (jnp.asarray(chip_of, jnp.int32) ^ chip).astype(jnp.int32))
-    kept = lax.dynamic_slice_in_dim(weight_grad, core * local_blocks, local_blocks, 0)
-    given = lax.dynamic_slice_in_dim(weight_grad, (1 - core) * local_blocks, local_blocks, 0)
-    given = core_swap(given)
-    halves = jnp.stack(
-        [jnp.where(core == 0, kept, given), jnp.where(core == 0, given, kept)], axis=0
-    ).astype(F32)
-    mats_grad = halves[:, :, :part].reshape(2, local_blocks, part, 3, LANES)
-    mats_grad = mats_grad.transpose(3, 2, 1, 0, 4).reshape(3, part, local_blocks * block_width)
-    gates_grad = halves[:, :, part : part + gate_rows, : 2 * LANES]
-    gates_grad = gates_grad.reshape(2, local_blocks, gate_rows, 2, LANES)
-    gates_grad = gates_grad.transpose(3, 1, 2, 0, 4).reshape(
-        2, local_blocks, gate_rows, block_width
-    )
-    small_sum = halves[0, :, part:, 2 * LANES :] + halves[1, :, part:, 2 * LANES :]
-    small_sum = small_sum[:, : taps + 3, :gate_rows].transpose(1, 0, 2)
-    gain1_part = jnp.sum(
-        mats_grad[0] * gelu_weight.astype(F32) + mats_grad[1] * scan_weight.astype(F32), axis=1
-    )
-
-    gain_parts = jnp.stack([gain1_part, gain2_part])
+    weight_grad = all_to_all(after(jnp.concatenate([gate_grad, weight_grad], axis=1), wide_grad))
+    low = jnp.stack([weight_grad[c] for c in chip_of[:local_blocks]])
+    high = jnp.stack([weight_grad[c] for c in chip_of[local_blocks:]])
+    kept = jnp.where(core == 0, low, high)
+    given = core_swap(jnp.where(core == 0, high, low))
+    halves = jnp.stack([jnp.where(core == 0, kept, given), jnp.where(core == 0, given, kept)])
+    (
+        gelu_grad_out,
+        scan_grad_out,
+        output_grad_out,
+        input_gate_out,
+        decay_gate_out,
+        gain1_part,
+    ) = unpacked_narrow(halves, gain1, gelu_weight, scan_weight, gate_rows)
+    small_sum = halves[:, :, : taps + 3, 2 * LANES : 2 * LANES + gate_rows].astype(F32)
+    small_sum = (small_sum[0] + small_sum[1]).transpose(1, 0, 2)
+
+    yv_both = jnp.concatenate([weight_yv, weights_other[:, : 2 * LANES]], axis=1)
+    back1 = grouped(after(dyv, wide_grad))
+    back1[0] = after(back1[0], gain1_part, gain2_part, out_half)
+    (back1,) = scattered((back1, yv_both))
+    in_half = dr + s1 * back1 - x * (s1 * s1 * s1) * jnp.mean(back1 * x, axis=-1, keepdims=True)
+
+    gain_parts = jnp.stack([jnp.sum(gain1_part, axis=1), jnp.sum(gain2_part, axis=1)])
     gain_grads = gain_parts + core_swap(gain_parts)
 
     def both_halves(half):
@@ -599,19 +761,19 @@
         both_halves(out_half),
         both_halves(in_half),
         gain_grads[0],
-        mats_grad[0] * gain1,
-        mats_grad[1] * gain1,
+        gelu_grad_out,
+        scan_grad_out,
         small_sum[:taps],
-        gates_grad[0],
+        input_gate_out,
         small_sum[taps],
-        gates_grad[1],
+        decay_gate_out,
         small_sum[taps + 1],
         small_sum[taps + 2],
-        mats_grad[2].T,
+        output_grad_out.T,
         gain_grads[1],
-        gate_hat * gain2,
-        value_hat * gain2,
-        contract_t.T,
+        gate_grad_out,
+        value_grad_out,
+        contract_grad_out.T,
     )
 
 

time: 1560 us -> 883 us (0.57)
  starting transfers between devices: 606 us -> 205 us
  local copies, waits for them, and re-layouts: 221 us -> 90.4 us
  waiting for transfers between devices: 439 us -> 371 us
  other arithmetic: 79.5 us -> 37.7 us
  Pallas kernels: 115 us -> 77 us
    ppermute x180 -> x77, starting transfers between devices: 542 us -> 99.1 us  [xor_send(): return lax.ppermute(value, BOTH, pairs)]
    ppermute x180 -> x77, waiting for transfers between devices: 431 us -> 305 us  [xor_send(): return lax.ppermute(value, BOTH, pairs)]
    all_to_all x0 -> x4, waiting for transfers between devices: none -> 63.9 us  [all_to_all(): return lax.all_to_all(pieces, 'seq', 0, 0, tiled=True)]
    pallas_call x8 -> x4, Pallas kernels: 81.1 us -> 36.5 us  [the longest x1 12 us: unpacked_wide(): pl.pallas_call(unpack_wide, out_shape=[jax.ShapeDtypeStruct((part, hidden...]
    all_to_all x0 -> x4, starting transfers between devices: none -> 43.8 us  [all_to_all(): return lax.all_to_all(pieces, 'seq', 0, 0, tiled=True)]
    unnamed x297 -> x231, local copies, waits for them, and re-layouts: 77.9 us -> 46.7 us
    reshape x6 -> x0, local copies, waits for them, and re-layouts: 29.2 us -> none  [the longest x1 12.3 us: shards(): wide_grad.transpose(1, 0, 2).reshape(part, hidden_chips, 3, lanes)]
    slice x19 -> x48, local copies, waits for them, and re-layouts: 46.4 us -> 21.7 us  [the longest x8 13 us: shards(): piece[:, 1].reshape(4 * th, width)]
  transfers between devices with their start and end apart: 210 -> 108, of which waited for: 87 -> 39; matrix products, arithmetic and copies ran while one was open for 20% -> 21% of each run, Pallas kernels for 5% -> 9%
where the time goes in v2:
time: 883 us; the launch traced here: 872 us
  waiting for transfers between devices  371 us (42%)
  starting transfers between devices  205 us (23%)
  local copies, waits for them, and re-layouts  90.4 us (10%)
  matrix products  87.3 us (10%)
  Pallas kernels  77 us (9%)
  other arithmetic  37.7 us (4%)
    ppermute x77, waiting for transfers between devices, xor_send(): return lax.ppermute(value, BOTH, pairs)  305 us
    ppermute x77, starting transfers between devices, xor_send(): return lax.ppermute(value, BOTH, pairs)  99.1 us
    dot_general x40, matrix products, dot(): lax.dot_general(left, right, (over, ((), ())), preferred_element_type=F32)  87.3 us
    all_to_all x4, waiting for transfers between devices, all_to_all(): return lax.all_to_all(pieces, 'seq', 0, 0, tiled=True)  63.9 us
    ppermute x27, starting transfers between devices, core_swap(): return lax.ppermute(value, 'head', [(0, 1), (1, 0)])  62.5 us
    unnamed x231, local copies, waits for them, and re-layouts  46.7 us
    all_to_all x4, starting transfers between devices, all_to_all(): return lax.all_to_all(pieces, 'seq', 0, 0, tiled=True)  43.8 us
    pallas_call x5, Pallas kernels, on_chip(): pl.pallas_call(kernel, out_shape=[jax.ShapeDtypeStruct(shape, dtype) for...  40.5 us
  transfers between devices with their start and end apart: 108, of which 39 were waited for; matrix products, arithmetic and copies ran while one was open for 21% of the time, Pallas kernels for 9%

profile of v2, /device:TPU:5, one launch (start us, length us, event | category | flops | bytes accessed | tf_op | source)
XLA Modules:
  0.0 871.8 jit_solution(12867238521705329669)
XLA Ops:
  10.9 6.8 shard_map.279
  20.2 10.5 %shard_map.282 = bf16[16,160,768]{2,1,0:T(8,128)(2,1)} custom-call(f32[160,1]{1,0:T(8,128)} %copy.41.gain, bf16[160,3840]{1,0:T(8,128)(2,1)} %gate.3, bf16[160,3840]{1,0:T(8,128)(2,1)} %value.3, bf16[160,3840]{1,0:T(8,128)(2,1)} %bitcast.154), custom_call_target="tpu_custom_call" | custom-call | tf_op jit(solution)/shard_map/pallas_call | solution.py:104
  39.8 12.7 %collective-permute-done.9 = bf16[128,2560]{1,0:T(8,128)(2,1)} collective-permute-done((bf16[128,2560]{1,0:T(8,128)(2,1)S(1)}, bf16[128,2560]{1,0:T(8,128)(2,1)}, u32[]{:S(2)}, u32[]{:S(2)}) %collective-permute-start.9) | collective-permute-done | bytes 655392 | tf_op jit(solution)/shard_map/ppermute | solution.py:30
  64.9 18.8 %all-to-all-start = ((bf16[16,176,384]{2,1,0:T(8,128)(2,1)}), bf16[16,176,384]{2,1,0:T(8,128)(2,1)S(1)}, u32[]{:S(2)}, u32[]{:S(2)}) async-start(bf16[16,176,384]{2,1,0:T(8,128)(2,1)} %constant_dynamic-update-slice_fusion), calls=%async_computation | async-start | bytes 4325376 | tf_op jit(solution)/shard_map/all_to_all | solution.py:84
  99.0 20.6 %collective-permute-done.5 = bf16[256,2560]{1,0:T(8,128)(2,1)S(1)} collective-permute-done((bf16[256,2560]{1,0:T(8,128)(2,1)S(1)}, bf16[256,2560]{1,0:T(8,128)(2,1)S(1)}, u32[]{:S(2)}, u32[]{:S(2)}) %collective-permute-start.5) | collective-permute-done | bytes 1310752 | tf_op jit(solution)/shard_map/ppermute | solution.py:30
  119.7 16.8 %collective-permute-done.8 = bf16[256,2560]{1,0:T(8,128)(2,1)S(1)} collective-permute-done((bf16[256,2560]{1,0:T(8,128)(2,1)S(1)}, bf16[256,2560]{1,0:T(8,128)(2,1)S(1)}, u32[]{:S(2)}, u32[]{:S(2)}) %collective-permute-start.8) | collective-permute-done | bytes 1310752 | tf_op jit(solution)/shard_map/ppermute | solution.py:30
  142.8 7.8 collective-permute-done.11
  196.5 10.7 %shard_map.281 = (f32[2048,128]{1,0:T(8,128)}, f32[2048,128]{1,0:T(8,128)}, f32[2056,128]{1,0:T(8,128)}, bf16[2048,128]{1,0:T(8,128)(2,1)}) custom-call(s32[32]{0:T(128)} %fusion.77.slot, bf16[2048,128]{1,0:T(8,128)(2,1)} %get-tuple-element.62.cbo, bf16[2048,128]{1,0:T(8,128)(2,1)} %copy-done.35, bf16[128,256]{1,0:T(8,128)(2,1)} %get-tuple-element.158.near, ...), custom_call_target="tpu_custom_call" | custom-call | tf_op jit(solution)/shard_map/pallas_call | solution.py:491
  208.3 37.5 %all-to-all-done.1 = bf16[16,160,768]{2,1,0:T(8,128)(2,1)} async-done(((bf16[16,160,768]{2,1,0:T(8,128)(2,1)}), bf16[16,160,768]{2,1,0:T(8,128)(2,1)}, u32[]{:S(2)}, u32[]{:S(2)}) %all-to-all-start.1) | async-done | bytes 3932192 | tf_op jit(solution)/shard_map/all_to_all | solution.py:84
  248.8 8.5 fusion.95.dz
  269.9 7.3 collective-permute-done.24
  279.6 8.2 collective-permute-done.21
  290.1 8.2 collective-permute-done.19
  300.7 10.2 %collective-permute-start.29 = (bf16[64,2560]{1,0:T(8,128)(2,1)S(1)}, bf16[64,2560]{1,0:T(8,128)(2,1)S(1)}, u32[]{:S(2)}, u32[]{:S(2)}) collective-permute-start(bf16[64,2560]{1,0:T(8,128)(2,1)S(1)} %fusion.30), channel_id=1, source_target_pairs={{0,24},{1,25},{2,26},{3,27},{4,28},{5,29},{6,30},{7,31},{8,16},{9,... | collective-permute-start | bytes 983048 | tf_op jit(solution)/shard_map/ppermute | solution.py:30
  312.4 4.9 collective-permute-done.29
  317.2 23.0 %collective-permute-done.26 = bf16[64,2560]{1,0:T(8,128)(2,1)S(1)} collective-permute-done((bf16[64,2560]{1,0:T(8,128)(2,1)S(1)}, bf16[64,2560]{1,0:T(8,128)(2,1)S(1)}, u32[]{:S(2)}, u32[]{:S(2)}) %collective-permute-start.26) | collective-permute-done | bytes 327712 | tf_op jit(solution)/shard_map/ppermute | solution.py:30
  348.6 10.8 %collective-permute-done.32 = bf16[64,2560]{1,0:T(8,128)(2,1)S(1)} collective-permute-done((bf16[64,2560]{1,0:T(8,128)(2,1)S(1)}, bf16[64,2560]{1,0:T(8,128)(2,1)S(1)}, u32[]{:S(2)}, u32[]{:S(2)}) %collective-permute-start.32) | collective-permute-done | bytes 327712 | tf_op jit(solution)/shard_map/ppermute | solution.py:30
  360.3 8.8 %collective-permute-start.36 = (bf16[64,2560]{1,0:T(8,128)(2,1)S(1)}, bf16[64,2560]{1,0:T(8,128)(2,1)S(1)}, u32[]{:S(2)}, u32[]{:S(2)}) collective-permute-start(bf16[64,2560]{1,0:T(8,128)(2,1)S(1)} %collective-permute-done.35), channel_id=1, source_target_pairs={{0,4},{1,3},{2,6},{3,1},{4,0},{5,7},{6,2},{7,5},{8,12},{9,11},{10,... | collective-permute-start | bytes 983048 | tf_op jit(solution)/shard_map/ppermute | solution.py:30
  381.3 7.5 collective-permute-start.41
  393.3 6.6 collective-permute-done.40
  407.0 9.1 %fusion.97.ge = f32[2048,512]{1,0:T(8,128)} fusion(bf16[2048,2560]{1,0:T(8,128)(2,1)S(1)} %constant_dynamic-update-slice_fusion.25, bf16[2560,768]{1,0:T(8,128)(2,1)} %bitcast.29), kind=kOutput, calls=%fused_computation.361 | convolution fusion | flops 5368709120 | bytes 17301504 | tf_op jit(solution)/shard_map/dot_general | solution.py:502
  416.1 6.5 shard_map.283
  440.4 7.8 collective-permute-done.52
  450.0 8.8 %collective-permute-done.49 = bf16[128,2560]{1,0:T(8,128)(2,1)S(1)} collective-permute-done((bf16[128,2560]{1,0:T(8,128)(2,1)S(1)}, bf16[128,2560]{1,0:T(8,128)(2,1)S(1)}, u32[]{:S(2)}, u32[]{:S(2)}) %collective-permute-start.49) | collective-permute-done | bytes 655392 | tf_op jit(solution)/shard_map/ppermute | solution.py:30
  460.5 8.8 %collective-permute-done.47 = bf16[128,2560]{1,0:T(8,128)(2,1)S(1)} collective-permute-done((bf16[128,2560]{1,0:T(8,128)(2,1)S(1)}, bf16[128,2560]{1,0:T(8,128)(2,1)S(1)}, u32[]{:S(2)}, u32[]{:S(2)}) %collective-permute-start.47) | collective-permute-done | bytes 655392 | tf_op jit(solution)/shard_map/ppermute | solution.py:30
  480.7 23.0 %collective-permute-done.54 = bf16[64,2560]{1,0:T(8,128)(2,1)S(1)} collective-permute-done((bf16[64,2560]{1,0:T(8,128)(2,1)S(1)}, bf16[64,2560]{1,0:T(8,128)(2,1)S(1)}, u32[]{:S(2)}, u32[]{:S(2)}) %collective-permute-start.54) | collective-permute-done | bytes 327712 | tf_op jit(solution)/shard_map/ppermute | solution.py:30
  518.6 8.9 %collective-permute-done.65 = bf16[128,2560]{1,0:T(8,128)(2,1)S(1)} collective-permute-done((bf16[128,2560]{1,0:T(8,128)(2,1)S(1)}, bf16[128,2560]{1,0:T(8,128)(2,1)S(1)}, u32[]{:S(2)}, u32[]{:S(2)}) %collective-permute-start.65) | collective-permute-done | bytes 655392 | tf_op jit(solution)/shard_map/ppermute | solution.py:30
  527.8 10.2 %collective-permute-done.62 = bf16[128,2560]{1,0:T(8,128)(2,1)S(1)} collective-permute-done((bf16[128,2560]{1,0:T(8,128)(2,1)S(1)}, bf16[128,2560]{1,0:T(8,128)(2,1)S(1)}, u32[]{:S(2)}, u32[]{:S(2)}) %collective-permute-start.62) | collective-permute-done | bytes 655392 | tf_op jit(solution)/shard_map/ppermute | solution.py:30
  538.3 10.2 %collective-permute-done.60 = bf16[128,2560]{1,0:T(8,128)(2,1)S(1)} collective-permute-done((bf16[128,2560]{1,0:T(8,128)(2,1)S(1)}, bf16[128,2560]{1,0:T(8,128)(2,1)S(1)}, u32[]{:S(2)}, u32[]{:S(2)}) %collective-permute-start.60) | collective-permute-done | bytes 655392 | tf_op jit(solution)/shard_map/ppermute | solution.py:30
  557.1 19.9 %collective-permute-done.67 = bf16[64,2560]{1,0:T(8,128)(2,1)S(1)} collective-permute-done((bf16[64,2560]{1,0:T(8,128)(2,1)S(1)}, bf16[64,2560]{1,0:T(8,128)(2,1)S(1)}, u32[]{:S(2)}, u32[]{:S(2)}) %collective-permute-start.67) | collective-permute-done | bytes 327712 | tf_op jit(solution)/shard_map/ppermute | solution.py:30
  579.0 8.8 %convolution_convert_fusion = bf16[2560,512]{1,0:T(8,128)(2,1)S(1)} fusion(bf16[2048,2560]{1,0:T(8,128)(2,1)} %copy-done.75, bf16[2048,512]{1,0:T(8,128)(2,1)S(1)} %copy-done.34), kind=kOutput, calls=%fused_computation.1 | convolution fusion | flops 5370019840 | bytes 15204352 | tf_op jit(solution)/shard_map/dot_general | solution.py:502
  591.9 9.5 %collective-permute-done.74 = bf16[64,2560]{1,0:T(8,128)(2,1)S(1)} collective-permute-done((bf16[64,2560]{1,0:T(8,128)(2,1)S(1)}, bf16[64,2560]{1,0:T(8,128)(2,1)S(1)}, u32[]{:S(2)}, u32[]{:S(2)}) %collective-permute-start.74) | collective-permute-done | bytes 327712 | tf_op jit(solution)/shard_map/ppermute | solution.py:30
  603.2 8.4 collective-permute-start.78
  620.2 14.0 %collective-permute-start.83 = (bf16[256,2560]{1,0:T(8,128)(2,1)S(1)}, bf16[256,2560]{1,0:T(8,128)(2,1)S(1)}, u32[]{:S(2)}, u32[]{:S(2)}) collective-permute-start(bf16[256,2560]{1,0:T(8,128)(2,1)S(1)} %pad_maximum_fusion.16), channel_id=1, source_target_pairs={{0,1},{1,0},{2,3},{3,2},{4,5},{5,4},{6,7},{7,6},{8,9},{9,8},{10,11... | collective-permute-start | bytes 3932168 | tf_op jit(solution)/shard_map/ppermute | solution.py:34
  637.0 5.7 collective-permute-done.82
  644.0 6.9 convolution_convert_fusion.6
  655.9 6.0 all-to-all-start.2
  671.6 11.8 %shard_map.284 = (bf16[2048,128]{1,0:T(8,128)(2,1)}, bf16[2048,256]{1,0:T(8,128)(2,1)}, f32[2048,128]{1,0:T(8,128)}, f32[8,128]{1,0:T(8,128)}) custom-call(s32[32]{0:T(128)} %fusion.77.slot, f32[2048,128]{1,0:T(8,128)} %convolution_dynamic-update-slice_fusion.8.dob, f32[2048,128]{1,0:T(8,128)} %get-tuple-element.64.y, f32[2056,128]{1,0:T(8,128)} %get-tuple-element.82.hp, ...), custom_call_target="tpu_custom_call" | custom-call | tf_op jit(solution)/shard_map/pallas_call | solution.py:491
  697.5 7.1 shard_map.285
  706.5 6.9 convolution_convert_fusion.5
  715.3 26.4 %all-to-all-done.2.grads = bf16[16,160,768]{2,1,0:T(8,128)(2,1)} async-done(((bf16[16,160,768]{2,1,0:T(8,128)(2,1)}), bf16[16,160,768]{2,1,0:T(8,128)(2,1)}, u32[]{:S(2)}, u32[]{:S(2)}) %all-to-all-start.2) | async-done | bytes 3932192 | tf_op jit(solution)/shard_map/all_to_all | solution.py:84
  744.2 14.4 %all-to-all-start.3 = ((bf16[16,176,384]{2,1,0:T(8,128)(2,1)}), bf16[16,176,384]{2,1,0:T(8,128)(2,1)S(1)}, u32[]{:S(2)}, u32[]{:S(2)}) async-start(bf16[16,176,384]{2,1,0:T(8,128)(2,1)} %fusion.4), calls=%async_computation.3 | async-start | bytes 4325376 | tf_op jit(solution)/shard_map/all_to_all | solution.py:84
  765.5 12.0 %shard_map.287 = (f32[160,3840]{1,0:T(8,128)}, f32[160,3840]{1,0:T(8,128)}, f32[160,3840]{1,0:T(8,128)}, f32[160,128]{1,0:T(8,128)}) custom-call(bf16[16,160,768]{2,1,0:T(8,128)(2,1)} %all-to-all-done.2.grads, f32[160,1]{1,0:T(8,128)} %copy.41.gain, bf16[160,3840]{1,0:T(8,128)(2,1)} %gate.3, bf16[160,3840]{1,0:T(8,128)(2,1)} %value.3), custom_call_target="tpu_custom_call" | custom-call | tf_op jit(solution)/shard_map/pallas_call | solution.py:141
  786.5 13.8 %collective-permute-done.96 = bf16[128,2560]{1,0:T(8,128)(2,1)S(1)} collective-permute-done((bf16[128,2560]{1,0:T(8,128)(2,1)S(1)}, bf16[128,2560]{1,0:T(8,128)(2,1)S(1)}, u32[]{:S(2)}, u32[]{:S(2)}) %collective-permute-start.96) | collective-permute-done | bytes 655392 | tf_op jit(solution)/shard_map/ppermute | solution.py:30
  802.7 7.5 collective-permute-done.93
  814.4 14.7 %collective-permute-start.90 = (bf16[5,176,384]{2,1,0:T(8,128)(2,1)S(1)}, bf16[5,176,384]{2,1,0:T(8,128)(2,1)S(1)}, u32[]{:S(2)}, u32[]{:S(2)}) collective-permute-start(bf16[5,176,384]{2,1,0:T(8,128)(2,1)S(1)} %broadcast_select_fusion), channel_id=1, source_target_pairs={{0,1},{1,0},{2,3},{3,2},{4,5},{5,4},{6,7},{7,6},{8,9},{9,8},{10,11... | collective-permute-start | bytes 2027528 | tf_op jit(solution)/shard_map/ppermute | solution.py:34
  835.3 7.3 shard_map.286
  849.0 5.5 collective-permute-done.91
  (628 shorter events, 322.8 us)
Async XLA Ops:
  4.6 26.2 %collective-permute-start = (bf16[128,2560]{1,0:T(8,128)(2,1)S(1)}, bf16[128,2560]{1,0:T(8,128)(2,1)S(1)}, u32[]{:S(2)}, u32[]{:S(2)}) collective-permute-start(bf16[128,2560]{1,0:T(8,128)(2,1)S(1)} %pad_maximum_fusion.20), channel_id=1, source_target_pairs={{0,4},{1,3},{2,6},{3,1},{4,0},{5,7},{6,2},{7,5},{8,12},{9,11},{10,... | collective-permute-start | bytes 1966088 | tf_op jit(solution)/shard_map/ppermute | solution.py:30
  5.8 30.5 %collective-permute-start.3 = (bf16[128,2560]{1,0:T(8,128)(2,1)S(1)}, bf16[128,2560]{1,0:T(8,128)(2,1)}, u32[]{:S(2)}, u32[]{:S(2)}) collective-permute-start(bf16[128,2560]{1,0:T(8,128)(2,1)S(1)} %pad_maximum_fusion.20), channel_id=1, source_target_pairs={{0,8},{1,9},{2,10},{3,11},{4,12},{5,13},{6,14},{7,15},{8,0},{9,1},... | collective-permute-start | bytes 1966088 | tf_op jit(solution)/shard_map/ppermute | solution.py:30
  7.1 29.2 %collective-permute-start.6 = (bf16[128,2560]{1,0:T(8,128)(2,1)S(1)}, bf16[128,2560]{1,0:T(8,128)(2,1)}, u32[]{:S(2)}, u32[]{:S(2)}) collective-permute-start(bf16[128,2560]{1,0:T(8,128)(2,1)S(1)} %pad_maximum_fusion.20), channel_id=1, source_target_pairs={{0,16},{1,17},{2,18},{3,19},{4,20},{5,21},{6,22},{7,23},{8,24},{9,... | collective-permute-start | bytes 1966088 | tf_op jit(solution)/shard_map/ppermute | solution.py:30
  9.4 43.1 %collective-permute-start.9 = (bf16[128,2560]{1,0:T(8,128)(2,1)S(1)}, bf16[128,2560]{1,0:T(8,128)(2,1)}, u32[]{:S(2)}, u32[]{:S(2)}) collective-permute-start(bf16[128,2560]{1,0:T(8,128)(2,1)S(1)} %pad_maximum_fusion.20), channel_id=1, source_target_pairs={{0,24},{1,25},{2,26},{3,27},{4,28},{5,29},{6,30},{7,31},{8,16},{9,... | collective-permute-start | bytes 1966088 | tf_op jit(solution)/shard_map/ppermute | solution.py:30
  18.9 37.6 %collective-permute-start.2 = (bf16[5,176,384]{2,1,0:T(8,128)(2,1)S(1)}, bf16[5,176,384]{2,1,0:T(8,128)(2,1)S(1)}, u32[]{:S(2)}, u32[]{:S(2)}) collective-permute-start(bf16[5,176,384]{2,1,0:T(8,128)(2,1)S(1)} %dynamic-slice_bitcast_fusion), channel_id=1, source_target_pairs={{0,1},{1,0},{2,3},{3,2},{4,5},{5,4},{6,7},{7,6},{8,9},{9,8},{10,11... | collective-permute-start | bytes 2027528 | tf_op jit(solution)/shard_map/ppermute | solution.py:34
  31.9 61.7 %collective-permute-start.1 = (bf16[256,2560]{1,0:T(8,128)(2,1)}, bf16[256,2560]{1,0:T(8,128)(2,1)}, u32[]{:S(2)}, u32[]{:S(2)}) collective-permute-start(bf16[256,2560]{1,0:T(8,128)(2,1)} %pad_maximum_fusion.7), channel_id=1, source_target_pairs={{0,2},{1,5},{2,0},{3,7},{4,6},{5,1},{6,4},{7,3},{8,10},{9,13},{10,... | collective-permute-start | bytes 3932168 | tf_op jit(solution)/shard_map/ppermute | solution.py:30
  36.3 47.4 %collective-permute-start.4 = (bf16[128,2560]{1,0:T(8,128)(2,1)}, bf16[128,2560]{1,0:T(8,128)(2,1)}, u32[]{:S(2)}, u32[]{:S(2)}) collective-permute-start(bf16[128,2560]{1,0:T(8,128)(2,1)} %collective-permute-done.3), channel_id=1, source_target_pairs={{0,4},{1,3},{2,6},{3,1},{4,0},{5,7},{6,2},{7,5},{8,12},{9,11},{10,... | collective-permute-start | bytes 1966088 | tf_op jit(solution)/shard_map/ppermute | solution.py:30
  36.3 49.1 %collective-permute-start.7 = (bf16[128,2560]{1,0:T(8,128)(2,1)}, bf16[128,2560]{1,0:T(8,128)(2,1)}, u32[]{:S(2)}, u32[]{:S(2)}) collective-permute-start(bf16[128,2560]{1,0:T(8,128)(2,1)} %collective-permute-done.6), channel_id=1, source_target_pairs={{0,4},{1,3},{2,6},{3,1},{4,0},{5,7},{6,2},{7,5},{8,12},{9,11},{10,... | collective-permute-start | bytes 1966088 | tf_op jit(solution)/shard_map/ppermute | solution.py:30
  52.5 35.9 %collective-permute-start.10 = (bf16[128,2560]{1,0:T(8,128)(2,1)}, bf16[128,2560]{1,0:T(8,128)(2,1)}, u32[]{:S(2)}, u32[]{:S(2)}) collective-permute-start(bf16[128,2560]{1,0:T(8,128)(2,1)} %collective-permute-done.9), channel_id=1, source_target_pairs={{0,4},{1,3},{2,6},{3,1},{4,0},{5,7},{6,2},{7,5},{8,12},{9,11},{10,... | collective-permute-start | bytes 1966088 | tf_op jit(solution)/shard_map/ppermute | solution.py:30
  64.9 97.0 %all-to-all-start = ((bf16[16,176,384]{2,1,0:T(8,128)(2,1)}), bf16[16,176,384]{2,1,0:T(8,128)(2,1)S(1)}, u32[]{:S(2)}, u32[]{:S(2)}) async-start(bf16[16,176,384]{2,1,0:T(8,128)(2,1)} %constant_dynamic-update-slice_fusion), calls=%async_computation | async-start | bytes 4325376 | tf_op jit(solution)/shard_map/all_to_all | solution.py:84
  85.3 34.3 %collective-permute-start.5 = (bf16[256,2560]{1,0:T(8,128)(2,1)S(1)}, bf16[256,2560]{1,0:T(8,128)(2,1)S(1)}, u32[]{:S(2)}, u32[]{:S(2)}) collective-permute-start(bf16[256,2560]{1,0:T(8,128)(2,1)S(1)} %pad_maximum_fusion.8), channel_id=1, source_target_pairs={{0,2},{1,5},{2,0},{3,7},{4,6},{5,1},{6,4},{7,3},{8,10},{9,13},{10,... | collective-permute-start | bytes 3932168 | tf_op jit(solution)/shard_map/ppermute | solution.py:30
  87.0 49.6 %collective-permute-start.8 = (bf16[256,2560]{1,0:T(8,128)(2,1)S(1)}, bf16[256,2560]{1,0:T(8,128)(2,1)S(1)}, u32[]{:S(2)}, u32[]{:S(2)}) collective-permute-start(bf16[256,2560]{1,0:T(8,128)(2,1)S(1)} %pad_maximum_fusion.9), channel_id=1, source_target_pairs={{0,2},{1,5},{2,0},{3,7},{4,6},{5,1},{6,4},{7,3},{8,10},{9,13},{10,... | collective-permute-start | bytes 3932168 | tf_op jit(solution)/shard_map/ppermute | solution.py:30
  89.8 60.8 %collective-permute-start.11 = (bf16[256,2560]{1,0:T(8,128)(2,1)S(1)}, bf16[256,2560]{1,0:T(8,128)(2,1)S(1)}, u32[]{:S(2)}, u32[]{:S(2)}) collective-permute-start(bf16[256,2560]{1,0:T(8,128)(2,1)S(1)} %pad_maximum_fusion.10), channel_id=1, source_target_pairs={{0,2},{1,5},{2,0},{3,7},{4,6},{5,1},{6,4},{7,3},{8,10},{9,13},{10,... | collective-permute-start | bytes 3932168 | tf_op jit(solution)/shard_map/ppermute | solution.py:30
  94.9 60.2 %collective-permute-start.12 = (bf16[512,2560]{1,0:T(8,128)(2,1)S(1)}, bf16[512,2560]{1,0:T(8,128)(2,1)S(1)}, u32[]{:S(2)}, u32[]{:S(2)}) collective-permute-start(bf16[512,2560]{1,0:T(8,128)(2,1)S(1)} %pad_maximum_fusion.2), channel_id=1, source_target_pairs={{0,1},{1,0},{2,3},{3,2},{4,5},{5,4},{6,7},{7,6},{8,9},{9,8},{10,11... | collective-permute-start | bytes 7864328 | tf_op jit(solution)/shard_map/ppermute | solution.py:34
  119.7 37.1 %collective-permute-start.13 = (bf16[512,2560]{1,0:T(8,128)(2,1)S(1)}, bf16[512,2560]{1,0:T(8,128)(2,1)S(1)}, u32[]{:S(2)}, u32[]{:S(2)}) collective-permute-start(bf16[512,2560]{1,0:T(8,128)(2,1)S(1)} %constant_dynamic-update-slice_fusion.8), channel_id=1, source_target_pairs={{0,1},{1,0},{2,3},{3,2},{4,5},{5,4},{6,7},{7,6},{8,9},{9,8},{10,11... | collective-permute-start | bytes 7864328 | tf_op jit(solution)/shard_map/ppermute | solution.py:34
  161.8 84.0 %all-to-all-start.1 = ((bf16[16,160,768]{2,1,0:T(8,128)(2,1)}), bf16[16,160,768]{2,1,0:T(8,128)(2,1)}, u32[]{:S(2)}, u32[]{:S(2)}) async-start(bf16[16,160,768]{2,1,0:T(8,128)(2,1)} %shard_map.282), calls=%async_computation.1 | async-start | bytes 7864320 | tf_op jit(solution)/shard_map/all_to_all | solution.py:84
  174.3 33.0 %collective-permute-start.18 = (bf16[2560,384]{1,0:T(8,128)(2,1)S(1)}, bf16[2560,384]{1,0:T(8,128)(2,1)}, u32[]{:S(2)}, u32[]{:S(2)}) collective-permute-start(bf16[2560,384]{1,0:T(8,128)(2,1)S(1)} %bitcast.103), channel_id=1, source_target_pairs={{0,1},{1,0},{2,3},{3,2},{4,5},{5,4},{6,7},{7,6},{8,9},{9,8},{10,11... | collective-permute-start | bytes 5898248 | tf_op jit(solution)/shard_map/ppermute | solution.py:34
  260.8 27.0 %collective-permute-start.21 = (bf16[128,2560]{1,0:T(8,128)(2,1)S(1)}, bf16[128,2560]{1,0:T(8,128)(2,1)S(1)}, u32[]{:S(2)}, u32[]{:S(2)}) collective-permute-start(bf16[128,2560]{1,0:T(8,128)(2,1)S(1)} %slice.578), channel_id=1, source_target_pairs={{0,2},{1,5},{2,0},{3,7},{4,6},{5,1},{6,4},{7,3},{8,10},{9,13},{10,... | collective-permute-start | bytes 1966088 | tf_op jit(solution)/shard_map/ppermute | solution.py:30
  261.5 36.9 %collective-permute-start.19 = (bf16[128,2560]{1,0:T(8,128)(2,1)S(1)}, bf16[128,2560]{1,0:T(8,128)(2,1)S(1)}, u32[]{:S(2)}, u32[]{:S(2)}) collective-permute-start(bf16[128,2560]{1,0:T(8,128)(2,1)S(1)} %slice.574), channel_id=1, source_target_pairs={{0,2},{1,5},{2,0},{3,7},{4,6},{5,1},{6,4},{7,3},{8,10},{9,13},{10,... | collective-permute-start | bytes 1966088 | tf_op jit(solution)/shard_map/ppermute | solution.py:30
  268.0 32.7 %collective-permute-start.28 = (bf16[64,2560]{1,0:T(8,128)(2,1)S(1)}, bf16[64,2560]{1,0:T(8,128)(2,1)S(1)}, u32[]{:S(2)}, u32[]{:S(2)}) collective-permute-start(bf16[64,2560]{1,0:T(8,128)(2,1)S(1)} %slice.835), channel_id=1, source_target_pairs={{0,4},{1,3},{2,6},{3,1},{4,0},{5,7},{6,2},{7,5},{8,12},{9,11},{10,... | collective-permute-start | bytes 983048 | tf_op jit(solution)/shard_map/ppermute | solution.py:30
  277.5 33.5 %collective-permute-start.25 = (bf16[64,2560]{1,0:T(8,128)(2,1)S(1)}, bf16[64,2560]{1,0:T(8,128)(2,1)S(1)}, u32[]{:S(2)}, u32[]{:S(2)}) collective-permute-start(bf16[64,2560]{1,0:T(8,128)(2,1)S(1)} %slice.836), channel_id=1, source_target_pairs={{0,4},{1,3},{2,6},{3,1},{4,0},{5,7},{6,2},{7,5},{8,12},{9,11},{10,... | collective-permute-start | bytes 983048 | tf_op jit(solution)/shard_map/ppermute | solution.py:30
  311.0 29.2 %collective-permute-start.26 = (bf16[64,2560]{1,0:T(8,128)(2,1)S(1)}, bf16[64,2560]{1,0:T(8,128)(2,1)S(1)}, u32[]{:S(2)}, u32[]{:S(2)}) collective-permute-start(bf16[64,2560]{1,0:T(8,128)(2,1)S(1)} %fusion.31), channel_id=1, source_target_pairs={{0,16},{1,17},{2,18},{3,19},{4,20},{5,21},{6,22},{7,23},{8,24},{9,... | collective-permute-start | bytes 983048 | tf_op jit(solution)/shard_map/ppermute | solution.py:30
  312.3 27.9 %collective-permute-start.23 = (bf16[64,2560]{1,0:T(8,128)(2,1)S(1)}, bf16[64,2560]{1,0:T(8,128)(2,1)S(1)}, u32[]{:S(2)}, u32[]{:S(2)}) collective-permute-start(bf16[64,2560]{1,0:T(8,128)(2,1)S(1)} %fusion.32), channel_id=1, source_target_pairs={{0,8},{1,9},{2,10},{3,11},{4,12},{5,13},{6,14},{7,15},{8,0},{9,1},... | collective-permute-start | bytes 983048 | tf_op jit(solution)/shard_map/ppermute | solution.py:30
  343.5 83.5 %collective-permute-start.46 = (bf16[2560,512]{1,0:T(8,128)(2,1)S(1)}, bf16[2560,512]{1,0:T(8,128)(2,1)S(1)}, u32[]{:S(2)}, u32[]{:S(2)}) collective-permute-start(bf16[2560,512]{1,0:T(8,128)(2,1)S(1)} %slice.589), channel_id=1, source_target_pairs={{0,1},{1,0},{2,3},{3,2},{4,5},{5,4},{6,7},{7,6},{8,9},{9,8},{10,11... | collective-permute-start | bytes 7864328 | tf_op jit(solution)/shard_map/ppermute | solution.py:34
  347.4 33.8 %collective-permute-start.31 = (bf16[128,2560]{1,0:T(8,128)(2,1)S(1)}, bf16[128,2560]{1,0:T(8,128)(2,1)S(1)}, u32[]{:S(2)}, u32[]{:S(2)}) collective-permute-start(bf16[128,2560]{1,0:T(8,128)(2,1)S(1)} %pad_maximum_fusion.21), channel_id=1, source_target_pairs={{0,2},{1,5},{2,0},{3,7},{4,6},{5,1},{6,4},{7,3},{8,10},{9,13},{10,... | collective-permute-start | bytes 1966088 | tf_op jit(solution)/shard_map/ppermute | solution.py:30
  434.2 24.6 %collective-permute-start.49 = (bf16[128,2560]{1,0:T(8,128)(2,1)S(1)}, bf16[128,2560]{1,0:T(8,128)(2,1)S(1)}, u32[]{:S(2)}, u32[]{:S(2)}) collective-permute-start(bf16[128,2560]{1,0:T(8,128)(2,1)S(1)} %slice.595), channel_id=1, source_target_pairs={{0,2},{1,5},{2,0},{3,7},{4,6},{5,1},{6,4},{7,3},{8,10},{9,13},{10,... | collective-permute-start | bytes 1966088 | tf_op jit(solution)/shard_map/ppermute | solution.py:30
  437.5 31.8 %collective-permute-start.47 = (bf16[128,2560]{1,0:T(8,128)(2,1)S(1)}, bf16[128,2560]{1,0:T(8,128)(2,1)S(1)}, u32[]{:S(2)}, u32[]{:S(2)}) collective-permute-start(bf16[128,2560]{1,0:T(8,128)(2,1)S(1)} %slice.591), channel_id=1, source_target_pairs={{0,2},{1,5},{2,0},{3,7},{4,6},{5,1},{6,4},{7,3},{8,10},{9,13},{10,... | collective-permute-start | bytes 1966088 | tf_op jit(solution)/shard_map/ppermute | solution.py:30
  438.9 32.1 %collective-permute-start.56 = (bf16[64,2560]{1,0:T(8,128)(2,1)S(1)}, bf16[64,2560]{1,0:T(8,128)(2,1)S(1)}, u32[]{:S(2)}, u32[]{:S(2)}) collective-permute-start(bf16[64,2560]{1,0:T(8,128)(2,1)S(1)} %slice.831), channel_id=1, source_target_pairs={{0,4},{1,3},{2,6},{3,1},{4,0},{5,7},{6,2},{7,5},{8,12},{9,11},{10,... | collective-permute-start | bytes 983048 | tf_op jit(solution)/shard_map/ppermute | solution.py:30
  472.6 31.1 %collective-permute-start.54 = (bf16[64,2560]{1,0:T(8,128)(2,1)S(1)}, bf16[64,2560]{1,0:T(8,128)(2,1)S(1)}, u32[]{:S(2)}, u32[]{:S(2)}) collective-permute-start(bf16[64,2560]{1,0:T(8,128)(2,1)S(1)} %fusion.25), channel_id=1, source_target_pairs={{0,16},{1,17},{2,18},{3,19},{4,20},{5,21},{6,22},{7,23},{8,24},{9,... | collective-permute-start | bytes 983048 | tf_op jit(solution)/shard_map/ppermute | solution.py:30
  475.8 27.9 %collective-permute-start.51 = (bf16[64,2560]{1,0:T(8,128)(2,1)S(1)}, bf16[64,2560]{1,0:T(8,128)(2,1)S(1)}, u32[]{:S(2)}, u32[]{:S(2)}) collective-permute-start(bf16[64,2560]{1,0:T(8,128)(2,1)S(1)} %fusion.26), channel_id=1, source_target_pairs={{0,8},{1,9},{2,10},{3,11},{4,12},{5,13},{6,14},{7,15},{8,0},{9,1},... | collective-permute-start | bytes 983048 | tf_op jit(solution)/shard_map/ppermute | solution.py:30
  476.0 30.8 %collective-permute-start.88 = (bf16[256,256]{1,0:T(8,128)(2,1)S(1)}, bf16[256,256]{1,0:T(8,128)(2,1)S(1)}, u32[]{:S(2)}, u32[]{:S(2)}) collective-permute-start(bf16[256,256]{1,0:T(8,128)(2,1)S(1)} %bitcast.157), channel_id=1, source_target_pairs={{0,1},{1,0},{2,3},{3,2},{4,5},{5,4},{6,7},{7,6},{8,9},{9,8},{10,11... | collective-permute-start | bytes 393224 | tf_op jit(solution)/shard_map/ppermute | solution.py:34
  480.6 26.9 %collective-permute-start.59 = (bf16[2560,256]{1,0:T(8,128)(2,1)S(1)}, bf16[2560,256]{1,0:T(8,128)(2,1)S(1)}, u32[]{:S(2)}, u32[]{:S(2)}) collective-permute-start(bf16[2560,256]{1,0:T(8,128)(2,1)S(1)} %slice.570), channel_id=1, source_target_pairs={{0,1},{1,0},{2,3},{3,2},{4,5},{5,4},{6,7},{7,6},{8,9},{9,8},{10,11... | collective-permute-start | bytes 3932168 | tf_op jit(solution)/shard_map/ppermute | solution.py:34
  513.0 25.0 %collective-permute-start.62 = (bf16[128,2560]{1,0:T(8,128)(2,1)S(1)}, bf16[128,2560]{1,0:T(8,128)(2,1)S(1)}, u32[]{:S(2)}, u32[]{:S(2)}) collective-permute-start(bf16[128,2560]{1,0:T(8,128)(2,1)S(1)} %slice.611), channel_id=1, source_target_pairs={{0,2},{1,5},{2,0},{3,7},{4,6},{5,1},{6,4},{7,3},{8,10},{9,13},{10,... | collective-permute-start | bytes 1966088 | tf_op jit(solution)/shard_map/ppermute | solution.py:30
  514.3 34.3 %collective-permute-start.60 = (bf16[128,2560]{1,0:T(8,128)(2,1)S(1)}, bf16[128,2560]{1,0:T(8,128)(2,1)S(1)}, u32[]{:S(2)}, u32[]{:S(2)}) collective-permute-start(bf16[128,2560]{1,0:T(8,128)(2,1)S(1)} %slice.607), channel_id=1, source_target_pairs={{0,2},{1,5},{2,0},{3,7},{4,6},{5,1},{6,4},{7,3},{8,10},{9,13},{10,... | collective-permute-start | bytes 1966088 | tf_op jit(solution)/shard_map/ppermute | solution.py:30
  518.5 30.4 %collective-permute-start.69 = (bf16[64,2560]{1,0:T(8,128)(2,1)S(1)}, bf16[64,2560]{1,0:T(8,128)(2,1)S(1)}, u32[]{:S(2)}, u32[]{:S(2)}) collective-permute-start(bf16[64,2560]{1,0:T(8,128)(2,1)S(1)} %slice.827), channel_id=1, source_target_pairs={{0,4},{1,3},{2,6},{3,1},{4,0},{5,7},{6,2},{7,5},{8,12},{9,11},{10,... | collective-permute-start | bytes 983048 | tf_op jit(solution)/shard_map/ppermute | solution.py:30
  551.8 25.3 %collective-permute-start.67 = (bf16[64,2560]{1,0:T(8,128)(2,1)S(1)}, bf16[64,2560]{1,0:T(8,128)(2,1)S(1)}, u32[]{:S(2)}, u32[]{:S(2)}) collective-permute-start(bf16[64,2560]{1,0:T(8,128)(2,1)S(1)} %fusion.17), channel_id=1, source_target_pairs={{0,16},{1,17},{2,18},{3,19},{4,20},{5,21},{6,22},{7,23},{8,24},{9,... | collective-permute-start | bytes 983048 | tf_op jit(solution)/shard_map/ppermute | solution.py:30
  552.0 25.1 %collective-permute-start.64 = (bf16[64,2560]{1,0:T(8,128)(2,1)S(1)}, bf16[64,2560]{1,0:T(8,128)(2,1)S(1)}, u32[]{:S(2)}, u32[]{:S(2)}) collective-permute-start(bf16[64,2560]{1,0:T(8,128)(2,1)S(1)} %fusion.18), channel_id=1, source_target_pairs={{0,8},{1,9},{2,10},{3,11},{4,12},{5,13},{6,14},{7,15},{8,0},{9,1},... | collective-permute-start | bytes 983048 | tf_op jit(solution)/shard_map/ppermute | solution.py:30
  591.4 28.7 %collective-permute-start.73 = (bf16[128,2560]{1,0:T(8,128)(2,1)S(1)}, bf16[128,2560]{1,0:T(8,128)(2,1)S(1)}, u32[]{:S(2)}, u32[]{:S(2)}) collective-permute-start(bf16[128,2560]{1,0:T(8,128)(2,1)S(1)} %pad_maximum_fusion.26), channel_id=1, source_target_pairs={{0,2},{1,5},{2,0},{3,7},{4,6},{5,1},{6,4},{7,3},{8,10},{9,13},{10,... | collective-permute-start | bytes 1966088 | tf_op jit(solution)/shard_map/ppermute | solution.py:30
  620.2 33.3 %collective-permute-start.83 = (bf16[256,2560]{1,0:T(8,128)(2,1)S(1)}, bf16[256,2560]{1,0:T(8,128)(2,1)S(1)}, u32[]{:S(2)}, u32[]{:S(2)}) collective-permute-start(bf16[256,2560]{1,0:T(8,128)(2,1)S(1)} %pad_maximum_fusion.16), channel_id=1, source_target_pairs={{0,1},{1,0},{2,3},{3,2},{4,5},{5,4},{6,7},{7,6},{8,9},{9,8},{10,11... | collective-permute-start | bytes 3932168 | tf_op jit(solution)/shard_map/ppermute | solution.py:34
  653.1 105.6 %collective-permute-start.71 = (bf16[64,2560]{1,0:T(8,128)(2,1)}, bf16[64,2560]{1,0:T(8,128)(2,1)}, u32[]{:S(2)}, u32[]{:S(2)}) collective-permute-start(bf16[64,2560]{1,0:T(8,128)(2,1)} %get-tuple-element.150), channel_id=1, source_target_pairs={{0,1},{1,0},{2,3},{3,2},{4,5},{5,4},{6,7},{7,6},{8,9},{9,8},{10,11... | collective-permute-start | bytes 983048 | tf_op jit(solution)/shard_map/ppermute | solution.py:34
  655.9 85.8 %all-to-all-start.2 = ((bf16[16,160,768]{2,1,0:T(8,128)(2,1)}), bf16[16,160,768]{2,1,0:T(8,128)(2,1)}, u32[]{:S(2)}, u32[]{:S(2)}) async-start(bf16[16,160,768]{2,1,0:T(8,128)(2,1)} %bitcast.101), calls=%async_computation.2 | async-start | bytes 7864320 | tf_op jit(solution)/shard_map/all_to_all | solution.py:84
  744.2 69.9 %all-to-all-start.3 = ((bf16[16,176,384]{2,1,0:T(8,128)(2,1)}), bf16[16,176,384]{2,1,0:T(8,128)(2,1)S(1)}, u32[]{:S(2)}, u32[]{:S(2)}) async-start(bf16[16,176,384]{2,1,0:T(8,128)(2,1)} %fusion.4), calls=%async_computation.3 | async-start | bytes 4325376 | tf_op jit(solution)/shard_map/all_to_all | solution.py:84
  783.7 26.4 %collective-permute-start.93 = (bf16[128,2560]{1,0:T(8,128)(2,1)S(1)}, bf16[128,2560]{1,0:T(8,128)(2,1)S(1)}, u32[]{:S(2)}, u32[]{:S(2)}) collective-permute-start(bf16[128,2560]{1,0:T(8,128)(2,1)S(1)} %slice.634), channel_id=1, source_target_pairs={{0,2},{1,5},{2,0},{3,7},{4,6},{5,1},{6,4},{7,3},{8,10},{9,13},{10,... | collective-permute-start | bytes 1966088 | tf_op jit(solution)/shard_map/ppermute | solution.py:30
  785.3 26.6 %collective-permute-start.100 = (bf16[64,2560]{1,0:T(8,128)(2,1)S(1)}, bf16[64,2560]{1,0:T(8,128)(2,1)S(1)}, u32[]{:S(2)}, u32[]{:S(2)}) collective-permute-start(bf16[64,2560]{1,0:T(8,128)(2,1)S(1)} %slice.823), channel_id=1, source_target_pairs={{0,4},{1,3},{2,6},{3,1},{4,0},{5,7},{6,2},{7,5},{8,12},{9,11},{10,... | collective-permute-start | bytes 983048 | tf_op jit(solution)/shard_map/ppermute | solution.py:30
  801.3 27.8 %collective-permute-start.97 = (bf16[64,2560]{1,0:T(8,128)(2,1)}, bf16[64,2560]{1,0:T(8,128)(2,1)}, u32[]{:S(2)}, u32[]{:S(2)}) collective-permute-start(bf16[64,2560]{1,0:T(8,128)(2,1)} %slice.824), channel_id=1, source_target_pairs={{0,4},{1,3},{2,6},{3,1},{4,0},{5,7},{6,2},{7,5},{8,12},{9,11},{10,... | collective-permute-start | bytes 983048 | tf_op jit(solution)/shard_map/ppermute | solution.py:30
  811.1 33.3 %collective-permute-start.94 = (bf16[64,2560]{1,0:T(8,128)(2,1)}, bf16[64,2560]{1,0:T(8,128)(2,1)}, u32[]{:S(2)}, u32[]{:S(2)}) collective-permute-start(bf16[64,2560]{1,0:T(8,128)(2,1)} %slice.825), channel_id=1, source_target_pairs={{0,4},{1,3},{2,6},{3,1},{4,0},{5,7},{6,2},{7,5},{8,12},{9,11},{10,... | collective-permute-start | bytes 983048 | tf_op jit(solution)/shard_map/ppermute | solution.py:30
  812.8 43.9 %collective-permute-start.101 = (bf16[64,2560]{1,0:T(8,128)(2,1)}, bf16[64,2560]{1,0:T(8,128)(2,1)}, u32[]{:S(2)}, u32[]{:S(2)}) collective-permute-start(bf16[64,2560]{1,0:T(8,128)(2,1)} %fusion.10), channel_id=1, source_target_pairs={{0,24},{1,25},{2,26},{3,27},{4,28},{5,29},{6,30},{7,31},{8,16},{9,... | collective-permute-start | bytes 983048 | tf_op jit(solution)/shard_map/ppermute | solution.py:30
  830.8 25.8 %collective-permute-start.98 = (bf16[64,2560]{1,0:T(8,128)(2,1)}, bf16[64,2560]{1,0:T(8,128)(2,1)S(1)}, u32[]{:S(2)}, u32[]{:S(2)}) collective-permute-start(bf16[64,2560]{1,0:T(8,128)(2,1)} %fusion.11), channel_id=1, source_target_pairs={{0,16},{1,17},{2,18},{3,19},{4,20},{5,21},{6,22},{7,23},{8,24},{9,... | collective-permute-start | bytes 983048 | tf_op jit(solution)/shard_map/ppermute | solution.py:30
  (145 other events, 1399.3 us)

commit v3 on v2

v3 whole, which is shorter than its diff:
```python
import functools

import jax
import jax.numpy as jnp
from jax import lax
from jax.experimental import pallas as pl
from jax.experimental.pallas import tpu as pltpu
from jax.sharding import PartitionSpec as P

BF16 = jnp.bfloat16
F32 = jnp.float32
EPSILON = 1e-06
BOTH = ("seq", "head")
LANES = 128
CHUNK = 128
GELU_A = 0.7978845608028654
GELU_B = 0.044715
VMEM_BYTES = 56 * 1024 * 1024


def xor_send(value, mask_first, mask_second=None, allowed=None):
    count = lax.axis_size("seq")
    masks = (mask_first, mask_first if mask_second is None else mask_second)
    pairs = [
        (chip * 2 + core, (chip ^ masks[core]) * 2 + core)
        for chip in range(count)
        for core in range(2)
        if allowed is None or allowed(chip, chip ^ masks[core])
    ]
    return lax.ppermute(value, BOTH, pairs)


def core_swap(value):
    return lax.ppermute(value, "head", [(0, 1), (1, 0)])


def row_send(value, to):
    pairs = [
        (row * 8 + device, to[row] * 8 + device) for row in sorted(to) for device in range(8)
    ]
    return lax.ppermute(value, BOTH, pairs)


PAIRED = {0: 1, 1: 0, 2: 3, 3: 2}
CROSSED = {1: 2, 2: 1}
OUTWARD = {1: 0, 2: 3}


def row_gathered(rows):
    count = lax.axis_size("seq")
    if count != 16:
        return [rows] + [xor_send(rows, 4 * g) for g in range(1, count // 4)]
    one = row_send(rows, PAIRED)
    cross = row_send(rows, CROSSED)
    far = row_send(one, CROSSED)
    return [rows, one, far + row_send(cross, OUTWARD), cross + row_send(far, OUTWARD)]


def gathered(rows, early=()):
    own = []
    columns = row_gathered(rows)
    for g, block in enumerate(columns):
        pair = jnp.concatenate([block, xor_send(block, 2, 1)], axis=0)
        if g == len(columns) - 1 and early:
            pair = after(pair, *early)
        own.append(jnp.concatenate([pair, xor_send(pair, 1, 2)], axis=0))
    return own + [core_swap(group) for group in own]


def scattered(*products):
    count = lax.axis_size("seq") // 4
    rows = products[0][0][0].shape[0] // 4
    parts = len(products)

    def sent(arrays, *masks):
        moved = xor_send(jnp.concatenate([a.astype(BF16) for a in arrays]), *masks)
        return [a.astype(F32) for a in jnp.split(moved, parts)]

    own = None
    arriving = []
    for g in list(range(1, count)) + [0]:
        sums = [dot(groups[g], right, ((1,), (1,))).astype(BF16) for groups, right in products]
        more = sent([a[2 * rows :] for a in sums], 1, 2)
        sums = [a[: 2 * rows].astype(F32) + b for a, b in zip(sums, more)]
        more = sent([a[rows:] for a in sums], 2, 1)
        sums = [a[:rows] + b for a, b in zip(sums, more)]
        if g:
            arriving.append(sent(sums, 4 * g))
        else:
            own = sums
    for more in arriving:
        own = [a + b for a, b in zip(own, more)]
    return own


INWARD = {0: 1, 3: 2}


def row_scattered(parts):
    own = parts[0].astype(F32)
    if len(parts) != 4:
        moved = [xor_send(part, 4 * g).astype(F32) for g, part in enumerate(parts) if g]
        return functools.reduce(jnp.add, moved, own)
    _, one, two, three = parts
    two, three = (
        two.astype(F32) + row_send(three, INWARD).astype(F32),
        three.astype(F32) + row_send(two, INWARD).astype(F32),
    )
    own = own + row_send(three.astype(BF16), CROSSED).astype(F32)
    one = one.astype(F32) + row_send(two.astype(BF16), CROSSED).astype(F32)
    return own + row_send(one.astype(BF16), PAIRED).astype(F32)


def near_gathered(rows):
    pair = jnp.concatenate([rows, xor_send(rows, 2, 1)], axis=0)
    own = jnp.concatenate([pair, xor_send(pair, 1, 2)], axis=0)
    return jnp.concatenate([own, core_swap(own)], axis=0)


def near_scattered(rows, *right):
    half = rows.shape[0] // 2
    th = half // 4
    both = (rows[:half], core_swap(rows[half:]))
    if len(right) == 1:
        both = (jnp.concatenate(both, axis=1),)
    partial = sum(dot(a, b, ((1,), (1,))) for a, b in zip(both, right)).astype(BF16)
    pair = partial[: 2 * th].astype(F32) + xor_send(partial[2 * th :], 1, 2).astype(F32)
    return pair[:th] + xor_send(pair[th:].astype(BF16), 2, 1).astype(F32)


def near_exchanged(pieces):
    count = lax.axis_size("seq")
    fours = [list(range(first, first + 4)) for first in range(0, count, 4)]
    return lax.all_to_all(pieces, "seq", 0, 0, tiled=True, axis_index_groups=fours)


def next_four(value, step):
    count = lax.axis_size("seq")
    pairs = [
        (chip * 2 + core, (chip + 4 * step) * 2 + core)
        for chip in range(count)
        for core in range(2)
        if 0 <= chip + 4 * step < count
    ]
    return lax.ppermute(value, BOTH, pairs)


def carried(pair, place, reverse):
    count = lax.axis_size("seq") // 4
    pairs = jnp.stack([pair] + [xor_send(pair, 4 * g) for g in range(1, count)])
    state = jnp.zeros_like(pair[:1])
    for lap in range(count - 1):
        source = count - 1 - lap if reverse else lap
        one = lax.dynamic_index_in_dim(pairs, place ^ source, 0, False)
        ahead = source > place if reverse else source < place
        state = jnp.where(ahead, one[0:1] * state + one[1:2], state)
    return state


def grouped(rows):
    half = rows.shape[0] // 2
    both = jnp.concatenate([rows[:half], core_swap(rows[half:])], axis=1)
    return list(both.reshape(lax.axis_size("seq") // 4, -1, both.shape[1]))


def after(value, *others):
    return lax.optimization_barrier((value,) + others)[0]


def all_to_all(pieces):
    return lax.all_to_all(pieces, "seq", 0, 0, tiled=True)


def params(**more):
    return pltpu.CompilerParams(vmem_limit_bytes=VMEM_BYTES, **more)


def pack_wide(gain, gate, value, contract, out, *, chips):
    lanes = gate.shape[1]
    live = pl.program_id(0) < chips
    scale = jnp.where(live, gain[...], 0.0)
    out[0, :, :lanes] = (gate[...].astype(F32) * scale).astype(BF16)
    out[0, :, lanes : 2 * lanes] = (value[...].astype(F32) * scale).astype(BF16)
    out[0, :, 2 * lanes :] = jnp.where(live, contract[...].astype(F32), 0.0).astype(BF16)


def packed_wide(gain, gate, value, contract, count, lanes):
    part, hidden = gate.shape
    chips = hidden // lanes
    column = pl.BlockSpec((part, lanes), lambda j: (0, jnp.minimum(j, chips - 1)))
    return pl.pallas_call(
        functools.partial(pack_wide, chips=chips),
        out_shape=jax.ShapeDtypeStruct((count, part, 3 * lanes), BF16),
        grid=(count,),
        in_specs=[
            pl.BlockSpec((part, 1), lambda j: (0, 0)),
            column,
            column,
            column,
        ],
        out_specs=pl.BlockSpec((1, part, 3 * lanes), lambda j: (j, 0, 0)),
        compiler_params=params(),
    )(gain, gate, value, contract)


def unpack_wide(grads, gain, gate, value, gate_out, value_out, contract_out, sums):
    lanes = gate.shape[1] // grads.shape[0]

    @pl.when(pl.program_id(0) == 0)
    def _():
        sums[...] = jnp.zeros_like(sums)

    total = sums[...]
    for i in range(grads.shape[0]):
        at = slice(i * lanes, (i + 1) * lanes)
        gate_hat = grads[i, :, :lanes].astype(F32)
        value_hat = grads[i, :, lanes : 2 * lanes].astype(F32)
        gate_out[:, at] = gate_hat * gain[...]
        value_out[:, at] = value_hat * gain[...]
        contract_out[:, at] = grads[i, :, 2 * lanes :].astype(F32)
        both = gate_hat * gate[:, at].astype(F32) + value_hat * value[:, at].astype(F32)
        for start in range(0, lanes, LANES):
            total = total + both[:, start : start + LANES]
    sums[...] = total


def unpacked_wide(grads, gain, gate, value, lanes):
    part, hidden = gate.shape
    chips = hidden // lanes
    at_once = 3 if chips % 3 == 0 else 1
    column = pl.BlockSpec((part, at_once * lanes), lambda j: (0, j))
    return pl.pallas_call(
        unpack_wide,
        out_shape=[
            jax.ShapeDtypeStruct((part, hidden), F32),
            jax.ShapeDtypeStruct((part, hidden), F32),
            jax.ShapeDtypeStruct((part, hidden), F32),
            jax.ShapeDtypeStruct((part, LANES), F32),
        ],
        grid=(chips // at_once,),
        in_specs=[
            pl.BlockSpec((at_once, part, 3 * lanes), lambda j: (j, 0, 0)),
            pl.BlockSpec((part, 1), lambda j: (0, 0)),
            column,
            column,
        ],
        out_specs=[
            column,
            column,
            column,
            pl.BlockSpec((part, LANES), lambda j: (0, 0)),
        ],
        compiler_params=params(),
    )(grads, gain, gate, value)


HALVES = (((0, 1, 2), (4, 5, 3)), ((6, 7, None), (8, 9, None)))


def pack_narrow(gain, gelu, scan, output, in_gate, de_gate, small, yv_out, wo_out, *, extra):
    for core in range(2):
        for side in range(2):
            halves = HALVES[side][core]
            few = yv_out.at[core, side, extra : 2 * extra, :]
            few[...] = jnp.zeros_like(few)
            for place, half in enumerate(halves):
                at = slice(place * LANES, (place + 1) * LANES)
                more = slice((3 + place) * LANES, (4 + place) * LANES)
                if half is None:
                    yv_out[core, side, :, at] = jnp.zeros_like(yv_out[core, side, :, at])
                    yv_out[core, side, :, more] = jnp.zeros_like(yv_out[core, side, :, more])
                    wo_out[core, side, :, at] = jnp.zeros_like(wo_out[core, side, :, at])
                    continue
                block, odd = half // 2, half % 2
                column = slice(half * LANES, (half + 1) * LANES)
                lanes = slice(odd * LANES, (odd + 1) * LANES)
                yv_out[core, side, :extra, at] = in_gate[block, :, lanes]
                yv_out[core, side, :extra, more] = de_gate[block, :, lanes]
                if place != 1:
                    spot = slice((place // 2) * LANES, (place // 2 + 1) * LANES)
                    yv_out[core, side, extra : 2 * extra, spot] = small[block]
                yv_out[core, side, 2 * extra :, at] = (
                    gelu[:, column].astype(F32) * gain[...]
                ).astype(BF16)
                yv_out[core, side, 2 * extra :, more] = (
                    scan[:, column].astype(F32) * gain[...]
                ).astype(BF16)
                wo_out[core, side, :, at] = output[:, column]


def packed_narrow(gain, gelu, scan, output, in_gate, de_gate, small):
    part = gelu.shape[0]
    extra = small.shape[1]
    return in_vmem(
        functools.partial(pack_narrow, extra=extra),
        [gain, gelu, scan, output, in_gate, de_gate, small],
        [((2, 2, 2 * extra + part, 6 * LANES), BF16), ((2, 2, part, 3 * LANES), BF16)],
    )


def unpack_narrow(
    yv, wo, gain, gelu, scan, gelu_out, scan_out, output_out, in_out, de_out, sums, *, extra
):
    rows = in_out.shape[1]
    sums[...] = jnp.zeros_like(sums)
    for core in range(2):
        for side in range(2):
            for place, half in enumerate(HALVES[side][core]):
                if half is None:
                    continue
                block, odd = half // 2, half % 2
                at = slice(place * LANES, (place + 1) * LANES)
                more = slice((3 + place) * LANES, (4 + place) * LANES)
                column = slice(half * LANES, (half + 1) * LANES)
                lanes = slice(odd * LANES, (odd + 1) * LANES)
                gelu_hat = yv[core, side, 2 * extra :, at].astype(F32)
                scan_hat = yv[core, side, 2 * extra :, more].astype(F32)
                gelu_out[:, column] = gelu_hat * gain[...]
                scan_out[:, column] = scan_hat * gain[...]
                output_out[:, column] = wo[core, side, :, at].astype(F32)
                in_out[block, :, lanes] = yv[core, side, :extra, at].astype(F32)[:rows]
                de_out[block, :, lanes] = yv[core, side, :extra, more].astype(F32)[:rows]
                sums[...] += gelu_hat * gelu[:, column].astype(F32) + scan_hat * scan[
                    :, column
                ].astype(F32)


def unpacked_narrow(yv, wo, gain, gelu, scan, local_blocks, gate_rows, extra):
    part, width = gelu.shape
    gate = ((local_blocks, gate_rows, 2 * LANES), F32)
    return in_vmem(
        functools.partial(unpack_narrow, extra=extra),
        [yv, wo, gain, gelu, scan],
        [((part, width), F32)] * 3 + [gate, gate, ((part, LANES), F32)],
    )


def gelu_parts(w):
    inner = jnp.tanh(GELU_A * (w + GELU_B * w * w * w))
    return 0.5 * w * (1.0 + inner), inner


def gelu_slope(w, inner):
    return 0.5 * (1.0 + inner) + 0.5 * w * (1.0 - inner * inner) * GELU_A * (
        1.0 + 3.0 * GELU_B * w * w
    )


def rate_parts(ga, soft_row):
    log_rate = -8.0 * ga * soft_row
    twice = 2.0 * log_rate
    near = -twice * (
        1.0 + twice * (0.5 + twice * (1.0 / 6 + twice * (1.0 / 24 + twice * (1.0 / 120))))
    )
    rate = jnp.exp(log_rate)
    far = 1.0 - jnp.exp(twice)
    return rate, jnp.sqrt(jnp.where(twice > -0.1, near, far))


def filter_kernel(slot, yv, before, rows, y, vp, c, cb, *, th, taps):
    total, wide = y.shape
    vp[0:8, :] = before[...]

    def order(b, carry):
        block = yv[pl.ds(pl.multiple_of(slot[b] * th, th), th), :]
        y[pl.ds(pl.multiple_of(b * th, th), th), :] = block[:, :wide]
        vp[pl.ds(pl.multiple_of(b * th + 8, 8), th), :] = block[:, wide:]
        return carry

    lax.fori_loop(0, total // th, order, 0)

    def chunk(i, carry):
        start = pl.multiple_of(i * CHUNK, CHUNK)
        window = vp[pl.ds(start, CHUNK + 8), :]
        out = rows[0:1, :] * window[8 : 8 + CHUNK]
        for k in range(1, taps):
            out = out + rows[k : k + 1, :] * window[8 - k : 8 - k + CHUNK]
        c[pl.ds(start, CHUNK), :] = out
        cb[pl.ds(start, CHUNK), :] = out.astype(BF16)
        return carry

    lax.fori_loop(0, total // CHUNK, chunk, 0)


def put(ref, at, value):
    for i in range(ref.shape[0]):
        ref[i, at, :] = value[:, i * LANES : (i + 1) * LANES]


def got(ref, at):
    return jnp.concatenate([ref[i, at, :] for i in range(ref.shape[0])], axis=1)


def states_kernel(cb, far, whole, near_gates, far_gates, c, rows, gi, ga, hp, p, ends, pair, a):
    total, wide = c.shape
    length = total // 8
    bias_i, bias_a, soft = rows[0:1, :], rows[1:2, :], rows[2:3, :]

    def chunk(i, carry):
        at = pl.ds(pl.multiple_of(i * CHUNK, CHUNK), CHUNK)
        full = jnp.dot(cb[at, : 2 * LANES], whole[...], preferred_element_type=F32)
        half = jnp.dot(cb[at, 2 * LANES :], near_gates[...], preferred_element_type=F32)
        half = half + jnp.dot(far[at, :], far_gates[...], preferred_element_type=F32)
        pre_i = jnp.concatenate([full[:, : 2 * LANES], half[:, :LANES]], axis=1)
        pre_a = jnp.concatenate([full[:, 2 * LANES :], half[:, LANES:]], axis=1)
        open_i = jax.nn.sigmoid(pre_i + bias_i)
        open_a = jax.nn.sigmoid(pre_a + bias_a)
        rate, scale = rate_parts(open_a, soft)
        gi[at, :] = open_i
        ga[at, :] = open_a
        put(a, at, rate)
        put(hp, at, scale * open_i * c[at, :])
        return carry

    lax.fori_loop(0, total // CHUNK, chunk, 0)

    tiles = wide // LANES

    def step(t, carry):
        at = pl.ds(t, 8, stride=length)
        out = []
        for i, (h, q) in enumerate(carry):
            rate = a[i, at, :]
            h = rate * h + hp[i, at, :]
            q = q * rate
            hp[i, at, :] = h
            p[i, at, :] = q
            out.append((h, q))
        return tuple(out)

    start = ((jnp.zeros((8, LANES), F32), jnp.ones((8, LANES), F32)),) * tiles
    last, product = (
        jnp.concatenate(parts, axis=1)
        for parts in zip(*lax.fori_loop(0, length, step, start, unroll=8))
    )
    ends[0:8, :] = product
    ends[8:16, :] = last
    rates, state = product[0:1], last[0:1]
    for j in range(1, 8):
        state = product[j : j + 1] * state + last[j : j + 1]
        rates = rates * product[j : j + 1]
    pair[...] = jnp.zeros_like(pair)
    pair[0:1, :] = rates
    pair[1:2, :] = state


def merge_kernel(slot, hp, p, ends, carry_in, y, h, ob, *, th):
    total = y.shape[0]
    per = total // 8 // th
    enter = carry_in[...]
    h[0:8, :] = jnp.broadcast_to(enter, (8, enter.shape[1]))
    for j in range(8):

        def finish(i, carry, j=j, enter=enter):
            b = j * per + i
            at = pl.ds(pl.multiple_of(b * th, th), th)
            state = got(hp, at) + got(p, at) * enter
            h[pl.ds(pl.multiple_of(b * th + 8, 8), th), :] = state
            out, _ = gelu_parts(y[at, :])
            ob[pl.ds(pl.multiple_of(slot[b] * th, th), th), :] = (state * out).astype(BF16)
            return carry

        lax.fori_loop(0, per, finish, 0)
        enter = ends[8 + j : 9 + j, :] + ends[j : j + 1, :] * enter


def adjoint_kernel(slot, dob, y, h, ga, rows, dy, lam, q, ends, pair, a, *, th):
    total, wide = y.shape
    length = total // 8
    soft = rows[2:3, :]

    def order(b, carry):
        at = pl.ds(pl.multiple_of(b * th, th), th)
        there = pl.ds(pl.multiple_of(slot[b] * th, th), th)
        block = dob[there, :]
        w = y[at, :]
        out, inner = gelu_parts(w)
        put(lam, at, block * out)
        state = h[pl.ds(pl.multiple_of(b * th + 8, 8), th), :]
        dy[there, :] = (block * state * gelu_slope(w, inner)).astype(BF16)
        put(a, at, jnp.exp(-8.0 * ga[at, :] * soft))
        return carry

    lax.fori_loop(0, total // th, order, 0)

    tiles = wide // LANES

    def step(t, carry):
        at = pl.ds(length - 1 - t, 8, stride=length)
        out = []
        for i, (later, product) in enumerate(carry):
            here = lam[i, at, :] + later
            lam[i, at, :] = here
            q[i, at, :] = product
            rate = a[i, at, :]
            out.append((rate * here, product * rate))
        return tuple(out)

    start = ((jnp.zeros((8, LANES), F32), jnp.ones((8, LANES), F32)),) * tiles
    first, product = (
        jnp.concatenate(parts, axis=1)
        for parts in zip(*lax.fori_loop(0, length, step, start, unroll=8))
    )
    ends[0:8, :] = product
    ends[8:16, :] = first
    rates, state = product[7:8], first[7:8]
    for j in range(6, -1, -1):
        state = product[j : j + 1] * state + first[j : j + 1]
        rates = rates * product[j : j + 1]
    pair[...] = jnp.zeros_like(pair)
    pair[0:1, :] = rates
    pair[1:2, :] = state


def gates_kernel(lam, q, ends, carry_in, h, gi, ga, c, rows, dpi, dpa, dc, sums):
    total, wide = c.shape
    length = total // 8
    soft = rows[2:3, :]
    step = min(length, 64)
    enter = carry_in[...]
    carry = (jnp.zeros((1, wide), F32),) * 3
    for j in range(7, -1, -1):

        def finish(i, carry, j=j, enter=enter):
            start = pl.multiple_of(j * length + i * step, 8)
            at = pl.ds(start, step)
            state_grad = got(lam, at) + got(q, at) * enter
            before = h[pl.ds(start, step + 8), :][7 : 7 + step]
            open_i, open_a, filtered = gi[at, :], ga[at, :], c[at, :]
            rate, scale = rate_parts(open_a, soft)
            dla = state_grad * before * rate - state_grad * open_i * filtered * rate * rate / scale
            grad_i = state_grad * scale * filtered * open_i * (1.0 - open_i)
            slope = -8.0 * open_a * dla
            grad_a = soft * slope * (1.0 - open_a)
            dpi[at, :] = grad_i.astype(BF16)
            dpa[at, :] = grad_a.astype(BF16)
            dc[at, :] = state_grad * scale * open_i
            return (
                carry[0] + jnp.sum(grad_i, axis=0, keepdims=True),
                carry[1] + jnp.sum(grad_a, axis=0, keepdims=True),
                carry[2] + jnp.sum(slope, axis=0, keepdims=True),
            )

        carry = lax.fori_loop(0, length // step, finish, carry)
        enter = ends[8 + j : 9 + j, :] + ends[j : j + 1, :] * enter
    sums[...] = jnp.zeros_like(sums)
    for row in range(3):
        sums[row : row + 1, :] = carry[row]


def ungate_kernel(dpi, dpa, far, in_whole, de_whole, near_gates, far_gates, dc, vp, dcp, sums, *, taps):
    total = dc.shape[0]
    last = (((1,), (1,)), ((), ()))
    full, half = slice(0, 2 * LANES), slice(2 * LANES, 3 * LANES)
    turned = lambda left, right: lax.dot_general(left, right, last, preferred_element_type=F32)

    def chunk(i, carry):
        start = pl.multiple_of(i * CHUNK, CHUNK)
        at = pl.ds(start, CHUNK)
        whole = turned(dpi[at, full], in_whole[...]) + turned(dpa[at, full], de_whole[...])
        middle = (
            turned(dpi[at, half], near_gates[:, :LANES])
            + turned(dpa[at, half], near_gates[:, LANES:])
            + turned(far[at, :], far_gates[...])
        )
        out = dc[at, :] + jnp.concatenate([whole, middle], axis=1)
        dcp[at, :] = out
        window = vp[pl.ds(start, CHUNK + 8), :]
        return tuple(
            carry[k] + jnp.sum(out * window[8 - k : 8 - k + CHUNK], axis=0, keepdims=True)
            for k in range(taps)
        )

    zero = jnp.zeros((1, dc.shape[1]), F32)
    carry = lax.fori_loop(0, total // CHUNK, chunk, (zero,) * taps)
    sums[...] = jnp.zeros_like(sums)
    for k in range(taps):
        sums[k : k + 1, :] = carry[k]


def unfilter_kernel(slot, dc, following, rows, dv, dcp, *, th, taps):
    total = dc.shape[0]
    dcp[0:total, :] = dc[...]
    dcp[total : total + 8, :] = following[...]

    def order(b, carry):
        window = dcp[pl.ds(pl.multiple_of(b * th, th), th + 8), :]
        out = rows[0:1, :] * window[0:th]
        for k in range(1, taps):
            out = out + rows[k : k + 1, :] * window[k : k + th]
        dv[pl.ds(pl.multiple_of(slot[b] * th, th), th), :] = out.astype(BF16)
        return carry

    lax.fori_loop(0, total // th, order, 0)


def feed_kernel(ge, dz, zb, dge, *, th):
    lanes = dz.shape[1]

    def block(b, carry):
        at = pl.ds(pl.multiple_of(b * th, th), th)
        g, e, d = ge[at, :lanes], ge[at, lanes:], dz[at, :]
        act, inner = gelu_parts(g)
        zb[at, :] = (act * e).astype(BF16)
        dge[at, :lanes] = (d * e * gelu_slope(g, inner)).astype(BF16)
        dge[at, lanes:] = (d * act).astype(BF16)
        return carry

    lax.fori_loop(0, dz.shape[0] // th, block, 0)


def on_chip(kernel, slot, inputs, outs, scratch=()):
    vmem = pl.BlockSpec(memory_space=pltpu.VMEM)
    return pl.pallas_call(
        kernel,
        out_shape=[jax.ShapeDtypeStruct(shape, dtype) for shape, dtype in outs],
        in_specs=[pl.BlockSpec(memory_space=pltpu.SMEM)] + [vmem] * len(inputs),
        out_specs=[vmem] * len(outs),
        scratch_shapes=[pltpu.VMEM(shape, dtype) for shape, dtype in scratch],
        compiler_params=params(),
    )(slot, *inputs)


def in_vmem(kernel, inputs, outs, scratch=()):
    vmem = pl.BlockSpec(memory_space=pltpu.VMEM)
    return pl.pallas_call(
        kernel,
        out_shape=[jax.ShapeDtypeStruct(shape, dtype) for shape, dtype in outs],
        in_specs=[vmem] * len(inputs),
        out_specs=[vmem] * len(outs),
        scratch_shapes=[pltpu.VMEM(shape, dtype) for shape, dtype in scratch],
        compiler_params=params(),
    )(*inputs)


def dot(left, right, over):
    return lax.dot_general(left, right, (over, ((), ())), preferred_element_type=F32)


def shards(
    block_input,
    first_gain,
    gelu_weight,
    scan_weight,
    filter_taps,
    input_gate,
    input_bias,
    decay_gate,
    decay_bias,
    decay_param,
    output_weight,
    second_gain,
    expand_gate,
    expand_value,
    contract_weight,
    output_cotangent,
):
    count = lax.axis_size("seq")
    chip = lax.axis_index("seq")
    core = lax.axis_index("head")
    th = block_input.shape[0] // 2
    width = block_input.shape[1]
    part = gelu_weight.shape[0]
    taps = filter_taps.shape[0]
    local_blocks, gate_rows, block_width = input_gate.shape
    assert block_width == 2 * LANES and width == part * count and local_blocks == 5
    place = chip // 4
    fours = count // 4
    near = 8 * th
    total = 2 * count * th
    lanes_r = 3 * LANES
    slab = 4 * part

    hidden = expand_gate.shape[1]
    lanes = LANES * -(-hidden // (count * LANES))
    hidden_chips = hidden // lanes
    assert hidden_chips * lanes == hidden

    number = jnp.arange(8, dtype=jnp.int32)
    relative = (chip & 3) ^ (number // 2)
    turned = ((relative & 1) << 1) | (relative >> 1)
    slot = jnp.where(number % 2 == 0, turned, relative) + jnp.where(number % 2 == core, 0, 4)
    slot = slot.astype(jnp.int32)

    def slabs(rows):
        return jnp.concatenate(
            [lax.dynamic_slice_in_dim(rows, (place ^ j) * slab, slab, 1) for j in range(fours)],
            axis=1,
        )

    extra = max(16, gate_rows)
    more_rows = ((0, 0), (0, extra - gate_rows), (0, 0))
    gain1 = first_gain.astype(F32)[:, None]
    small = jnp.concatenate(
        [
            filter_taps.transpose(1, 0, 2),
            input_bias[:, None],
            decay_bias[:, None],
            decay_param[:, None],
        ],
        axis=1,
    )
    small = jnp.pad(
        small, ((0, 0), (0, extra - small.shape[1]), (0, LANES - small.shape[2]))
    )
    packed = packed_narrow(
        gain1,
        gelu_weight,
        scan_weight,
        output_weight.T,
        jnp.pad(input_gate, more_rows),
        jnp.pad(decay_gate, more_rows),
        small,
    )

    def both_sides(pieces):
        kept = lax.dynamic_index_in_dim(pieces, core, 0, False)
        given = core_swap(lax.dynamic_index_in_dim(pieces, 1 - core, 0, False))
        return jnp.concatenate(
            [jnp.where(core == 0, kept, given), jnp.where(core == 0, given, kept)], axis=0
        )

    packed = [near_exchanged(both_sides(piece)) for piece in packed]
    pieces_yv = row_gathered(packed[0])
    weight_yv = jnp.concatenate([piece[:, 2 * extra :].reshape(slab, -1) for piece in pieces_yv])
    heads = jnp.stack([piece[:, : 2 * extra] for piece in pieces_yv])
    heads = jnp.concatenate(
        [lax.dynamic_index_in_dim(heads, place ^ j, 0, False) for j in range(fours)]
    )
    gates = heads[:, :gate_rows].reshape(block_width, 2 * lanes_r)
    small = heads[:, extra : extra + taps + 3]
    small = [
        small[:, :, i * LANES : i * LANES + gate_rows].transpose(1, 0, 2).reshape(taps + 3, -1)
        for i in range(2)
    ]
    own_half = lambda a, axis=0: lax.dynamic_slice_in_dim(a, core * LANES, LANES, axis)
    far_half = lambda a, axis=0: lax.dynamic_slice_in_dim(a, (1 - core) * LANES, LANES, axis)
    small = jnp.concatenate([small[0], own_half(small[1], 1)], axis=1).astype(F32)
    tap_rows = jnp.pad(small[:taps], ((0, 8 - taps), (0, 0)))
    param_row = small[taps + 2 :]
    gate_rows_of = jnp.pad(
        jnp.concatenate([small[taps : taps + 2], jax.nn.softplus(param_row)], axis=0),
        ((0, 5), (0, 0)),
    )
    in_whole, de_whole = gates[:, : 2 * LANES], gates[:, lanes_r : lanes_r + 2 * LANES]
    half_gates = jnp.concatenate([gates[:, 2 * LANES : lanes_r], gates[:, lanes_r + 2 * LANES :]], 1)

    x = lax.dynamic_slice_in_dim(block_input, core * th, th, 0).astype(F32)
    s1 = lax.rsqrt(jnp.mean(x * x, axis=-1, keepdims=True) + EPSILON)
    first = near_gathered(slabs((x * s1).astype(BF16)))
    cotangent = lax.dynamic_slice_in_dim(output_cotangent, core * th, th, 0)
    given_out = jnp.concatenate(gathered(after(cotangent, first)))
    pieces_out = row_gathered(after(packed[1], *pieces_yv))
    weight_out = jnp.concatenate([piece.reshape(slab, lanes_r) for piece in pieces_out])

    gain2 = second_gain.astype(F32)[:, None]
    wide = packed_wide(gain2, expand_gate, expand_value, contract_weight.T, count, lanes)
    wide = all_to_all(after(wide, weight_yv)).reshape(width, 3 * lanes)

    yv = dot(first, weight_yv, ((1,), (0,)))
    tail = lax.dynamic_slice_in_dim(yv[:, lanes_r:], slot[7] * th + th - 8, 8, 0)
    token_f32, token_bf16 = ((near, lanes_r), F32), ((near, lanes_r), BF16)
    padded = ((near + 8, lanes_r), F32)
    few = ((8, lanes_r), F32)
    tiled = ((3, near, LANES), F32)
    y, vp, c, cb = on_chip(
        functools.partial(filter_kernel, th=th, taps=taps),
        slot,
        [yv, next_four(tail, 1), tap_rows],
        [token_f32, padded, token_f32, token_bf16],
    )
    cb_far = core_swap(cb[:, 2 * LANES :])
    near_gates, far_gates = own_half(half_gates), far_half(half_gates)
    gi, ga, hp, p, ends, pair = in_vmem(
        states_kernel,
        [
            cb,
            cb_far,
            jnp.concatenate([in_whole, de_whole], axis=1),
            near_gates,
            far_gates,
            c,
            gate_rows_of,
        ],
        [token_f32, token_f32, tiled, tiled, ((16, lanes_r), F32), few],
        [tiled],
    )
    h, ob = on_chip(
        functools.partial(merge_kernel, th=th),
        slot,
        [hp, p, ends, carried(pair, place, False), y],
        [padded, token_bf16],
    )
    weight_ge, weight_c = wide[:, : 2 * lanes], wide[:, 2 * lanes :]
    dz = dot(given_out, weight_c, ((1,), (0,)))
    out_both = jnp.concatenate([weight_out, core_swap(weight_out)], axis=1)
    r = x + slabs(near_scattered(ob, out_both))

    s2 = lax.rsqrt(jnp.mean(r * r, axis=-1, keepdims=True) + EPSILON)
    second = gathered((r * s2).astype(BF16), [dz])
    second = jnp.concatenate(second)
    zb, dge = in_vmem(
        functools.partial(feed_kernel, th=th),
        [dot(second, weight_ge, ((1,), (0,))), dz],
        [((total, lanes), BF16), ((total, 2 * lanes), BF16)],
    )
    ge_both = jnp.concatenate([weight_ge, core_swap(weight_ge)], axis=1)
    c_both = jnp.concatenate([weight_c, core_swap(weight_c)], axis=1)
    (back2,) = scattered((grouped(dge), ge_both))
    dr = (
        cotangent.astype(F32)
        + s2 * back2
        - r * (s2 * s2 * s2) * jnp.mean(back2 * r, axis=-1, keepdims=True)
    )
    dq = near_gathered(slabs(dr.astype(BF16)))

    wide_grad = jnp.concatenate(
        lax.optimization_barrier(
            (
                dot(second, dge, ((0,), (0,))).astype(BF16),
                dot(given_out, zb, ((0,), (0,))).astype(BF16),
            )
        ),
        axis=1,
    )
    dq, wide_grad = lax.optimization_barrier((dq, wide_grad))
    (out_sum,) = scattered((grouped(after(zb, dq)), c_both))
    out_half = (r + out_sum).astype(BF16)
    wide_grad = all_to_all(wide_grad.reshape(count, part, 3 * lanes))
    gate_grad_out, value_grad_out, contract_grad_out, gain2_part = unpacked_wide(
        wide_grad, gain2, expand_gate, expand_value, lanes
    )

    dob = dot(dq, weight_out, ((1,), (0,)))
    dy, lam, q, ends, pair = on_chip(
        functools.partial(adjoint_kernel, th=th),
        slot,
        [dob, y, h, ga, gate_rows_of],
        [token_bf16, tiled, tiled, ((16, lanes_r), F32), few],
        [tiled],
    )
    dpi, dpa, dc, sums = in_vmem(
        gates_kernel,
        [lam, q, ends, carried(pair, place, True), h, gi, ga, c, gate_rows_of],
        [token_bf16, token_bf16, token_f32, few],
    )
    half_grads = jnp.concatenate([dpi[:, 2 * LANES :], dpa[:, 2 * LANES :]], axis=1)
    dc, tap_sums = in_vmem(
        functools.partial(ungate_kernel, taps=taps),
        [
            dpi,
            dpa,
            core_swap(half_grads),
            in_whole,
            de_whole,
            near_gates,
            own_half(core_swap(half_gates)),
            dc,
            vp,
        ],
        [token_f32, few],
    )
    dv = on_chip(
        functools.partial(unfilter_kernel, th=th, taps=taps),
        slot,
        [dc, next_four(dc[:8], -1), tap_rows],
        [token_bf16],
        [padded],
    )[0]
    dyv = jnp.concatenate([dy, dv], axis=1)

    def to_owners(grad):
        grad = row_scattered(list(grad)).astype(BF16)
        grad = near_exchanged(grad)
        kept = lax.dynamic_slice_in_dim(grad, 2 * core, 2, 0)
        given = core_swap(lax.dynamic_slice_in_dim(grad, 2 * (1 - core), 2, 0))
        return jnp.stack([jnp.where(core == 0, kept, given), jnp.where(core == 0, given, kept)])

    out_grad = lax.optimization_barrier(dot(dq, ob, ((0,), (0,))).astype(BF16))
    out_grad = to_owners(out_grad.reshape(fours, 4, part, lanes_r))
    yv_grad = lax.optimization_barrier(dot(first, dyv, ((0,), (0,))).astype(BF16))
    yv_grad = yv_grad.reshape(fours, 4, part, 2 * lanes_r)

    def gate_grad(grad):
        whole = dot(cb[:, : 2 * LANES], grad[:, : 2 * LANES], ((0,), (0,)))
        own_rows = dot(cb[:, 2 * LANES :], grad[:, 2 * LANES :], ((0,), (0,)))
        far_rows = dot(cb_far, grad[:, 2 * LANES :], ((0,), (0,)))
        half = jnp.concatenate(
            [jnp.where(core == 0, own_rows, far_rows), jnp.where(core == 0, far_rows, own_rows)]
        )
        return jnp.concatenate([whole, half], axis=1)

    head_grad = jnp.concatenate([gate_grad(dpi), gate_grad(dpa)], axis=1)
    head_grad = head_grad.reshape(count, gate_rows, 2 * lanes_r)
    head_grad = jnp.pad(head_grad, ((0, 0), (0, extra - gate_rows), (0, 0)))
    small_grad = jnp.concatenate(
        [tap_sums[:taps], sums[:2], sums[2:3] * jax.nn.sigmoid(param_row)], axis=0
    )
    middle = small_grad[:, 2 * LANES :]
    nothing = jnp.zeros_like(middle)
    small_grad = [
        small_grad[:, : 2 * LANES],
        jnp.where(
            core == 0,
            jnp.concatenate([middle, nothing], axis=1),
            jnp.concatenate([nothing, middle], axis=1),
        ),
    ]
    small_grad = [
        jnp.pad(
            a.reshape(taps + 3, count, gate_rows).transpose(1, 0, 2),
            ((0, 0), (0, extra - taps - 3), (0, LANES - gate_rows)),
        )
        for a in small_grad
    ]
    small_grad = jnp.concatenate(small_grad, axis=2)
    small_grad = jnp.pad(small_grad, ((0, 0), (0, 0), (0, 2 * lanes_r - 2 * LANES)))
    head_grad = jnp.concatenate([head_grad, small_grad], axis=1).astype(BF16)
    head_grad = head_grad.reshape(fours, 4, 2 * extra, 2 * lanes_r)
    head_grad = jnp.stack(
        [lax.dynamic_index_in_dim(head_grad, place ^ j, 0, False) for j in range(fours)]
    )
    yv_grad = to_owners(jnp.concatenate([head_grad, yv_grad], axis=2))
    (
        gelu_grad_out,
        scan_grad_out,
        output_grad_out,
        input_gate_out,
        decay_gate_out,
        gain1_part,
    ) = unpacked_narrow(
        yv_grad, out_grad, gain1, gelu_weight, scan_weight, local_blocks, gate_rows, extra
    )
    small_sum = yv_grad[:, :, extra : extra + taps + 3].astype(F32)
    whole_sum = small_sum[..., :gate_rows]
    half_sum = small_sum[..., LANES : LANES + gate_rows]
    half_sum = half_sum[0] + half_sum[1]
    small_sum = jnp.stack(
        [whole_sum[0, 0], half_sum[0], whole_sum[1, 0], whole_sum[0, 1], whole_sum[1, 1]], axis=1
    )

    back1 = slabs(near_scattered(dyv, weight_yv, core_swap(weight_yv)))
    in_half = dr + s1 * back1 - x * (s1 * s1 * s1) * jnp.mean(back1 * x, axis=-1, keepdims=True)

    gain_parts = jnp.stack([jnp.sum(gain1_part, axis=1), jnp.sum(gain2_part, axis=1)])
    gain_grads = gain_parts + core_swap(gain_parts)

    def both_halves(half):
        swapped = core_swap(half)
        return jnp.concatenate(
            [jnp.where(core == 0, half, swapped), jnp.where(core == 0, swapped, half)], axis=0
        )

    return (
        both_halves(out_half),
        both_halves(in_half),
        gain_grads[0],
        gelu_grad_out,
        scan_grad_out,
        small_sum[:taps],
        input_gate_out,
        small_sum[taps],
        decay_gate_out,
        small_sum[taps + 1],
        small_sum[taps + 2],
        output_grad_out.T,
        gain_grads[1],
        gate_grad_out,
        value_grad_out,
        contract_grad_out.T,
    )


def solution(mesh):
    in_specs = (
        P("seq", None),
        P("seq"),
        P("seq", "head"),
        P("seq", "head"),
        P(None, "head", "seq"),
        P("head", "seq", None),
        P("head", "seq"),
        P("head", "seq", None),
        P("head", "seq"),
        P("head", "seq"),
        P("head", "seq"),
        P("seq"),
        P("seq", "head"),
        P("seq", "head"),
        P("head", "seq"),
        P("seq", None),
    )
    out_specs = (
        P("seq", None),
        P("seq", None),
        P("seq"),
        P("seq", "head"),
        P("seq", "head"),
        P(None, "head", "seq"),
        P("head", "seq", None),
        P("head", "seq"),
        P("head", "seq", None),
        P("head", "seq"),
        P("head", "seq"),
        P("head", "seq"),
        P("seq"),
        P("seq", "head"),
        P("seq", "head"),
        P("head", "seq"),
    )
    return jax.shard_map(shards, mesh=mesh, in_specs=in_specs, out_specs=out_specs, check_vma=False)
```

time: 883 us -> 850 us (0.963)
  other arithmetic: 37.7 us -> 70.1 us
  local copies, waits for them, and re-layouts: 90.4 us -> 70.8 us
  Pallas kernels: 77 us -> 62 us
  starting transfers between devices: 205 us -> 190 us
  matrix products: 87.3 us -> 74.6 us
    ppermute x0 -> x32, waiting for transfers between devices: none -> 133 us  [the longest x30 132 us: row_send(): return lax.ppermute(value, BOTH, pairs)]
    ppermute x77 -> x52, waiting for transfers between devices: 305 us -> 220 us  [xor_send(): return lax.ppermute(value, BOTH, pairs)]
    ppermute x0 -> x32, starting transfers between devices: none -> 71.9 us  [the longest x30 66.7 us: row_send(): return lax.ppermute(value, BOTH, pairs)]
    all_to_all x4 -> x2, waiting for transfers between devices: 63.9 us -> 0.01 us  [all_to_all(): return lax.all_to_all(pieces, 'seq', 0, 0, tiled=True)]
    ppermute x77 -> x52, starting transfers between devices: 99.1 us -> 63.1 us  [xor_send(): return lax.ppermute(value, BOTH, pairs)]
    ppermute x27 -> x28, starting transfers between devices: 62.5 us -> 27.1 us  [core_swap(): return lax.ppermute(value, 'head', [(0, 1), (1, 0)])]
    all_to_all x4 -> x2, starting transfers between devices: 43.8 us -> 9.74 us  [all_to_all(): return lax.all_to_all(pieces, 'seq', 0, 0, tiled=True)]
    pallas_call x5 -> x4, Pallas kernels: 40.5 us -> 15 us  [on_chip(): pl.pallas_call(kernel, out_shape=[jax.ShapeDtypeStruct(shape, dtype) for...]
  transfers between devices with their start and end apart: 108 -> 118, of which waited for: 39 -> 35; matrix products, arithmetic and copies ran while one was open for 21% -> 23% of each run, Pallas kernels for 9% -> 6%
where the time goes in v3:
time: 850 us; the launch traced here: 838 us
  waiting for transfers between devices  368 us (43%)
  starting transfers between devices  190 us (22%)
  matrix products  74.6 us (9%)
  local copies, waits for them, and re-layouts  70.8 us (8%)
  other arithmetic  70.1 us (8%)
  Pallas kernels  62 us (7%)
    ppermute x52, waiting for transfers between devices, xor_send(): return lax.ppermute(value, BOTH, pairs)  220 us
    ppermute x30, waiting for transfers between devices, row_send(): return lax.ppermute(value, BOTH, pairs)  132 us
    dot_general x25, matrix products, dot(): lax.dot_general(left, right, (over, ((), ())), preferred_element_type=F32)  74.6 us
    ppermute x30, starting transfers between devices, row_send(): return lax.ppermute(value, BOTH, pairs)  66.7 us
    ppermute x52, starting transfers between devices, xor_send(): return lax.ppermute(value, BOTH, pairs)  63.1 us
    unnamed x162, local copies, waits for them, and re-layouts  34.3 us
    pallas_call x6, Pallas kernels, in_vmem(): pl.pallas_call(kernel, out_shape=[jax.ShapeDtypeStruct(shape, dtype) for...  28.8 us
    ppermute x28, starting transfers between devices, core_swap(): return lax.ppermute(value, 'head', [(0, 1), (1, 0)])  27.1 us
  transfers between devices with their start and end apart: 118, of which 35 were waited for; matrix products, arithmetic and copies ran while one was open for 23% of the time, Pallas kernels for 6%

profile of v3, /device:TPU:5, one launch (start us, length us, event | category | flops | bytes accessed | tf_op | source)
XLA Modules:
  0.0 838.4 jit_solution(2891311461436630835)
XLA Ops:
  17.6 7.6 collective-permute-done.1
  28.9 4.2 all-to-all-start
  35.5 10.6 %shard_map.283 = bf16[16,160,768]{2,1,0:T(8,128)(2,1)} custom-call(f32[160,1]{1,0:T(8,128)} %copy.54.gain, bf16[160,3840]{1,0:T(8,128)(2,1)} %gate.3, bf16[160,3840]{1,0:T(8,128)(2,1)} %value.3, bf16[160,3840]{1,0:T(8,128)(2,1)} %bitcast.206), custom_call_target="tpu_custom_call" | custom-call | tf_op jit(solution)/shard_map/pallas_call | solution.py:191
  48.1 4.4 all-to-all-start.1
  54.6 4.2 pad_maximum_fusion.4
  59.9 3.8 collective-permute-start.38
  65.5 20.4 %collective-permute-done.38 = bf16[64,2560]{1,0:T(8,128)(2,1)S(1)} collective-permute-done((bf16[64,2560]{1,0:T(8,128)(2,1)S(1)}, bf16[64,2560]{1,0:T(8,128)(2,1)S(1)}, u32[]{:S(2)}, u32[]{:S(2)}) %collective-permute-start.38) | collective-permute-done | bytes 327712 | tf_op jit(solution)/shard_map/ppermute | solution.py:41
  97.6 5.8 collective-permute-done.40
  107.2 4.1 collective-permute-done.44
  112.8 13.5 %collective-permute-done.7 = bf16[4,192,768]{2,1,0:T(8,128)(2,1)S(1)} collective-permute-done((bf16[4,192,768]{2,1,0:T(8,128)(2,1)S(1)}, bf16[4,192,768]{2,1,0:T(8,128)(2,1)S(1)}, u32[]{:S(2)}, u32[]{:S(2)}) %collective-permute-start.7) | collective-permute-done | bytes 1179680 | tf_op jit(solution)/shard_map/ppermute | solution.py:41
  136.5 3.9 collective-permute-done.47
  141.8 16.9 %collective-permute-done.8 = bf16[4,192,768]{2,1,0:T(8,128)(2,1)S(1)} collective-permute-done((bf16[4,192,768]{2,1,0:T(8,128)(2,1)S(1)}, bf16[4,192,768]{2,1,0:T(8,128)(2,1)S(1)}, u32[]{:S(2)}, u32[]{:S(2)}) %collective-permute-start.8) | collective-permute-done | bytes 1179680 | tf_op jit(solution)/shard_map/ppermute | solution.py:41
  165.5 3.9 collective-permute-start.9
  176.2 7.9 collective-permute-done.19
  184.2 11.3 %collective-permute-done.20 = bf16[4,160,384]{2,1,0:T(8,128)(2,1)S(1)} collective-permute-done((bf16[4,160,384]{2,1,0:T(8,128)(2,1)S(1)}, bf16[4,160,384]{2,1,0:T(8,128)(2,1)S(1)}, u32[]{:S(2)}, u32[]{:S(2)}) %collective-permute-start.20) | collective-permute-done | bytes 491552 | tf_op jit(solution)/shard_map/ppermute | solution.py:41
  208.6 6.8 shard_map.281
  219.8 4.8 all-to-all-start.2
  243.3 18.5 %collective-permute-done.22 = bf16[128,2560]{1,0:T(8,128)(2,1)S(1)} collective-permute-done((bf16[128,2560]{1,0:T(8,128)(2,1)S(1)}, bf16[128,2560]{1,0:T(8,128)(2,1)S(1)}, u32[]{:S(2)}, u32[]{:S(2)}) %collective-permute-start.22) | collective-permute-done | bytes 655392 | tf_op jit(solution)/shard_map/ppermute | solution.py:30
  262.0 3.6 collective-permute-start.23
  266.8 14.3 %collective-permute-done.23 = bf16[64,2560]{1,0:T(8,128)(2,1)S(1)} collective-permute-done((bf16[64,2560]{1,0:T(8,128)(2,1)S(1)}, bf16[64,2560]{1,0:T(8,128)(2,1)S(1)}, u32[]{:S(2)}, u32[]{:S(2)}) %collective-permute-start.23) | collective-permute-done | bytes 327712 | tf_op jit(solution)/shard_map/ppermute | solution.py:30
  284.6 9.9 %collective-permute-done.24 = bf16[64,2560]{1,0:T(8,128)(2,1)S(1)} collective-permute-done((bf16[64,2560]{1,0:T(8,128)(2,1)S(1)}, bf16[64,2560]{1,0:T(8,128)(2,1)S(1)}, u32[]{:S(2)}, u32[]{:S(2)}) %collective-permute-start.24) | collective-permute-done | bytes 327712 | tf_op jit(solution)/shard_map/ppermute | solution.py:30
  294.6 10.9 %collective-permute-start.25 = (bf16[128,2560]{1,0:T(8,128)(2,1)S(1)}, bf16[128,2560]{1,0:T(8,128)(2,1)S(1)}, u32[]{:S(2)}, u32[]{:S(2)}) collective-permute-start(bf16[128,2560]{1,0:T(8,128)(2,1)S(1)} %pad_maximum_fusion.25), channel_id=1, source_target_pairs={{0,2},{1,5},{2,0},{3,7},{4,6},{5,1},{6,4},{7,3},{8,10},{9,13},{10,... | collective-permute-start | bytes 1966088 | tf_op jit(solution)/shard_map/ppermute | solution.py:30
  313.1 22.4 %collective-permute-done.34 = bf16[64,2560]{1,0:T(8,128)(2,1)S(1)} collective-permute-done((bf16[64,2560]{1,0:T(8,128)(2,1)S(1)}, bf16[64,2560]{1,0:T(8,128)(2,1)S(1)}, u32[]{:S(2)}, u32[]{:S(2)}) %collective-permute-start.34) | collective-permute-done | bytes 327712 | tf_op jit(solution)/shard_map/ppermute | solution.py:41
  350.9 7.5 collective-permute-done.33
  361.0 8.7 %fusion.138.dz = f32[2048,256]{1,0:T(8,128)} fusion(bf16[2048,2560]{1,0:T(8,128)(2,1)} %constant_dynamic-update-slice_fusion, bf16[2560,768]{1,0:T(8,128)(2,1)} %bitcast.42), kind=kOutput, calls=%fused_computation.411 | convolution fusion | flops 2684354560 | bytes 13893632 | tf_op jit(solution)/shard_map/dot_general | solution.py:637
  373.5 6.2 collective-permute-done.53
  384.8 4.0 copy-done.59
  388.8 9.4 %fusion.140.ge = f32[2048,512]{1,0:T(8,128)} fusion(bf16[2048,2560]{1,0:T(8,128)(2,1)S(1)} %constant_dynamic-update-slice_fusion.16, bf16[2560,768]{1,0:T(8,128)(2,1)} %bitcast.42), kind=kOutput, calls=%fused_computation.413 | convolution fusion | flops 5368709120 | bytes 17301504 | tf_op jit(solution)/shard_map/dot_general | solution.py:637
  398.2 6.4 shard_map.284
  430.0 12.6 %collective-permute-done.62 = bf16[128,2560]{1,0:T(8,128)(2,1)S(1)} collective-permute-done((bf16[128,2560]{1,0:T(8,128)(2,1)S(1)}, bf16[128,2560]{1,0:T(8,128)(2,1)S(1)}, u32[]{:S(2)}, u32[]{:S(2)}) %collective-permute-start.62) | collective-permute-done | bytes 655392 | tf_op jit(solution)/shard_map/ppermute | solution.py:30
  442.9 10.4 %collective-permute-done.60 = bf16[128,2560]{1,0:T(8,128)(2,1)S(1)} collective-permute-done((bf16[128,2560]{1,0:T(8,128)(2,1)S(1)}, bf16[128,2560]{1,0:T(8,128)(2,1)S(1)}, u32[]{:S(2)}, u32[]{:S(2)}) %collective-permute-start.60) | collective-permute-done | bytes 655392 | tf_op jit(solution)/shard_map/ppermute | solution.py:30
  455.6 5.0 collective-permute-start.67
  461.5 24.4 %collective-permute-done.67 = bf16[64,2560]{1,0:T(8,128)(2,1)S(1)} collective-permute-done((bf16[64,2560]{1,0:T(8,128)(2,1)S(1)}, bf16[64,2560]{1,0:T(8,128)(2,1)S(1)}, u32[]{:S(2)}, u32[]{:S(2)}) %collective-permute-start.67) | collective-permute-done | bytes 327712 | tf_op jit(solution)/shard_map/ppermute | solution.py:30
  497.2 9.0 %convolution_convert_fusion.1 = bf16[2560,512]{1,0:T(8,128)(2,1)S(1)} fusion(bf16[2048,2560]{1,0:T(8,128)(2,1)} %copy-done.59, bf16[2048,512]{1,0:T(8,128)(2,1)S(1)} %copy-done.25), kind=kOutput, calls=%fused_computation.3 | convolution fusion | flops 5370019840 | bytes 15204352 | tf_op jit(solution)/shard_map/dot_general | solution.py:637
  516.9 6.1 shard_map.285
  535.6 5.0 shard_map.286
  549.5 4.0 shard_map.287
  572.4 4.1 collective-permute-start.99
  601.7 24.0 %collective-permute-done.101 = bf16[4,192,768]{2,1,0:T(8,128)(2,1)S(1)} collective-permute-done((bf16[4,192,768]{2,1,0:T(8,128)(2,1)S(1)}, bf16[4,192,768]{2,1,0:T(8,128)(2,1)S(1)}, u32[]{:S(2)}, u32[]{:S(2)}) %collective-permute-start.101) | collective-permute-done | bytes 1179680 | tf_op jit(solution)/shard_map/ppermute | solution.py:41
  636.3 25.4 %collective-permute-start.103 = (bf16[4,192,768]{2,1,0:T(8,128)(2,1)}, bf16[4,192,768]{2,1,0:T(8,128)(2,1)}, u32[]{:S(2)}, u32[]{:S(2)}) collective-permute-start(bf16[4,192,768]{2,1,0:T(8,128)(2,1)} %fusion.14), channel_id=1, source_target_pairs={{0,8},{1,9},{2,10},{3,11},{4,12},{5,13},{6,14},{7,15},{8,0},{9,1},... | collective-permute-start | bytes 3538952 | tf_op jit(solution)/shard_map/ppermute | solution.py:41
  665.9 5.5 all-to-all-start.4
  675.9 9.5 %collective-permute-done.103 = bf16[4,192,768]{2,1,0:T(8,128)(2,1)} collective-permute-done((bf16[4,192,768]{2,1,0:T(8,128)(2,1)}, bf16[4,192,768]{2,1,0:T(8,128)(2,1)}, u32[]{:S(2)}, u32[]{:S(2)}) %collective-permute-start.103) | collective-permute-done | bytes 1179680 | tf_op jit(solution)/shard_map/ppermute | solution.py:41
  698.3 8.5 %all-to-all-done.3 = bf16[4,192,768]{2,1,0:T(8,128)(2,1)S(1)} async-done(((bf16[4,192,768]{2,1,0:T(8,128)(2,1)}), bf16[4,192,768]{2,1,0:T(8,128)(2,1)S(1)}, u32[]{:S(2)}, u32[]{:S(2)}) %all-to-all-start.3) | async-done | bytes 1179680 | tf_op jit(solution)/shard_map/all_to_all | solution.py:134
  706.8 4.9 all-to-all-start.5
  719.4 6.6 collective-permute-start.98
  727.0 86.6 %collective-permute-done.83 = bf16[64,2560]{1,0:T(8,128)(2,1)S(1)} collective-permute-done((bf16[64,2560]{1,0:T(8,128)(2,1)S(1)}, bf16[64,2560]{1,0:T(8,128)(2,1)S(1)}, u32[]{:S(2)}, u32[]{:S(2)}) %collective-permute-start.83) | collective-permute-done | bytes 327712 | tf_op jit(solution)/shard_map/ppermute | solution.py:30
  822.6 3.7 shard_map.289
  827.4 7.6 shard_map.290
  (596 shorter events, 316.0 us)
Async XLA Ops:
  26.4 28.1 %collective-permute-start.2 = (bf16[256,2560]{1,0:T(8,128)(2,1)}, bf16[256,2560]{1,0:T(8,128)(2,1)}, u32[]{:S(2)}, u32[]{:S(2)}) collective-permute-start(bf16[256,2560]{1,0:T(8,128)(2,1)} %pad_maximum_fusion.9), channel_id=1, source_target_pairs={{0,1},{1,0},{2,3},{3,2},{4,5},{5,4},{6,7},{7,6},{8,9},{9,8},{10,11... | collective-permute-start | bytes 3932168 | tf_op jit(solution)/shard_map/ppermute | solution.py:34
  48.1 110.9 %all-to-all-start.1 = ((bf16[4,160,384]{2,1,0:T(8,128)(2,1)}), bf16[4,160,384]{2,1,0:T(8,128)(2,1)}, u32[]{:S(2)}, u32[]{:S(2)}) async-start(bf16[4,160,384]{2,1,0:T(8,128)(2,1)} %pad_maximum_fusion.38), calls=%async_computation.1 | async-start | bytes 983040 | tf_op jit(solution)/shard_map/all_to_all | solution.py:134
  52.4 36.0 %collective-permute-start.4 = (bf16[4,192,768]{2,1,0:T(8,128)(2,1)S(1)}, bf16[4,192,768]{2,1,0:T(8,128)(2,1)S(1)}, u32[]{:S(2)}, u32[]{:S(2)}) collective-permute-start(bf16[4,192,768]{2,1,0:T(8,128)(2,1)S(1)} %all-to-all-done), channel_id=1, source_target_pairs={{0,8},{1,9},{2,10},{3,11},{4,12},{5,13},{6,14},{7,15},{8,0},{9,1},... | collective-permute-start | bytes 3538952 | tf_op jit(solution)/shard_map/ppermute | solution.py:41
  53.7 37.8 %collective-permute-start.6 = (bf16[4,192,768]{2,1,0:T(8,128)(2,1)S(1)}, bf16[4,192,768]{2,1,0:T(8,128)(2,1)S(1)}, u32[]{:S(2)}, u32[]{:S(2)}) collective-permute-start(bf16[4,192,768]{2,1,0:T(8,128)(2,1)S(1)} %all-to-all-done), channel_id=1, source_target_pairs={{8,16},{9,17},{10,18},{11,19},{12,20},{13,21},{14,22},{15,23},{16,... | collective-permute-start | bytes 3538952 | tf_op jit(solution)/shard_map/ppermute | solution.py:41
  65.1 28.8 %collective-permute-start.37 = (bf16[128,2560]{1,0:T(8,128)(2,1)S(1)}, bf16[128,2560]{1,0:T(8,128)(2,1)S(1)}, u32[]{:S(2)}, u32[]{:S(2)}) collective-permute-start(bf16[128,2560]{1,0:T(8,128)(2,1)S(1)} %pad_maximum_fusion.29), channel_id=1, source_target_pairs={{0,2},{1,5},{2,0},{3,7},{4,6},{5,1},{6,4},{7,3},{8,10},{9,13},{10,... | collective-permute-start | bytes 1966088 | tf_op jit(solution)/shard_map/ppermute | solution.py:30
  92.2 34.1 %collective-permute-start.7 = (bf16[4,192,768]{2,1,0:T(8,128)(2,1)S(1)}, bf16[4,192,768]{2,1,0:T(8,128)(2,1)S(1)}, u32[]{:S(2)}, u32[]{:S(2)}) collective-permute-start(bf16[4,192,768]{2,1,0:T(8,128)(2,1)S(1)} %collective-permute-done.6), channel_id=1, source_target_pairs={{8,0},{9,1},{10,2},{11,3},{12,4},{13,5},{14,6},{15,7},{16,24},{17,... | collective-permute-start | bytes 3538952 | tf_op jit(solution)/shard_map/ppermute | solution.py:41
  93.9 39.4 %collective-permute-start.46 = (bf16[64,2560]{1,0:T(8,128)(2,1)S(1)}, bf16[64,2560]{1,0:T(8,128)(2,1)S(1)}, u32[]{:S(2)}, u32[]{:S(2)}) collective-permute-start(bf16[64,2560]{1,0:T(8,128)(2,1)S(1)} %collective-permute-done.41), channel_id=1, source_target_pairs={{8,0},{9,1},{10,2},{11,3},{12,4},{13,5},{14,6},{15,7},{16,24},{17,... | collective-permute-start | bytes 983048 | tf_op jit(solution)/shard_map/ppermute | solution.py:41
  126.7 32.0 %collective-permute-start.8 = (bf16[4,192,768]{2,1,0:T(8,128)(2,1)S(1)}, bf16[4,192,768]{2,1,0:T(8,128)(2,1)S(1)}, u32[]{:S(2)}, u32[]{:S(2)}) collective-permute-start(bf16[4,192,768]{2,1,0:T(8,128)(2,1)S(1)} %collective-permute-done.5), channel_id=1, source_target_pairs={{8,0},{9,1},{10,2},{11,3},{12,4},{13,5},{14,6},{15,7},{16,24},{17,... | collective-permute-start | bytes 3538952 | tf_op jit(solution)/shard_map/ppermute | solution.py:41
  141.3 90.1 %collective-permute-start.48 = (bf16[128,2560]{1,0:T(8,128)(2,1)}, bf16[128,2560]{1,0:T(8,128)(2,1)}, u32[]{:S(2)}, u32[]{:S(2)}) collective-permute-start(bf16[128,2560]{1,0:T(8,128)(2,1)} %pad_maximum_fusion.32), channel_id=1, source_target_pairs={{0,2},{1,5},{2,0},{3,7},{4,6},{5,1},{6,4},{7,3},{8,10},{9,13},{10,... | collective-permute-start | bytes 1966088 | tf_op jit(solution)/shard_map/ppermute | solution.py:30
  165.5 36.7 %collective-permute-start.9 = (f32[8,384]{1,0:T(8,128)}, f32[8,384]{1,0:T(8,128)}, u32[]{:S(2)}, u32[]{:S(2)}) collective-permute-start(f32[8,384]{1,0:T(8,128)} %constant_dynamic-slice_fusion.29), channel_id=1, source_target_pairs={{0,8},{1,9},{2,10},{3,11},{4,12},{5,13},{6,14},{7,15},{8,16},{9,17... | collective-permute-start | bytes 36872 | tf_op jit(solution)/shard_map/ppermute | solution.py:145
  198.1 37.2 %collective-permute-start.21 = (bf16[2560,384]{1,0:T(8,128)(2,1)S(1)}, bf16[2560,384]{1,0:T(8,128)(2,1)}, u32[]{:S(2)}, u32[]{:S(2)}) collective-permute-start(bf16[2560,384]{1,0:T(8,128)(2,1)S(1)} %pad_maximum_fusion.7), channel_id=1, source_target_pairs={{0,1},{1,0},{2,3},{3,2},{4,5},{5,4},{6,7},{7,6},{8,9},{9,8},{10,11... | collective-permute-start | bytes 5898248 | tf_op jit(solution)/shard_map/ppermute | solution.py:34
  219.8 141.3 %all-to-all-start.2 = ((bf16[16,160,768]{2,1,0:T(8,128)(2,1)}), bf16[16,160,768]{2,1,0:T(8,128)(2,1)}, u32[]{:S(2)}, u32[]{:S(2)}) async-start(bf16[16,160,768]{2,1,0:T(8,128)(2,1)} %shard_map.283), calls=%async_computation.2 | async-start | bytes 7864320 | tf_op jit(solution)/shard_map/all_to_all | solution.py:171
  226.4 39.2 %collective-permute-start.51 = (bf16[256,2560]{1,0:T(8,128)(2,1)}, bf16[256,2560]{1,0:T(8,128)(2,1)S(1)}, u32[]{:S(2)}, u32[]{:S(2)}) collective-permute-start(bf16[256,2560]{1,0:T(8,128)(2,1)} %pad_maximum_fusion.12), channel_id=1, source_target_pairs={{0,1},{1,0},{2,3},{3,2},{4,5},{5,4},{6,7},{7,6},{8,9},{9,8},{10,11... | collective-permute-start | bytes 3932168 | tf_op jit(solution)/shard_map/ppermute | solution.py:34
  234.8 47.5 %collective-permute-start.52 = (bf16[256,2560]{1,0:T(8,128)(2,1)S(1)}, bf16[256,2560]{1,0:T(8,128)(2,1)S(1)}, u32[]{:S(2)}, u32[]{:S(2)}) collective-permute-start(bf16[256,2560]{1,0:T(8,128)(2,1)S(1)} %pad_maximum_fusion.13), channel_id=1, source_target_pairs={{0,1},{1,0},{2,3},{3,2},{4,5},{5,4},{6,7},{7,6},{8,9},{9,8},{10,11... | collective-permute-start | bytes 3932168 | tf_op jit(solution)/shard_map/ppermute | solution.py:34
  294.6 41.1 %collective-permute-start.25 = (bf16[128,2560]{1,0:T(8,128)(2,1)S(1)}, bf16[128,2560]{1,0:T(8,128)(2,1)S(1)}, u32[]{:S(2)}, u32[]{:S(2)}) collective-permute-start(bf16[128,2560]{1,0:T(8,128)(2,1)S(1)} %pad_maximum_fusion.25), channel_id=1, source_target_pairs={{0,2},{1,5},{2,0},{3,7},{4,6},{5,1},{6,4},{7,3},{8,10},{9,13},{10,... | collective-permute-start | bytes 1966088 | tf_op jit(solution)/shard_map/ppermute | solution.py:30
  307.0 34.3 %collective-permute-start.31 = (bf16[64,2560]{1,0:T(8,128)(2,1)S(1)}, bf16[64,2560]{1,0:T(8,128)(2,1)S(1)}, u32[]{:S(2)}, u32[]{:S(2)}) collective-permute-start(bf16[64,2560]{1,0:T(8,128)(2,1)S(1)} %collective-permute-done.30), channel_id=1, source_target_pairs={{8,0},{9,1},{10,2},{11,3},{12,4},{13,5},{14,6},{15,7},{16,24},{17,... | collective-permute-start | bytes 983048 | tf_op jit(solution)/shard_map/ppermute | solution.py:41
  312.2 28.2 %collective-permute-start.28 = (bf16[128,2560]{1,0:T(8,128)(2,1)S(1)}, bf16[128,2560]{1,0:T(8,128)(2,1)S(1)}, u32[]{:S(2)}, u32[]{:S(2)}) collective-permute-start(bf16[128,2560]{1,0:T(8,128)(2,1)S(1)} %pad_maximum_fusion.26), channel_id=1, source_target_pairs={{0,2},{1,5},{2,0},{3,7},{4,6},{5,1},{6,4},{7,3},{8,10},{9,13},{10,... | collective-permute-start | bytes 1966088 | tf_op jit(solution)/shard_map/ppermute | solution.py:30
  335.8 44.7 %collective-permute-start.54 = (bf16[256,2560]{1,0:T(8,128)(2,1)S(1)}, bf16[256,2560]{1,0:T(8,128)(2,1)}, u32[]{:S(2)}, u32[]{:S(2)}) collective-permute-start(bf16[256,2560]{1,0:T(8,128)(2,1)S(1)} %pad_maximum_fusion.14), channel_id=1, source_target_pairs={{0,1},{1,0},{2,3},{3,2},{4,5},{5,4},{6,7},{7,6},{8,9},{9,8},{10,11... | collective-permute-start | bytes 3932168 | tf_op jit(solution)/shard_map/ppermute | solution.py:34
  343.7 38.2 %collective-permute-start.55 = (bf16[256,2560]{1,0:T(8,128)(2,1)}, bf16[256,2560]{1,0:T(8,128)(2,1)}, u32[]{:S(2)}, u32[]{:S(2)}) collective-permute-start(bf16[256,2560]{1,0:T(8,128)(2,1)} %pad_maximum_fusion.15), channel_id=1, source_target_pairs={{0,1},{1,0},{2,3},{3,2},{4,5},{5,4},{6,7},{7,6},{8,9},{9,8},{10,11... | collective-permute-start | bytes 3932168 | tf_op jit(solution)/shard_map/ppermute | solution.py:34
  373.4 33.0 %collective-permute-start.59 = (bf16[2560,512]{1,0:T(8,128)(2,1)S(1)}, bf16[2560,512]{1,0:T(8,128)(2,1)}, u32[]{:S(2)}, u32[]{:S(2)}) collective-permute-start(bf16[2560,512]{1,0:T(8,128)(2,1)S(1)} %slice.529), channel_id=1, source_target_pairs={{0,1},{1,0},{2,3},{3,2},{4,5},{5,4},{6,7},{7,6},{8,9},{9,8},{10,11... | collective-permute-start | bytes 7864328 | tf_op jit(solution)/shard_map/ppermute | solution.py:34
  425.8 27.5 %collective-permute-start.60 = (bf16[128,2560]{1,0:T(8,128)(2,1)S(1)}, bf16[128,2560]{1,0:T(8,128)(2,1)S(1)}, u32[]{:S(2)}, u32[]{:S(2)}) collective-permute-start(bf16[128,2560]{1,0:T(8,128)(2,1)S(1)} %slice.531), channel_id=1, source_target_pairs={{0,2},{1,5},{2,0},{3,7},{4,6},{5,1},{6,4},{7,3},{8,10},{9,13},{10,... | collective-permute-start | bytes 1966088 | tf_op jit(solution)/shard_map/ppermute | solution.py:30
  426.1 27.5 %collective-permute-start.69 = (bf16[64,2560]{1,0:T(8,128)(2,1)S(1)}, bf16[64,2560]{1,0:T(8,128)(2,1)S(1)}, u32[]{:S(2)}, u32[]{:S(2)}) collective-permute-start(bf16[64,2560]{1,0:T(8,128)(2,1)S(1)} %slice.713), channel_id=1, source_target_pairs={{0,4},{1,3},{2,6},{3,1},{4,0},{5,7},{6,2},{7,5},{8,12},{9,11},{10,... | collective-permute-start | bytes 983048 | tf_op jit(solution)/shard_map/ppermute | solution.py:30
  455.6 30.3 %collective-permute-start.67 = (bf16[64,2560]{1,0:T(8,128)(2,1)S(1)}, bf16[64,2560]{1,0:T(8,128)(2,1)S(1)}, u32[]{:S(2)}, u32[]{:S(2)}) collective-permute-start(bf16[64,2560]{1,0:T(8,128)(2,1)S(1)} %fusion.34), channel_id=1, source_target_pairs={{0,16},{1,17},{2,18},{3,19},{4,20},{5,21},{6,22},{7,23},{8,24},{9,... | collective-permute-start | bytes 983048 | tf_op jit(solution)/shard_map/ppermute | solution.py:30
  490.7 101.3 %collective-permute-start.95 = (bf16[2560,768]{1,0:T(8,128)(2,1)}, bf16[2560,768]{1,0:T(8,128)(2,1)}, u32[]{:S(2)}, u32[]{:S(2)}) collective-permute-start(bf16[2560,768]{1,0:T(8,128)(2,1)} %copy-done.1), channel_id=1, source_target_pairs={{0,1},{1,0},{2,3},{3,2},{4,5},{5,4},{6,7},{7,6},{8,9},{9,8},{10,11... | collective-permute-start | bytes 11796488 | tf_op jit(solution)/shard_map/ppermute | solution.py:34
  495.9 81.7 %collective-permute-start.75 = (bf16[2560,256]{1,0:T(8,128)(2,1)}, bf16[2560,256]{1,0:T(8,128)(2,1)}, u32[]{:S(2)}, u32[]{:S(2)}) collective-permute-start(bf16[2560,256]{1,0:T(8,128)(2,1)} %slice.528), channel_id=1, source_target_pairs={{0,1},{1,0},{2,3},{3,2},{4,5},{5,4},{6,7},{7,6},{8,9},{9,8},{10,11... | collective-permute-start | bytes 3932168 | tf_op jit(solution)/shard_map/ppermute | solution.py:34
  530.9 48.1 %collective-permute-start.74 = (bf16[1024,256]{1,0:T(8,128)(2,1)}, bf16[1024,256]{1,0:T(8,128)(2,1)}, u32[]{:S(2)}, u32[]{:S(2)}) collective-permute-start(bf16[1024,256]{1,0:T(8,128)(2,1)} %get-tuple-element.170), channel_id=1, source_target_pairs={{0,1},{1,0},{2,3},{3,2},{4,5},{5,4},{6,7},{7,6},{8,9},{9,8},{10,11... | collective-permute-start | bytes 1572872 | tf_op jit(solution)/shard_map/ppermute | solution.py:34
  532.3 37.1 %collective-permute-start.107 = (bf16[4,160,384]{2,1,0:T(8,128)(2,1)}, bf16[4,160,384]{2,1,0:T(8,128)(2,1)}, u32[]{:S(2)}, u32[]{:S(2)}) collective-permute-start(bf16[4,160,384]{2,1,0:T(8,128)(2,1)} %bitcast.64), channel_id=1, source_target_pairs={{0,8},{1,9},{2,10},{3,11},{4,12},{5,13},{6,14},{7,15},{24,16},{25,... | collective-permute-start | bytes 1474568 | tf_op jit(solution)/shard_map/ppermute | solution.py:41
  572.4 28.1 %collective-permute-start.99 = (bf16[4,192,768]{2,1,0:T(8,128)(2,1)S(1)}, bf16[4,192,768]{2,1,0:T(8,128)(2,1)S(1)}, u32[]{:S(2)}, u32[]{:S(2)}) collective-permute-start(bf16[4,192,768]{2,1,0:T(8,128)(2,1)S(1)} %get-tuple-element.156), channel_id=1, source_target_pairs={{0,8},{1,9},{2,10},{3,11},{4,12},{5,13},{6,14},{7,15},{24,16},{25,... | collective-permute-start | bytes 3538952 | tf_op jit(solution)/shard_map/ppermute | solution.py:41
  577.6 48.1 %collective-permute-start.101 = (bf16[4,192,768]{2,1,0:T(8,128)(2,1)S(1)}, bf16[4,192,768]{2,1,0:T(8,128)(2,1)S(1)}, u32[]{:S(2)}, u32[]{:S(2)}) collective-permute-start(bf16[4,192,768]{2,1,0:T(8,128)(2,1)S(1)} %get-tuple-element.157), channel_id=1, source_target_pairs={{0,8},{1,9},{2,10},{3,11},{4,12},{5,13},{6,14},{7,15},{24,16},{25,... | collective-permute-start | bytes 3538952 | tf_op jit(solution)/shard_map/ppermute | solution.py:41
  592.0 71.9 %collective-permute-start.106 = (bf16[4,160,384]{2,1,0:T(8,128)(2,1)S(1)}, bf16[4,160,384]{2,1,0:T(8,128)(2,1)S(1)}, u32[]{:S(2)}, u32[]{:S(2)}) collective-permute-start(bf16[4,160,384]{2,1,0:T(8,128)(2,1)S(1)} %add_convert_fusion.3), channel_id=1, source_target_pairs={{8,16},{9,17},{10,18},{11,19},{12,20},{13,21},{14,22},{15,23},{16,... | collective-permute-start | bytes 1474568 | tf_op jit(solution)/shard_map/ppermute | solution.py:41
  593.0 35.6 %collective-permute-start.76 = (bf16[128,2560]{1,0:T(8,128)(2,1)S(1)}, bf16[128,2560]{1,0:T(8,128)(2,1)S(1)}, u32[]{:S(2)}, u32[]{:S(2)}) collective-permute-start(bf16[128,2560]{1,0:T(8,128)(2,1)S(1)} %slice.547), channel_id=1, source_target_pairs={{0,2},{1,5},{2,0},{3,7},{4,6},{5,1},{6,4},{7,3},{8,10},{9,13},{10,... | collective-permute-start | bytes 1966088 | tf_op jit(solution)/shard_map/ppermute | solution.py:30
  599.8 29.7 %collective-permute-start.84 = (bf16[128,2560]{1,0:T(8,128)(2,1)S(1)}, bf16[128,2560]{1,0:T(8,128)(2,1)S(1)}, u32[]{:S(2)}, u32[]{:S(2)}) collective-permute-start(bf16[128,2560]{1,0:T(8,128)(2,1)S(1)} %slice.559), channel_id=1, source_target_pairs={{0,2},{1,5},{2,0},{3,7},{4,6},{5,1},{6,4},{7,3},{8,10},{9,13},{10,... | collective-permute-start | bytes 1966088 | tf_op jit(solution)/shard_map/ppermute | solution.py:30
  600.5 35.8 %collective-permute-start.81 = (bf16[128,2560]{1,0:T(8,128)(2,1)S(1)}, bf16[128,2560]{1,0:T(8,128)(2,1)S(1)}, u32[]{:S(2)}, u32[]{:S(2)}) collective-permute-start(bf16[128,2560]{1,0:T(8,128)(2,1)S(1)} %slice.555), channel_id=1, source_target_pairs={{0,2},{1,5},{2,0},{3,7},{4,6},{5,1},{6,4},{7,3},{8,10},{9,13},{10,... | collective-permute-start | bytes 1966088 | tf_op jit(solution)/shard_map/ppermute | solution.py:30
  625.7 45.6 %collective-permute-start.78 = (bf16[128,2560]{1,0:T(8,128)(2,1)}, bf16[128,2560]{1,0:T(8,128)(2,1)}, u32[]{:S(2)}, u32[]{:S(2)}) collective-permute-start(bf16[128,2560]{1,0:T(8,128)(2,1)} %slice.551), channel_id=1, source_target_pairs={{0,2},{1,5},{2,0},{3,7},{4,6},{5,1},{6,4},{7,3},{8,10},{9,13},{10,... | collective-permute-start | bytes 1966088 | tf_op jit(solution)/shard_map/ppermute | solution.py:30
  629.5 34.3 %collective-permute-start.109 = (bf16[4,160,384]{2,1,0:T(8,128)(2,1)S(1)}, bf16[4,160,384]{2,1,0:T(8,128)(2,1)S(1)}, u32[]{:S(2)}, u32[]{:S(2)}) collective-permute-start(bf16[4,160,384]{2,1,0:T(8,128)(2,1)S(1)} %fusion.17), channel_id=1, source_target_pairs={{0,8},{1,9},{2,10},{3,11},{4,12},{5,13},{6,14},{7,15},{8,0},{9,1},... | collective-permute-start | bytes 1474568 | tf_op jit(solution)/shard_map/ppermute | solution.py:41
  633.2 42.4 %collective-permute-start.100 = (bf16[4,192,768]{2,1,0:T(8,128)(2,1)}, bf16[4,192,768]{2,1,0:T(8,128)(2,1)}, u32[]{:S(2)}, u32[]{:S(2)}) collective-permute-start(bf16[4,192,768]{2,1,0:T(8,128)(2,1)} %get-tuple-element.154), channel_id=1, source_target_pairs={{8,16},{9,17},{10,18},{11,19},{12,20},{13,21},{14,22},{15,23},{16,... | collective-permute-start | bytes 3538952 | tf_op jit(solution)/shard_map/ppermute | solution.py:41
  636.3 49.1 %collective-permute-start.103 = (bf16[4,192,768]{2,1,0:T(8,128)(2,1)}, bf16[4,192,768]{2,1,0:T(8,128)(2,1)}, u32[]{:S(2)}, u32[]{:S(2)}) collective-permute-start(bf16[4,192,768]{2,1,0:T(8,128)(2,1)} %fusion.14), channel_id=1, source_target_pairs={{0,8},{1,9},{2,10},{3,11},{4,12},{5,13},{6,14},{7,15},{8,0},{9,1},... | collective-permute-start | bytes 3538952 | tf_op jit(solution)/shard_map/ppermute | solution.py:41
  663.8 29.7 %collective-permute-start.96 = (bf16[128,2560]{1,0:T(8,128)(2,1)}, bf16[128,2560]{1,0:T(8,128)(2,1)}, u32[]{:S(2)}, u32[]{:S(2)}) collective-permute-start(bf16[128,2560]{1,0:T(8,128)(2,1)} %slice.567), channel_id=1, source_target_pairs={{0,2},{1,5},{2,0},{3,7},{4,6},{5,1},{6,4},{7,3},{8,10},{9,13},{10,... | collective-permute-start | bytes 1966088 | tf_op jit(solution)/shard_map/ppermute | solution.py:30
  663.9 31.6 %collective-permute-start.85 = (bf16[64,2560]{1,0:T(8,128)(2,1)}, bf16[64,2560]{1,0:T(8,128)(2,1)}, u32[]{:S(2)}, u32[]{:S(2)}) collective-permute-start(bf16[64,2560]{1,0:T(8,128)(2,1)} %slice.709), channel_id=1, source_target_pairs={{0,4},{1,3},{2,6},{3,1},{4,0},{5,7},{6,2},{7,5},{8,12},{9,11},{10,... | collective-permute-start | bytes 983048 | tf_op jit(solution)/shard_map/ppermute | solution.py:30
  671.4 40.4 %collective-permute-start.82 = (bf16[64,2560]{1,0:T(8,128)(2,1)}, bf16[64,2560]{1,0:T(8,128)(2,1)}, u32[]{:S(2)}, u32[]{:S(2)}) collective-permute-start(bf16[64,2560]{1,0:T(8,128)(2,1)} %slice.710), channel_id=1, source_target_pairs={{0,4},{1,3},{2,6},{3,1},{4,0},{5,7},{6,2},{7,5},{8,12},{9,11},{10,... | collective-permute-start | bytes 983048 | tf_op jit(solution)/shard_map/ppermute | solution.py:30
  675.6 39.7 %collective-permute-start.79 = (bf16[64,2560]{1,0:T(8,128)(2,1)}, bf16[64,2560]{1,0:T(8,128)(2,1)}, u32[]{:S(2)}, u32[]{:S(2)}) collective-permute-start(bf16[64,2560]{1,0:T(8,128)(2,1)} %slice.711), channel_id=1, source_target_pairs={{0,4},{1,3},{2,6},{3,1},{4,0},{5,7},{6,2},{7,5},{8,12},{9,11},{10,... | collective-permute-start | bytes 983048 | tf_op jit(solution)/shard_map/ppermute | solution.py:30
  685.4 41.5 %collective-permute-start.77 = (bf16[64,2560]{1,0:T(8,128)(2,1)}, bf16[64,2560]{1,0:T(8,128)(2,1)}, u32[]{:S(2)}, u32[]{:S(2)}) collective-permute-start(bf16[64,2560]{1,0:T(8,128)(2,1)} %slice.712), channel_id=1, source_target_pairs={{0,4},{1,3},{2,6},{3,1},{4,0},{5,7},{6,2},{7,5},{8,12},{9,11},{10,... | collective-permute-start | bytes 983048 | tf_op jit(solution)/shard_map/ppermute | solution.py:30
  696.5 30.5 %collective-permute-start.86 = (bf16[64,2560]{1,0:T(8,128)(2,1)S(1)}, bf16[64,2560]{1,0:T(8,128)(2,1)}, u32[]{:S(2)}, u32[]{:S(2)}) collective-permute-start(bf16[64,2560]{1,0:T(8,128)(2,1)S(1)} %fusion.25), channel_id=1, source_target_pairs={{0,24},{1,25},{2,26},{3,27},{4,28},{5,29},{6,30},{7,31},{8,16},{9,... | collective-permute-start | bytes 983048 | tf_op jit(solution)/shard_map/ppermute | solution.py:30
  706.8 120.6 %all-to-all-start.5 = ((bf16[16,160,768]{2,1,0:T(8,128)(2,1)}), bf16[16,160,768]{2,1,0:T(8,128)(2,1)}, u32[]{:S(2)}, u32[]{:S(2)}) async-start(bf16[16,160,768]{2,1,0:T(8,128)(2,1)} %bitcast.188), calls=%async_computation.5 | async-start | bytes 7864320 | tf_op jit(solution)/shard_map/all_to_all | solution.py:171
  713.1 100.5 %collective-permute-start.83 = (bf16[64,2560]{1,0:T(8,128)(2,1)S(1)}, bf16[64,2560]{1,0:T(8,128)(2,1)S(1)}, u32[]{:S(2)}, u32[]{:S(2)}) collective-permute-start(bf16[64,2560]{1,0:T(8,128)(2,1)S(1)} %fusion.26), channel_id=1, source_target_pairs={{0,16},{1,17},{2,18},{3,19},{4,20},{5,21},{6,22},{7,23},{8,24},{9,... | collective-permute-start | bytes 983048 | tf_op jit(solution)/shard_map/ppermute | solution.py:30
  716.5 97.1 %collective-permute-start.80 = (bf16[64,2560]{1,0:T(8,128)(2,1)S(1)}, bf16[64,2560]{1,0:T(8,128)(2,1)S(1)}, u32[]{:S(2)}, u32[]{:S(2)}) collective-permute-start(bf16[64,2560]{1,0:T(8,128)(2,1)S(1)} %fusion.27), channel_id=1, source_target_pairs={{0,8},{1,9},{2,10},{3,11},{4,12},{5,13},{6,14},{7,15},{8,0},{9,1},... | collective-permute-start | bytes 983048 | tf_op jit(solution)/shard_map/ppermute | solution.py:30
  719.4 100.0 %collective-permute-start.98 = (f32[64,2560]{1,0:T(8,128)S(1)}, f32[64,2560]{1,0:T(8,128)S(1)}, u32[]{:S(2)}, u32[]{:S(2)}) collective-permute-start(f32[64,2560]{1,0:T(8,128)S(1)} %fusion.23), channel_id=1, source_target_pairs={{0,1},{1,0},{2,3},{3,2},{4,5},{5,4},{6,7},{7,6},{8,9},{9,8},{10,11... | collective-permute-start | bytes 1966088 | tf_op jit(solution)/shard_map/ppermute | solution.py:34
  726.9 89.6 %collective-permute-start.110 = (bf16[2,160,384]{2,1,0:T(8,128)(2,1)S(1)}, bf16[2,160,384]{2,1,0:T(8,128)(2,1)S(1)}, u32[]{:S(2)}, u32[]{:S(2)}) collective-permute-start(bf16[2,160,384]{2,1,0:T(8,128)(2,1)S(1)} %constant_dynamic-slice_fusion.6), channel_id=1, source_target_pairs={{0,1},{1,0},{2,3},{3,2},{4,5},{5,4},{6,7},{7,6},{8,9},{9,8},{10,11... | collective-permute-start | bytes 737288 | tf_op jit(solution)/shard_map/ppermute | solution.py:34
  (139 other events, 1651.3 us)

commit v4 on v3

--- a/solution.py
+++ b/solution.py
@@ -203,7 +203,7 @@
     )(gain, gate, value, contract)
 
 
-def unpack_wide(grads, gain, gate, value, gate_out, value_out, contract_out, sums):
+def unpack_wide(grads, turned, gain, gate, value, gate_out, value_out, contract_out, sums):
     lanes = gate.shape[1] // grads.shape[0]
 
     @pl.when(pl.program_id(0) == 0)
@@ -217,14 +217,14 @@
         value_hat = grads[i, :, lanes : 2 * lanes].astype(F32)
         gate_out[:, at] = gate_hat * gain[...]
         value_out[:, at] = value_hat * gain[...]
-        contract_out[:, at] = grads[i, :, 2 * lanes :].astype(F32)
+        contract_out[:, at] = turned[i].astype(F32)
         both = gate_hat * gate[:, at].astype(F32) + value_hat * value[:, at].astype(F32)
         for start in range(0, lanes, LANES):
             total = total + both[:, start : start + LANES]
     sums[...] = total
 
 
-def unpacked_wide(grads, gain, gate, value, lanes):
+def unpacked_wide(grads, turned, gain, gate, value, lanes):
     part, hidden = gate.shape
     chips = hidden // lanes
     at_once = 3 if chips % 3 == 0 else 1
@@ -239,7 +239,8 @@
         ],
         grid=(chips // at_once,),
         in_specs=[
-            pl.BlockSpec((at_once, part, 3 * lanes), lambda j: (j, 0, 0)),
+            pl.BlockSpec((at_once, part, 2 * lanes), lambda j: (j, 0, 0)),
+            pl.BlockSpec((at_once, part, lanes), lambda j: (j, 0, 0)),
             pl.BlockSpec((part, 1), lambda j: (0, 0)),
             column,
             column,
@@ -251,7 +252,7 @@
             pl.BlockSpec((part, LANES), lambda j: (0, 0)),
         ],
         compiler_params=params(),
-    )(grads, gain, gate, value)
+    )(grads, turned, gain, gate, value)
 
 
 HALVES = (((0, 1, 2), (4, 5, 3)), ((6, 7, None), (8, 9, None)))
@@ -812,23 +813,19 @@
         + s2 * back2
         - r * (s2 * s2 * s2) * jnp.mean(back2 * r, axis=-1, keepdims=True)
     )
-    dq = near_gathered(slabs(dr.astype(BF16)))
-
-    wide_grad = jnp.concatenate(
-        lax.optimization_barrier(
-            (
-                dot(second, dge, ((0,), (0,))).astype(BF16),
-                dot(given_out, zb, ((0,), (0,))).astype(BF16),
-            )
-        ),
-        axis=1,
-    )
+    wide_grad, turned_grad = (
+        dot(second, dge, ((0,), (0,))).astype(BF16).reshape(count, part, 2 * lanes),
+        dot(given_out, zb, ((0,), (0,))).astype(BF16).reshape(count, part, lanes),
+    )
+    wide_grad, turned_grad = lax.optimization_barrier((wide_grad, turned_grad))
+    turned_grad = all_to_all(turned_grad)
+    dq = after(near_gathered(slabs(dr.astype(BF16))), turned_grad)
     dq, wide_grad = lax.optimization_barrier((dq, wide_grad))
     (out_sum,) = scattered((grouped(after(zb, dq)), c_both))
     out_half = (r + out_sum).astype(BF16)
-    wide_grad = all_to_all(wide_grad.reshape(count, part, 3 * lanes))
+    wide_grad = all_to_all(wide_grad)
     gate_grad_out, value_grad_out, contract_grad_out, gain2_part = unpacked_wide(
-        wide_grad, gain2, expand_gate, expand_value, lanes
+        wide_grad, turned_grad, gain2, expand_gate, expand_value, lanes
     )
 
     dob = dot(dq, weight_out, ((1,), (0,)))

time: 850 us -> 833 us (0.980)
  waiting for transfers between devices: 368 us -> 341 us
    ppermute x52, waiting for transfers between devices: 220 us -> 144 us  [xor_send(): return lax.ppermute(value, BOTH, pairs)]
    all_to_all x2 -> x3, waiting for transfers between devices: 0.01 us -> 57.4 us  [all_to_all(): return lax.all_to_all(pieces, 'seq', 0, 0, tiled=True)]
    unnamed x162 -> x172, local copies, waits for them, and re-layouts: 34.3 us -> 38.3 us
  transfers between devices with their start and end apart: 118 -> 119, of which waited for: 35 -> 38; matrix products, arithmetic and copies ran while one was open for 23% -> 24% of each run, Pallas kernels for 6% -> 7%
where the time goes in v4:
time: 833 us; the launch traced here: 816 us
  waiting for transfers between devices  341 us (41%)
  starting transfers between devices  189 us (23%)
  matrix products  76.6 us (9%)
  local copies, waits for them, and re-layouts  71.8 us (9%)
  other arithmetic  71.7 us (9%)
  Pallas kernels  62.1 us (7%)
    ppermute x52, waiting for transfers between devices, xor_send(): return lax.ppermute(value, BOTH, pairs)  144 us
    ppermute x30, waiting for transfers between devices, row_send(): return lax.ppermute(value, BOTH, pairs)  125 us
    dot_general x25, matrix products, dot(): lax.dot_general(left, right, (over, ((), ())), preferred_element_type=F32)  76.6 us
    ppermute x30, starting transfers between devices, row_send(): return lax.ppermute(value, BOTH, pairs)  66.1 us
    ppermute x52, starting transfers between devices, xor_send(): return lax.ppermute(value, BOTH, pairs)  61.7 us
    all_to_all x3, waiting for transfers between devices, all_to_all(): return lax.all_to_all(pieces, 'seq', 0, 0, tiled=True)  57.4 us
    unnamed x172, local copies, waits for them, and re-layouts  38.3 us
    pallas_call x6, Pallas kernels, in_vmem(): pl.pallas_call(kernel, out_shape=[jax.ShapeDtypeStruct(shape, dtype) for...  28.8 us
  transfers between devices with their start and end apart: 119, of which 38 were waited for; matrix products, arithmetic and copies ran while one was open for 24% of the time, Pallas kernels for 7%

profile of v4, /device:TPU:5, one launch (start us, length us, event | category | flops | bytes accessed | tf_op | source)
XLA Modules:
  0.0 816.3 jit_solution(12472516584149969254)
XLA Ops:
  17.6 7.6 collective-permute-done.1
  28.9 4.2 all-to-all-start
  35.5 10.6 %shard_map.283 = bf16[16,160,768]{2,1,0:T(8,128)(2,1)} custom-call(f32[160,1]{1,0:T(8,128)} %copy.54.gain, bf16[160,3840]{1,0:T(8,128)(2,1)} %gate.3, bf16[160,3840]{1,0:T(8,128)(2,1)} %value.3, bf16[160,3840]{1,0:T(8,128)(2,1)} %bitcast.208), custom_call_target="tpu_custom_call" | custom-call | tf_op jit(solution)/shard_map/pallas_call | solution.py:191
  48.0 4.4 all-to-all-start.1
  54.6 4.1 pad_maximum_fusion.3
  65.5 20.4 %collective-permute-done.38 = bf16[64,2560]{1,0:T(8,128)(2,1)S(1)} collective-permute-done((bf16[64,2560]{1,0:T(8,128)(2,1)S(1)}, bf16[64,2560]{1,0:T(8,128)(2,1)S(1)}, u32[]{:S(2)}, u32[]{:S(2)}) %collective-permute-start.38) | collective-permute-done | bytes 327712 | tf_op jit(solution)/shard_map/ppermute | solution.py:41
  97.6 5.8 collective-permute-done.40
  107.3 4.1 collective-permute-done.44
  112.9 13.4 %collective-permute-done.7 = bf16[4,192,768]{2,1,0:T(8,128)(2,1)S(1)} collective-permute-done((bf16[4,192,768]{2,1,0:T(8,128)(2,1)S(1)}, bf16[4,192,768]{2,1,0:T(8,128)(2,1)S(1)}, u32[]{:S(2)}, u32[]{:S(2)}) %collective-permute-start.7) | collective-permute-done | bytes 1179680 | tf_op jit(solution)/shard_map/ppermute | solution.py:41
  141.8 16.9 %collective-permute-done.8 = bf16[4,192,768]{2,1,0:T(8,128)(2,1)S(1)} collective-permute-done((bf16[4,192,768]{2,1,0:T(8,128)(2,1)S(1)}, bf16[4,192,768]{2,1,0:T(8,128)(2,1)S(1)}, u32[]{:S(2)}, u32[]{:S(2)}) %collective-permute-start.8) | collective-permute-done | bytes 1179680 | tf_op jit(solution)/shard_map/ppermute | solution.py:41
  165.5 3.9 collective-permute-start.9
  176.2 7.9 collective-permute-done.19
  184.2 11.4 %collective-permute-done.20 = bf16[4,160,384]{2,1,0:T(8,128)(2,1)S(1)} collective-permute-done((bf16[4,160,384]{2,1,0:T(8,128)(2,1)S(1)}, bf16[4,160,384]{2,1,0:T(8,128)(2,1)S(1)}, u32[]{:S(2)}, u32[]{:S(2)}) %collective-permute-start.20) | collective-permute-done | bytes 491552 | tf_op jit(solution)/shard_map/ppermute | solution.py:41
  208.6 6.8 shard_map.281
  219.8 4.8 all-to-all-start.2
  243.4 18.5 %collective-permute-done.22 = bf16[128,2560]{1,0:T(8,128)(2,1)S(1)} collective-permute-done((bf16[128,2560]{1,0:T(8,128)(2,1)S(1)}, bf16[128,2560]{1,0:T(8,128)(2,1)S(1)}, u32[]{:S(2)}, u32[]{:S(2)}) %collective-permute-start.22) | collective-permute-done | bytes 655392 | tf_op jit(solution)/shard_map/ppermute | solution.py:30
  266.8 14.4 %collective-permute-done.23 = bf16[64,2560]{1,0:T(8,128)(2,1)S(1)} collective-permute-done((bf16[64,2560]{1,0:T(8,128)(2,1)S(1)}, bf16[64,2560]{1,0:T(8,128)(2,1)S(1)}, u32[]{:S(2)}, u32[]{:S(2)}) %collective-permute-start.23) | collective-permute-done | bytes 327712 | tf_op jit(solution)/shard_map/ppermute | solution.py:30
  284.6 10.0 %collective-permute-done.24 = bf16[64,2560]{1,0:T(8,128)(2,1)S(1)} collective-permute-done((bf16[64,2560]{1,0:T(8,128)(2,1)S(1)}, bf16[64,2560]{1,0:T(8,128)(2,1)S(1)}, u32[]{:S(2)}, u32[]{:S(2)}) %collective-permute-start.24) | collective-permute-done | bytes 327712 | tf_op jit(solution)/shard_map/ppermute | solution.py:30
  294.6 10.9 %collective-permute-start.25 = (bf16[128,2560]{1,0:T(8,128)(2,1)S(1)}, bf16[128,2560]{1,0:T(8,128)(2,1)S(1)}, u32[]{:S(2)}, u32[]{:S(2)}) collective-permute-start(bf16[128,2560]{1,0:T(8,128)(2,1)S(1)} %pad_maximum_fusion.24), channel_id=1, source_target_pairs={{0,2},{1,5},{2,0},{3,7},{4,6},{5,1},{6,4},{7,3},{8,10},{9,13},{10,... | collective-permute-start | bytes 1966088 | tf_op jit(solution)/shard_map/ppermute | solution.py:30
  313.2 22.4 %collective-permute-done.34 = bf16[64,2560]{1,0:T(8,128)(2,1)S(1)} collective-permute-done((bf16[64,2560]{1,0:T(8,128)(2,1)S(1)}, bf16[64,2560]{1,0:T(8,128)(2,1)S(1)}, u32[]{:S(2)}, u32[]{:S(2)}) %collective-permute-start.34) | collective-permute-done | bytes 327712 | tf_op jit(solution)/shard_map/ppermute | solution.py:41
  351.0 7.5 collective-permute-done.33
  361.1 8.7 %fusion.138.dz = f32[2048,256]{1,0:T(8,128)} fusion(bf16[2048,2560]{1,0:T(8,128)(2,1)} %constant_dynamic-update-slice_fusion, bf16[2560,768]{1,0:T(8,128)(2,1)} %bitcast.42), kind=kOutput, calls=%fused_computation.410 | convolution fusion | flops 2684354560 | bytes 13893632 | tf_op jit(solution)/shard_map/dot_general | solution.py:638
  373.6 6.2 collective-permute-done.53
  388.9 9.4 %fusion.140.ge = f32[2048,512]{1,0:T(8,128)} fusion(bf16[2048,2560]{1,0:T(8,128)(2,1)S(1)} %constant_dynamic-update-slice_fusion.16, bf16[2560,768]{1,0:T(8,128)(2,1)} %bitcast.42), kind=kOutput, calls=%fused_computation.412 | convolution fusion | flops 5368709120 | bytes 17301504 | tf_op jit(solution)/shard_map/dot_general | solution.py:638
  398.3 6.4 shard_map.284
  430.1 12.4 %collective-permute-done.62 = bf16[128,2560]{1,0:T(8,128)(2,1)S(1)} collective-permute-done((bf16[128,2560]{1,0:T(8,128)(2,1)S(1)}, bf16[128,2560]{1,0:T(8,128)(2,1)S(1)}, u32[]{:S(2)}, u32[]{:S(2)}) %collective-permute-start.62) | collective-permute-done | bytes 655392 | tf_op jit(solution)/shard_map/ppermute | solution.py:30
  442.8 10.6 %collective-permute-done.60 = bf16[128,2560]{1,0:T(8,128)(2,1)S(1)} collective-permute-done((bf16[128,2560]{1,0:T(8,128)(2,1)S(1)}, bf16[128,2560]{1,0:T(8,128)(2,1)S(1)}, u32[]{:S(2)}, u32[]{:S(2)}) %collective-permute-start.60) | collective-permute-done | bytes 655392 | tf_op jit(solution)/shard_map/ppermute | solution.py:30
  455.7 4.9 collective-permute-start.67
  461.6 24.3 %collective-permute-done.67 = bf16[64,2560]{1,0:T(8,128)(2,1)S(1)} collective-permute-done((bf16[64,2560]{1,0:T(8,128)(2,1)S(1)}, bf16[64,2560]{1,0:T(8,128)(2,1)S(1)}, u32[]{:S(2)}, u32[]{:S(2)}) %collective-permute-start.67) | collective-permute-done | bytes 327712 | tf_op jit(solution)/shard_map/ppermute | solution.py:30
  489.6 7.2 convolution_convert_fusion.1
  498.9 4.2 convolution_convert_fusion.7
  503.1 4.2 all-to-all-start.3
  516.2 4.1 pad_maximum_fusion.4
  520.4 15.6 %all-to-all-done.3.turned = bf16[16,160,256]{2,1,0:T(8,128)(2,1)S(1)} async-done(((bf16[16,160,256]{2,1,0:T(8,128)(2,1)}), bf16[16,160,256]{2,1,0:T(8,128)(2,1)S(1)}, u32[]{:S(2)}, u32[]{:S(2)}) %all-to-all-start.3) | async-done | bytes 1310752 | tf_op jit(solution)/shard_map/all_to_all | solution.py:171
  536.0 5.2 fusion.153.dob
  541.2 6.2 shard_map.285
  558.8 4.6 collective-permute-start.107
  564.1 5.0 shard_map.286
  578.0 4.0 shard_map.287
  601.0 4.1 collective-permute-start.99
  630.6 6.5 collective-permute-done.84
  639.6 14.7 %collective-permute-done.101 = bf16[4,192,768]{2,1,0:T(8,128)(2,1)S(1)} collective-permute-done((bf16[4,192,768]{2,1,0:T(8,128)(2,1)S(1)}, bf16[4,192,768]{2,1,0:T(8,128)(2,1)S(1)}, u32[]{:S(2)}, u32[]{:S(2)}) %collective-permute-start.101) | collective-permute-done | bytes 1179680 | tf_op jit(solution)/shard_map/ppermute | solution.py:41
  665.2 24.0 %collective-permute-start.103 = (bf16[4,192,768]{2,1,0:T(8,128)(2,1)}, bf16[4,192,768]{2,1,0:T(8,128)(2,1)}, u32[]{:S(2)}, u32[]{:S(2)}) collective-permute-start(bf16[4,192,768]{2,1,0:T(8,128)(2,1)} %fusion.14), channel_id=1, source_target_pairs={{0,8},{1,9},{2,10},{3,11},{4,12},{5,13},{6,14},{7,15},{8,0},{9,1},... | collective-permute-start | bytes 3538952 | tf_op jit(solution)/shard_map/ppermute | solution.py:41
  700.8 12.0 %collective-permute-done.103 = bf16[4,192,768]{2,1,0:T(8,128)(2,1)} collective-permute-done((bf16[4,192,768]{2,1,0:T(8,128)(2,1)}, bf16[4,192,768]{2,1,0:T(8,128)(2,1)}, u32[]{:S(2)}, u32[]{:S(2)}) %collective-permute-start.103) | collective-permute-done | bytes 1179680 | tf_op jit(solution)/shard_map/ppermute | solution.py:41
  727.9 7.5 all-to-all-done.4
  736.5 4.7 all-to-all-start.6
  752.3 41.8 %all-to-all-done.6.grads = bf16[16,160,512]{2,1,0:T(8,128)(2,1)S(1)} async-done(((bf16[16,160,512]{2,1,0:T(8,128)(2,1)}), bf16[16,160,512]{2,1,0:T(8,128)(2,1)S(1)}, u32[]{:S(2)}, u32[]{:S(2)}) %all-to-all-start.6) | async-done | bytes 2621472 | tf_op jit(solution)/shard_map/all_to_all | solution.py:171
  795.6 7.6 shard_map.290
  (608 shorter events, 336.2 us)
Async XLA Ops:
  26.4 28.1 %collective-permute-start.2 = (bf16[256,2560]{1,0:T(8,128)(2,1)}, bf16[256,2560]{1,0:T(8,128)(2,1)}, u32[]{:S(2)}, u32[]{:S(2)}) collective-permute-start(bf16[256,2560]{1,0:T(8,128)(2,1)} %pad_maximum_fusion.8), channel_id=1, source_target_pairs={{0,1},{1,0},{2,3},{3,2},{4,5},{5,4},{6,7},{7,6},{8,9},{9,8},{10,11... | collective-permute-start | bytes 3932168 | tf_op jit(solution)/shard_map/ppermute | solution.py:34
  48.0 110.9 %all-to-all-start.1 = ((bf16[4,160,384]{2,1,0:T(8,128)(2,1)}), bf16[4,160,384]{2,1,0:T(8,128)(2,1)}, u32[]{:S(2)}, u32[]{:S(2)}) async-start(bf16[4,160,384]{2,1,0:T(8,128)(2,1)} %pad_maximum_fusion.37), calls=%async_computation.1 | async-start | bytes 983040 | tf_op jit(solution)/shard_map/all_to_all | solution.py:134
  52.4 36.0 %collective-permute-start.4 = (bf16[4,192,768]{2,1,0:T(8,128)(2,1)S(1)}, bf16[4,192,768]{2,1,0:T(8,128)(2,1)S(1)}, u32[]{:S(2)}, u32[]{:S(2)}) collective-permute-start(bf16[4,192,768]{2,1,0:T(8,128)(2,1)S(1)} %all-to-all-done), channel_id=1, source_target_pairs={{0,8},{1,9},{2,10},{3,11},{4,12},{5,13},{6,14},{7,15},{8,0},{9,1},... | collective-permute-start | bytes 3538952 | tf_op jit(solution)/shard_map/ppermute | solution.py:41
  53.7 37.8 %collective-permute-start.6 = (bf16[4,192,768]{2,1,0:T(8,128)(2,1)S(1)}, bf16[4,192,768]{2,1,0:T(8,128)(2,1)S(1)}, u32[]{:S(2)}, u32[]{:S(2)}) collective-permute-start(bf16[4,192,768]{2,1,0:T(8,128)(2,1)S(1)} %all-to-all-done), channel_id=1, source_target_pairs={{8,16},{9,17},{10,18},{11,19},{12,20},{13,21},{14,22},{15,23},{16,... | collective-permute-start | bytes 3538952 | tf_op jit(solution)/shard_map/ppermute | solution.py:41
  59.9 26.0 %collective-permute-start.38 = (bf16[64,2560]{1,0:T(8,128)(2,1)S(1)}, bf16[64,2560]{1,0:T(8,128)(2,1)S(1)}, u32[]{:S(2)}, u32[]{:S(2)}) collective-permute-start(bf16[64,2560]{1,0:T(8,128)(2,1)S(1)} %constant_dynamic-slice_fusion.20), channel_id=1, source_target_pairs={{0,8},{1,9},{2,10},{3,11},{4,12},{5,13},{6,14},{7,15},{8,0},{9,1},... | collective-permute-start | bytes 983048 | tf_op jit(solution)/shard_map/ppermute | solution.py:41
  65.1 28.8 %collective-permute-start.37 = (bf16[128,2560]{1,0:T(8,128)(2,1)S(1)}, bf16[128,2560]{1,0:T(8,128)(2,1)S(1)}, u32[]{:S(2)}, u32[]{:S(2)}) collective-permute-start(bf16[128,2560]{1,0:T(8,128)(2,1)S(1)} %pad_maximum_fusion.28), channel_id=1, source_target_pairs={{0,2},{1,5},{2,0},{3,7},{4,6},{5,1},{6,4},{7,3},{8,10},{9,13},{10,... | collective-permute-start | bytes 1966088 | tf_op jit(solution)/shard_map/ppermute | solution.py:30
  92.2 34.1 %collective-permute-start.7 = (bf16[4,192,768]{2,1,0:T(8,128)(2,1)S(1)}, bf16[4,192,768]{2,1,0:T(8,128)(2,1)S(1)}, u32[]{:S(2)}, u32[]{:S(2)}) collective-permute-start(bf16[4,192,768]{2,1,0:T(8,128)(2,1)S(1)} %collective-permute-done.6), channel_id=1, source_target_pairs={{8,0},{9,1},{10,2},{11,3},{12,4},{13,5},{14,6},{15,7},{16,24},{17,... | collective-permute-start | bytes 3538952 | tf_op jit(solution)/shard_map/ppermute | solution.py:41
  93.9 39.4 %collective-permute-start.46 = (bf16[64,2560]{1,0:T(8,128)(2,1)S(1)}, bf16[64,2560]{1,0:T(8,128)(2,1)S(1)}, u32[]{:S(2)}, u32[]{:S(2)}) collective-permute-start(bf16[64,2560]{1,0:T(8,128)(2,1)S(1)} %collective-permute-done.41), channel_id=1, source_target_pairs={{8,0},{9,1},{10,2},{11,3},{12,4},{13,5},{14,6},{15,7},{16,24},{17,... | collective-permute-start | bytes 983048 | tf_op jit(solution)/shard_map/ppermute | solution.py:41
  126.7 32.0 %collective-permute-start.8 = (bf16[4,192,768]{2,1,0:T(8,128)(2,1)S(1)}, bf16[4,192,768]{2,1,0:T(8,128)(2,1)S(1)}, u32[]{:S(2)}, u32[]{:S(2)}) collective-permute-start(bf16[4,192,768]{2,1,0:T(8,128)(2,1)S(1)} %collective-permute-done.5), channel_id=1, source_target_pairs={{8,0},{9,1},{10,2},{11,3},{12,4},{13,5},{14,6},{15,7},{16,24},{17,... | collective-permute-start | bytes 3538952 | tf_op jit(solution)/shard_map/ppermute | solution.py:41
  141.4 90.2 %collective-permute-start.48 = (bf16[128,2560]{1,0:T(8,128)(2,1)}, bf16[128,2560]{1,0:T(8,128)(2,1)}, u32[]{:S(2)}, u32[]{:S(2)}) collective-permute-start(bf16[128,2560]{1,0:T(8,128)(2,1)} %pad_maximum_fusion.31), channel_id=1, source_target_pairs={{0,2},{1,5},{2,0},{3,7},{4,6},{5,1},{6,4},{7,3},{8,10},{9,13},{10,... | collective-permute-start | bytes 1966088 | tf_op jit(solution)/shard_map/ppermute | solution.py:30
  165.5 36.7 %collective-permute-start.9 = (f32[8,384]{1,0:T(8,128)}, f32[8,384]{1,0:T(8,128)}, u32[]{:S(2)}, u32[]{:S(2)}) collective-permute-start(f32[8,384]{1,0:T(8,128)} %constant_dynamic-slice_fusion.29), channel_id=1, source_target_pairs={{0,8},{1,9},{2,10},{3,11},{4,12},{5,13},{6,14},{7,15},{8,16},{9,17... | collective-permute-start | bytes 36872 | tf_op jit(solution)/shard_map/ppermute | solution.py:145
  198.2 37.1 %collective-permute-start.21 = (bf16[2560,384]{1,0:T(8,128)(2,1)S(1)}, bf16[2560,384]{1,0:T(8,128)(2,1)}, u32[]{:S(2)}, u32[]{:S(2)}) collective-permute-start(bf16[2560,384]{1,0:T(8,128)(2,1)S(1)} %pad_maximum_fusion.6), channel_id=1, source_target_pairs={{0,1},{1,0},{2,3},{3,2},{4,5},{5,4},{6,7},{7,6},{8,9},{9,8},{10,11... | collective-permute-start | bytes 5898248 | tf_op jit(solution)/shard_map/ppermute | solution.py:34
  219.8 141.3 %all-to-all-start.2 = ((bf16[16,160,768]{2,1,0:T(8,128)(2,1)}), bf16[16,160,768]{2,1,0:T(8,128)(2,1)}, u32[]{:S(2)}, u32[]{:S(2)}) async-start(bf16[16,160,768]{2,1,0:T(8,128)(2,1)} %shard_map.283), calls=%async_computation.2 | async-start | bytes 7864320 | tf_op jit(solution)/shard_map/all_to_all | solution.py:171
  226.4 39.2 %collective-permute-start.51 = (bf16[256,2560]{1,0:T(8,128)(2,1)}, bf16[256,2560]{1,0:T(8,128)(2,1)S(1)}, u32[]{:S(2)}, u32[]{:S(2)}) collective-permute-start(bf16[256,2560]{1,0:T(8,128)(2,1)} %pad_maximum_fusion.11), channel_id=1, source_target_pairs={{0,1},{1,0},{2,3},{3,2},{4,5},{5,4},{6,7},{7,6},{8,9},{9,8},{10,11... | collective-permute-start | bytes 3932168 | tf_op jit(solution)/shard_map/ppermute | solution.py:34
  234.9 47.5 %collective-permute-start.52 = (bf16[256,2560]{1,0:T(8,128)(2,1)S(1)}, bf16[256,2560]{1,0:T(8,128)(2,1)S(1)}, u32[]{:S(2)}, u32[]{:S(2)}) collective-permute-start(bf16[256,2560]{1,0:T(8,128)(2,1)S(1)} %pad_maximum_fusion.12), channel_id=1, source_target_pairs={{0,1},{1,0},{2,3},{3,2},{4,5},{5,4},{6,7},{7,6},{8,9},{9,8},{10,11... | collective-permute-start | bytes 3932168 | tf_op jit(solution)/shard_map/ppermute | solution.py:34
  294.6 41.1 %collective-permute-start.25 = (bf16[128,2560]{1,0:T(8,128)(2,1)S(1)}, bf16[128,2560]{1,0:T(8,128)(2,1)S(1)}, u32[]{:S(2)}, u32[]{:S(2)}) collective-permute-start(bf16[128,2560]{1,0:T(8,128)(2,1)S(1)} %pad_maximum_fusion.24), channel_id=1, source_target_pairs={{0,2},{1,5},{2,0},{3,7},{4,6},{5,1},{6,4},{7,3},{8,10},{9,13},{10,... | collective-permute-start | bytes 1966088 | tf_op jit(solution)/shard_map/ppermute | solution.py:30
  307.0 34.3 %collective-permute-start.31 = (bf16[64,2560]{1,0:T(8,128)(2,1)S(1)}, bf16[64,2560]{1,0:T(8,128)(2,1)S(1)}, u32[]{:S(2)}, u32[]{:S(2)}) collective-permute-start(bf16[64,2560]{1,0:T(8,128)(2,1)S(1)} %collective-permute-done.30), channel_id=1, source_target_pairs={{8,0},{9,1},{10,2},{11,3},{12,4},{13,5},{14,6},{15,7},{16,24},{17,... | collective-permute-start | bytes 983048 | tf_op jit(solution)/shard_map/ppermute | solution.py:41
  309.1 26.4 %collective-permute-start.34 = (bf16[64,2560]{1,0:T(8,128)(2,1)S(1)}, bf16[64,2560]{1,0:T(8,128)(2,1)S(1)}, u32[]{:S(2)}, u32[]{:S(2)}) collective-permute-start(bf16[64,2560]{1,0:T(8,128)(2,1)S(1)} %collective-permute-done.29), channel_id=1, source_target_pairs={{8,0},{9,1},{10,2},{11,3},{12,4},{13,5},{14,6},{15,7},{16,24},{17,... | collective-permute-start | bytes 983048 | tf_op jit(solution)/shard_map/ppermute | solution.py:41
  312.2 28.2 %collective-permute-start.28 = (bf16[128,2560]{1,0:T(8,128)(2,1)S(1)}, bf16[128,2560]{1,0:T(8,128)(2,1)S(1)}, u32[]{:S(2)}, u32[]{:S(2)}) collective-permute-start(bf16[128,2560]{1,0:T(8,128)(2,1)S(1)} %pad_maximum_fusion.25), channel_id=1, source_target_pairs={{0,2},{1,5},{2,0},{3,7},{4,6},{5,1},{6,4},{7,3},{8,10},{9,13},{10,... | collective-permute-start | bytes 1966088 | tf_op jit(solution)/shard_map/ppermute | solution.py:30
  335.8 44.8 %collective-permute-start.54 = (bf16[256,2560]{1,0:T(8,128)(2,1)S(1)}, bf16[256,2560]{1,0:T(8,128)(2,1)}, u32[]{:S(2)}, u32[]{:S(2)}) collective-permute-start(bf16[256,2560]{1,0:T(8,128)(2,1)S(1)} %pad_maximum_fusion.13), channel_id=1, source_target_pairs={{0,1},{1,0},{2,3},{3,2},{4,5},{5,4},{6,7},{7,6},{8,9},{9,8},{10,11... | collective-permute-start | bytes 3932168 | tf_op jit(solution)/shard_map/ppermute | solution.py:34
  343.8 38.2 %collective-permute-start.55 = (bf16[256,2560]{1,0:T(8,128)(2,1)}, bf16[256,2560]{1,0:T(8,128)(2,1)}, u32[]{:S(2)}, u32[]{:S(2)}) collective-permute-start(bf16[256,2560]{1,0:T(8,128)(2,1)} %pad_maximum_fusion.14), channel_id=1, source_target_pairs={{0,1},{1,0},{2,3},{3,2},{4,5},{5,4},{6,7},{7,6},{8,9},{9,8},{10,11... | collective-permute-start | bytes 3932168 | tf_op jit(solution)/shard_map/ppermute | solution.py:34
  373.5 33.0 %collective-permute-start.59 = (bf16[2560,512]{1,0:T(8,128)(2,1)S(1)}, bf16[2560,512]{1,0:T(8,128)(2,1)}, u32[]{:S(2)}, u32[]{:S(2)}) collective-permute-start(bf16[2560,512]{1,0:T(8,128)(2,1)S(1)} %slice.529), channel_id=1, source_target_pairs={{0,1},{1,0},{2,3},{3,2},{4,5},{5,4},{6,7},{7,6},{8,9},{9,8},{10,11... | collective-permute-start | bytes 7864328 | tf_op jit(solution)/shard_map/ppermute | solution.py:34
  426.1 27.3 %collective-permute-start.60 = (bf16[128,2560]{1,0:T(8,128)(2,1)S(1)}, bf16[128,2560]{1,0:T(8,128)(2,1)S(1)}, u32[]{:S(2)}, u32[]{:S(2)}) collective-permute-start(bf16[128,2560]{1,0:T(8,128)(2,1)S(1)} %slice.531), channel_id=1, source_target_pairs={{0,2},{1,5},{2,0},{3,7},{4,6},{5,1},{6,4},{7,3},{8,10},{9,13},{10,... | collective-permute-start | bytes 1966088 | tf_op jit(solution)/shard_map/ppermute | solution.py:30
  426.4 27.3 %collective-permute-start.69 = (bf16[64,2560]{1,0:T(8,128)(2,1)S(1)}, bf16[64,2560]{1,0:T(8,128)(2,1)S(1)}, u32[]{:S(2)}, u32[]{:S(2)}) collective-permute-start(bf16[64,2560]{1,0:T(8,128)(2,1)S(1)} %slice.713), channel_id=1, source_target_pairs={{0,4},{1,3},{2,6},{3,1},{4,0},{5,7},{6,2},{7,5},{8,12},{9,11},{10,... | collective-permute-start | bytes 983048 | tf_op jit(solution)/shard_map/ppermute | solution.py:30
  429.8 25.8 %collective-permute-start.66 = (bf16[64,2560]{1,0:T(8,128)(2,1)S(1)}, bf16[64,2560]{1,0:T(8,128)(2,1)S(1)}, u32[]{:S(2)}, u32[]{:S(2)}) collective-permute-start(bf16[64,2560]{1,0:T(8,128)(2,1)S(1)} %slice.714), channel_id=1, source_target_pairs={{0,4},{1,3},{2,6},{3,1},{4,0},{5,7},{6,2},{7,5},{8,12},{9,11},{10,... | collective-permute-start | bytes 983048 | tf_op jit(solution)/shard_map/ppermute | solution.py:30
  455.7 30.3 %collective-permute-start.67 = (bf16[64,2560]{1,0:T(8,128)(2,1)S(1)}, bf16[64,2560]{1,0:T(8,128)(2,1)S(1)}, u32[]{:S(2)}, u32[]{:S(2)}) collective-permute-start(bf16[64,2560]{1,0:T(8,128)(2,1)S(1)} %fusion.34), channel_id=1, source_target_pairs={{0,16},{1,17},{2,18},{3,19},{4,20},{5,21},{6,22},{7,23},{8,24},{9,... | collective-permute-start | bytes 983048 | tf_op jit(solution)/shard_map/ppermute | solution.py:30
  460.7 25.2 %collective-permute-start.64 = (bf16[64,2560]{1,0:T(8,128)(2,1)S(1)}, bf16[64,2560]{1,0:T(8,128)(2,1)S(1)}, u32[]{:S(2)}, u32[]{:S(2)}) collective-permute-start(bf16[64,2560]{1,0:T(8,128)(2,1)S(1)} %fusion.35), channel_id=1, source_target_pairs={{0,8},{1,9},{2,10},{3,11},{4,12},{5,13},{6,14},{7,15},{8,0},{9,1},... | collective-permute-start | bytes 983048 | tf_op jit(solution)/shard_map/ppermute | solution.py:30
  503.1 32.9 %all-to-all-start.3 = ((bf16[16,160,256]{2,1,0:T(8,128)(2,1)}), bf16[16,160,256]{2,1,0:T(8,128)(2,1)S(1)}, u32[]{:S(2)}, u32[]{:S(2)}) async-start(bf16[16,160,256]{2,1,0:T(8,128)(2,1)} %bitcast.207), calls=%async_computation.3 | async-start | bytes 2621440 | tf_op jit(solution)/shard_map/all_to_all | solution.py:171
  510.2 109.0 %collective-permute-start.95 = (bf16[2560,768]{1,0:T(8,128)(2,1)}, bf16[2560,768]{1,0:T(8,128)(2,1)}, u32[]{:S(2)}, u32[]{:S(2)}) collective-permute-start(bf16[2560,768]{1,0:T(8,128)(2,1)} %copy-done.1), channel_id=1, source_target_pairs={{0,1},{1,0},{2,3},{3,2},{4,5},{5,4},{6,7},{7,6},{8,9},{9,8},{10,11... | collective-permute-start | bytes 11796488 | tf_op jit(solution)/shard_map/ppermute | solution.py:34
  516.1 90.1 %collective-permute-start.75 = (bf16[2560,256]{1,0:T(8,128)(2,1)}, bf16[2560,256]{1,0:T(8,128)(2,1)}, u32[]{:S(2)}, u32[]{:S(2)}) collective-permute-start(bf16[2560,256]{1,0:T(8,128)(2,1)} %slice.528), channel_id=1, source_target_pairs={{0,1},{1,0},{2,3},{3,2},{4,5},{5,4},{6,7},{7,6},{8,9},{9,8},{10,11... | collective-permute-start | bytes 3932168 | tf_op jit(solution)/shard_map/ppermute | solution.py:34
  556.8 50.8 %collective-permute-start.74 = (bf16[1024,256]{1,0:T(8,128)(2,1)}, bf16[1024,256]{1,0:T(8,128)(2,1)}, u32[]{:S(2)}, u32[]{:S(2)}) collective-permute-start(bf16[1024,256]{1,0:T(8,128)(2,1)} %get-tuple-element.172), channel_id=1, source_target_pairs={{0,1},{1,0},{2,3},{3,2},{4,5},{5,4},{6,7},{7,6},{8,9},{9,8},{10,11... | collective-permute-start | bytes 1572872 | tf_op jit(solution)/shard_map/ppermute | solution.py:34
  558.8 39.1 %collective-permute-start.107 = (bf16[4,160,384]{2,1,0:T(8,128)(2,1)}, bf16[4,160,384]{2,1,0:T(8,128)(2,1)}, u32[]{:S(2)}, u32[]{:S(2)}) collective-permute-start(bf16[4,160,384]{2,1,0:T(8,128)(2,1)} %bitcast.66), channel_id=1, source_target_pairs={{0,8},{1,9},{2,10},{3,11},{4,12},{5,13},{6,14},{7,15},{24,16},{25,... | collective-permute-start | bytes 1474568 | tf_op jit(solution)/shard_map/ppermute | solution.py:41
  601.0 37.5 %collective-permute-start.99 = (bf16[4,192,768]{2,1,0:T(8,128)(2,1)S(1)}, bf16[4,192,768]{2,1,0:T(8,128)(2,1)S(1)}, u32[]{:S(2)}, u32[]{:S(2)}) collective-permute-start(bf16[4,192,768]{2,1,0:T(8,128)(2,1)S(1)} %get-tuple-element.158), channel_id=1, source_target_pairs={{0,8},{1,9},{2,10},{3,11},{4,12},{5,13},{6,14},{7,15},{24,16},{25,... | collective-permute-start | bytes 3538952 | tf_op jit(solution)/shard_map/ppermute | solution.py:41
  606.2 48.1 %collective-permute-start.101 = (bf16[4,192,768]{2,1,0:T(8,128)(2,1)S(1)}, bf16[4,192,768]{2,1,0:T(8,128)(2,1)S(1)}, u32[]{:S(2)}, u32[]{:S(2)}) collective-permute-start(bf16[4,192,768]{2,1,0:T(8,128)(2,1)S(1)} %get-tuple-element.159), channel_id=1, source_target_pairs={{0,8},{1,9},{2,10},{3,11},{4,12},{5,13},{6,14},{7,15},{24,16},{25,... | collective-permute-start | bytes 3538952 | tf_op jit(solution)/shard_map/ppermute | solution.py:41
  619.2 71.9 %collective-permute-start.106 = (bf16[4,160,384]{2,1,0:T(8,128)(2,1)S(1)}, bf16[4,160,384]{2,1,0:T(8,128)(2,1)S(1)}, u32[]{:S(2)}, u32[]{:S(2)}) collective-permute-start(bf16[4,160,384]{2,1,0:T(8,128)(2,1)S(1)} %add_convert_fusion.3), channel_id=1, source_target_pairs={{8,16},{9,17},{10,18},{11,19},{12,20},{13,21},{14,22},{15,23},{16,... | collective-permute-start | bytes 1474568 | tf_op jit(solution)/shard_map/ppermute | solution.py:41
  630.1 28.1 %collective-permute-start.81 = (bf16[128,2560]{1,0:T(8,128)(2,1)S(1)}, bf16[128,2560]{1,0:T(8,128)(2,1)S(1)}, u32[]{:S(2)}, u32[]{:S(2)}) collective-permute-start(bf16[128,2560]{1,0:T(8,128)(2,1)S(1)} %slice.555), channel_id=1, source_target_pairs={{0,2},{1,5},{2,0},{3,7},{4,6},{5,1},{6,4},{7,3},{8,10},{9,13},{10,... | collective-permute-start | bytes 1966088 | tf_op jit(solution)/shard_map/ppermute | solution.py:30
  638.5 26.7 %collective-permute-start.96 = (bf16[128,2560]{1,0:T(8,128)(2,1)S(1)}, bf16[128,2560]{1,0:T(8,128)(2,1)S(1)}, u32[]{:S(2)}, u32[]{:S(2)}) collective-permute-start(bf16[128,2560]{1,0:T(8,128)(2,1)S(1)} %slice.567), channel_id=1, source_target_pairs={{0,2},{1,5},{2,0},{3,7},{4,6},{5,1},{6,4},{7,3},{8,10},{9,13},{10,... | collective-permute-start | bytes 1966088 | tf_op jit(solution)/shard_map/ppermute | solution.py:30
  654.3 37.1 %collective-permute-start.109 = (bf16[4,160,384]{2,1,0:T(8,128)(2,1)S(1)}, bf16[4,160,384]{2,1,0:T(8,128)(2,1)S(1)}, u32[]{:S(2)}, u32[]{:S(2)}) collective-permute-start(bf16[4,160,384]{2,1,0:T(8,128)(2,1)S(1)} %fusion.17), channel_id=1, source_target_pairs={{0,8},{1,9},{2,10},{3,11},{4,12},{5,13},{6,14},{7,15},{8,0},{9,1},... | collective-permute-start | bytes 1474568 | tf_op jit(solution)/shard_map/ppermute | solution.py:41
  659.1 38.2 %collective-permute-start.85 = (bf16[64,2560]{1,0:T(8,128)(2,1)}, bf16[64,2560]{1,0:T(8,128)(2,1)}, u32[]{:S(2)}, u32[]{:S(2)}) collective-permute-start(bf16[64,2560]{1,0:T(8,128)(2,1)} %slice.709), channel_id=1, source_target_pairs={{0,4},{1,3},{2,6},{3,1},{4,0},{5,7},{6,2},{7,5},{8,12},{9,11},{10,... | collective-permute-start | bytes 983048 | tf_op jit(solution)/shard_map/ppermute | solution.py:30
  662.0 38.5 %collective-permute-start.100 = (bf16[4,192,768]{2,1,0:T(8,128)(2,1)}, bf16[4,192,768]{2,1,0:T(8,128)(2,1)}, u32[]{:S(2)}, u32[]{:S(2)}) collective-permute-start(bf16[4,192,768]{2,1,0:T(8,128)(2,1)} %get-tuple-element.156), channel_id=1, source_target_pairs={{8,16},{9,17},{10,18},{11,19},{12,20},{13,21},{14,22},{15,23},{16,... | collective-permute-start | bytes 3538952 | tf_op jit(solution)/shard_map/ppermute | solution.py:41
  665.2 47.6 %collective-permute-start.103 = (bf16[4,192,768]{2,1,0:T(8,128)(2,1)}, bf16[4,192,768]{2,1,0:T(8,128)(2,1)}, u32[]{:S(2)}, u32[]{:S(2)}) collective-permute-start(bf16[4,192,768]{2,1,0:T(8,128)(2,1)} %fusion.14), channel_id=1, source_target_pairs={{0,8},{1,9},{2,10},{3,11},{4,12},{5,13},{6,14},{7,15},{8,0},{9,1},... | collective-permute-start | bytes 3538952 | tf_op jit(solution)/shard_map/ppermute | solution.py:41
  691.1 31.4 %collective-permute-start.82 = (bf16[64,2560]{1,0:T(8,128)(2,1)}, bf16[64,2560]{1,0:T(8,128)(2,1)}, u32[]{:S(2)}, u32[]{:S(2)}) collective-permute-start(bf16[64,2560]{1,0:T(8,128)(2,1)} %slice.710), channel_id=1, source_target_pairs={{0,4},{1,3},{2,6},{3,1},{4,0},{5,7},{6,2},{7,5},{8,12},{9,11},{10,... | collective-permute-start | bytes 983048 | tf_op jit(solution)/shard_map/ppermute | solution.py:30
  691.4 33.5 %collective-permute-start.79 = (bf16[64,2560]{1,0:T(8,128)(2,1)}, bf16[64,2560]{1,0:T(8,128)(2,1)S(1)}, u32[]{:S(2)}, u32[]{:S(2)}) collective-permute-start(bf16[64,2560]{1,0:T(8,128)(2,1)} %slice.711), channel_id=1, source_target_pairs={{0,4},{1,3},{2,6},{3,1},{4,0},{5,7},{6,2},{7,5},{8,12},{9,11},{10,... | collective-permute-start | bytes 983048 | tf_op jit(solution)/shard_map/ppermute | solution.py:30
  697.3 48.6 %collective-permute-start.77 = (bf16[64,2560]{1,0:T(8,128)(2,1)}, bf16[64,2560]{1,0:T(8,128)(2,1)}, u32[]{:S(2)}, u32[]{:S(2)}) collective-permute-start(bf16[64,2560]{1,0:T(8,128)(2,1)} %slice.712), channel_id=1, source_target_pairs={{0,4},{1,3},{2,6},{3,1},{4,0},{5,7},{6,2},{7,5},{8,12},{9,11},{10,... | collective-permute-start | bytes 983048 | tf_op jit(solution)/shard_map/ppermute | solution.py:30
  700.5 40.8 %collective-permute-start.97 = (bf16[64,2560]{1,0:T(8,128)(2,1)}, bf16[64,2560]{1,0:T(8,128)(2,1)}, u32[]{:S(2)}, u32[]{:S(2)}) collective-permute-start(bf16[64,2560]{1,0:T(8,128)(2,1)} %slice.708), channel_id=1, source_target_pairs={{0,4},{1,3},{2,6},{3,1},{4,0},{5,7},{6,2},{7,5},{8,12},{9,11},{10,... | collective-permute-start | bytes 983048 | tf_op jit(solution)/shard_map/ppermute | solution.py:30
  712.7 33.7 %collective-permute-start.86 = (bf16[64,2560]{1,0:T(8,128)(2,1)}, bf16[64,2560]{1,0:T(8,128)(2,1)}, u32[]{:S(2)}, u32[]{:S(2)}) collective-permute-start(bf16[64,2560]{1,0:T(8,128)(2,1)} %fusion.25), channel_id=1, source_target_pairs={{0,24},{1,25},{2,26},{3,27},{4,28},{5,29},{6,30},{7,31},{8,16},{9,... | collective-permute-start | bytes 983048 | tf_op jit(solution)/shard_map/ppermute | solution.py:30
  736.5 57.6 %all-to-all-start.6 = ((bf16[16,160,512]{2,1,0:T(8,128)(2,1)}), bf16[16,160,512]{2,1,0:T(8,128)(2,1)S(1)}, u32[]{:S(2)}, u32[]{:S(2)}) async-start(bf16[16,160,512]{2,1,0:T(8,128)(2,1)} %bitcast.194), calls=%async_computation.6 | async-start | bytes 5242880 | tf_op jit(solution)/shard_map/all_to_all | solution.py:171
  750.7 53.5 %collective-permute-start.104 = (bf16[2,192,768]{2,1,0:T(8,128)(2,1)S(1)}, bf16[2,192,768]{2,1,0:T(8,128)(2,1)}, u32[]{:S(2)}, u32[]{:S(2)}) collective-permute-start(bf16[2,192,768]{2,1,0:T(8,128)(2,1)S(1)} %constant_dynamic-slice_fusion.7), channel_id=1, source_target_pairs={{0,1},{1,0},{2,3},{3,2},{4,5},{5,4},{6,7},{7,6},{8,9},{9,8},{10,11... | collective-permute-start | bytes 1769480 | tf_op jit(solution)/shard_map/ppermute | solution.py:34
  (145 other events, 1701.1 us)

commit v5 on v4

--- a/solution.py
+++ b/solution.py
@@ -819,7 +819,7 @@
     )
     wide_grad, turned_grad = lax.optimization_barrier((wide_grad, turned_grad))
     turned_grad = all_to_all(turned_grad)
-    dq = after(near_gathered(slabs(dr.astype(BF16))), turned_grad)
+    dq = near_gathered(slabs(dr.astype(BF16)))
     dq, wide_grad = lax.optimization_barrier((dq, wide_grad))
     (out_sum,) = scattered((grouped(after(zb, dq)), c_both))
     out_half = (r + out_sum).astype(BF16)
@@ -864,7 +864,7 @@
         [token_bf16],
         [padded],
     )[0]
-    dyv = jnp.concatenate([dy, dv], axis=1)
+    dyv = after(jnp.concatenate([dy, dv], axis=1), turned_grad)
 
     def to_owners(grad):
         grad = row_scattered(list(grad)).astype(BF16)

time: 833 us -> 832 us (level)
    all_to_all x3, waiting for transfers between devices: 57.4 us -> 42.7 us  [all_to_all(): return lax.all_to_all(pieces, 'seq', 0, 0, tiled=True)]
    ppermute x52, waiting for transfers between devices: 144 us -> 156 us  [xor_send(): return lax.ppermute(value, BOTH, pairs)]
    unnamed x172 -> x158, local copies, waits for them, and re-layouts: 38.3 us -> 39.8 us
  transfers between devices with their start and end apart: 119 -> 119, of which waited for: 38 -> 37; matrix products, arithmetic and copies ran while one was open for 24% -> 24% of each run, Pallas kernels for 7% -> 7%
where the time goes in v5:
time: 832 us; the launch traced here: 815 us
  waiting for transfers between devices  339 us (41%)
  starting transfers between devices  186 us (22%)
  matrix products  81 us (10%)
  local copies, waits for them, and re-layouts  72.4 us (9%)
  other arithmetic  71.5 us (9%)
  Pallas kernels  62 us (7%)
    ppermute x52, waiting for transfers between devices, xor_send(): return lax.ppermute(value, BOTH, pairs)  156 us
    ppermute x30, waiting for transfers between devices, row_send(): return lax.ppermute(value, BOTH, pairs)  126 us
    dot_general x25, matrix products, dot(): lax.dot_general(left, right, (over, ((), ())), preferred_element_type=F32)  81 us
    ppermute x30, starting transfers between devices, row_send(): return lax.ppermute(value, BOTH, pairs)  64.6 us
    ppermute x52, starting transfers between devices, xor_send(): return lax.ppermute(value, BOTH, pairs)  60.3 us
    all_to_all x3, waiting for transfers between devices, all_to_all(): return lax.all_to_all(pieces, 'seq', 0, 0, tiled=True)  42.7 us
    unnamed x158, local copies, waits for them, and re-layouts  39.8 us
    pallas_call x6, Pallas kernels, in_vmem(): pl.pallas_call(kernel, out_shape=[jax.ShapeDtypeStruct(shape, dtype) for...  28.8 us
  transfers between devices with their start and end apart: 119, of which 37 were waited for; matrix products, arithmetic and copies ran while one was open for 24% of the time, Pallas kernels for 7%

profile of v5, /device:TPU:5, one launch (start us, length us, event | category | flops | bytes accessed | tf_op | source)
XLA Modules:
  0.0 815.5 jit_solution(4914917286955653567)
XLA Ops:
  17.6 7.6 collective-permute-done.1
  28.9 4.2 all-to-all-start
  35.5 10.6 %shard_map.283 = bf16[16,160,768]{2,1,0:T(8,128)(2,1)} custom-call(f32[160,1]{1,0:T(8,128)} %copy.54.gain, bf16[160,3840]{1,0:T(8,128)(2,1)} %gate.3, bf16[160,3840]{1,0:T(8,128)(2,1)} %value.3, bf16[160,3840]{1,0:T(8,128)(2,1)} %bitcast.207), custom_call_target="tpu_custom_call" | custom-call | tf_op jit(solution)/shard_map/pallas_call | solution.py:191
  48.1 4.4 all-to-all-start.1
  54.6 4.2 pad_maximum_fusion.3
  65.5 20.4 %collective-permute-done.38 = bf16[64,2560]{1,0:T(8,128)(2,1)S(1)} collective-permute-done((bf16[64,2560]{1,0:T(8,128)(2,1)S(1)}, bf16[64,2560]{1,0:T(8,128)(2,1)S(1)}, u32[]{:S(2)}, u32[]{:S(2)}) %collective-permute-start.38) | collective-permute-done | bytes 327712 | tf_op jit(solution)/shard_map/ppermute | solution.py:41
  97.6 5.8 collective-permute-done.40
  107.2 4.1 collective-permute-done.44
  112.8 13.5 %collective-permute-done.7 = bf16[4,192,768]{2,1,0:T(8,128)(2,1)S(1)} collective-permute-done((bf16[4,192,768]{2,1,0:T(8,128)(2,1)S(1)}, bf16[4,192,768]{2,1,0:T(8,128)(2,1)S(1)}, u32[]{:S(2)}, u32[]{:S(2)}) %collective-permute-start.7) | collective-permute-done | bytes 1179680 | tf_op jit(solution)/shard_map/ppermute | solution.py:41
  141.8 16.9 %collective-permute-done.8 = bf16[4,192,768]{2,1,0:T(8,128)(2,1)S(1)} collective-permute-done((bf16[4,192,768]{2,1,0:T(8,128)(2,1)S(1)}, bf16[4,192,768]{2,1,0:T(8,128)(2,1)S(1)}, u32[]{:S(2)}, u32[]{:S(2)}) %collective-permute-start.8) | collective-permute-done | bytes 1179680 | tf_op jit(solution)/shard_map/ppermute | solution.py:41
  176.1 7.9 collective-permute-done.19
  184.2 11.3 %collective-permute-done.20 = bf16[4,160,384]{2,1,0:T(8,128)(2,1)S(1)} collective-permute-done((bf16[4,160,384]{2,1,0:T(8,128)(2,1)S(1)}, bf16[4,160,384]{2,1,0:T(8,128)(2,1)S(1)}, u32[]{:S(2)}, u32[]{:S(2)}) %collective-permute-start.20) | collective-permute-done | bytes 491552 | tf_op jit(solution)/shard_map/ppermute | solution.py:41
  208.6 6.8 shard_map.281
  219.8 4.8 all-to-all-start.2
  243.3 18.5 %collective-permute-done.22 = bf16[128,2560]{1,0:T(8,128)(2,1)S(1)} collective-permute-done((bf16[128,2560]{1,0:T(8,128)(2,1)S(1)}, bf16[128,2560]{1,0:T(8,128)(2,1)S(1)}, u32[]{:S(2)}, u32[]{:S(2)}) %collective-permute-start.22) | collective-permute-done | bytes 655392 | tf_op jit(solution)/shard_map/ppermute | solution.py:30
  266.8 14.3 %collective-permute-done.23 = bf16[64,2560]{1,0:T(8,128)(2,1)S(1)} collective-permute-done((bf16[64,2560]{1,0:T(8,128)(2,1)S(1)}, bf16[64,2560]{1,0:T(8,128)(2,1)S(1)}, u32[]{:S(2)}, u32[]{:S(2)}) %collective-permute-start.23) | collective-permute-done | bytes 327712 | tf_op jit(solution)/shard_map/ppermute | solution.py:30
  284.6 9.9 %collective-permute-done.24 = bf16[64,2560]{1,0:T(8,128)(2,1)S(1)} collective-permute-done((bf16[64,2560]{1,0:T(8,128)(2,1)S(1)}, bf16[64,2560]{1,0:T(8,128)(2,1)S(1)}, u32[]{:S(2)}, u32[]{:S(2)}) %collective-permute-start.24) | collective-permute-done | bytes 327712 | tf_op jit(solution)/shard_map/ppermute | solution.py:30
  294.6 10.9 %collective-permute-start.25 = (bf16[128,2560]{1,0:T(8,128)(2,1)S(1)}, bf16[128,2560]{1,0:T(8,128)(2,1)S(1)}, u32[]{:S(2)}, u32[]{:S(2)}) collective-permute-start(bf16[128,2560]{1,0:T(8,128)(2,1)S(1)} %pad_maximum_fusion.23), channel_id=1, source_target_pairs={{0,2},{1,5},{2,0},{3,7},{4,6},{5,1},{6,4},{7,3},{8,10},{9,13},{10,... | collective-permute-start | bytes 1966088 | tf_op jit(solution)/shard_map/ppermute | solution.py:30
  313.2 22.4 %collective-permute-done.34 = bf16[64,2560]{1,0:T(8,128)(2,1)S(1)} collective-permute-done((bf16[64,2560]{1,0:T(8,128)(2,1)S(1)}, bf16[64,2560]{1,0:T(8,128)(2,1)S(1)}, u32[]{:S(2)}, u32[]{:S(2)}) %collective-permute-start.34) | collective-permute-done | bytes 327712 | tf_op jit(solution)/shard_map/ppermute | solution.py:41
  350.9 7.5 collective-permute-done.33
  361.0 8.7 %fusion.135.dz = f32[2048,256]{1,0:T(8,128)} fusion(bf16[2048,2560]{1,0:T(8,128)(2,1)} %constant_dynamic-update-slice_fusion, bf16[2560,768]{1,0:T(8,128)(2,1)} %bitcast.42), kind=kOutput, calls=%fused_computation.404 | convolution fusion | flops 2684354560 | bytes 13893632 | tf_op jit(solution)/shard_map/dot_general | solution.py:638
  373.5 6.2 collective-permute-done.53
  384.8 4.0 copy-done.57
  388.8 9.4 %fusion.137.ge = f32[2048,512]{1,0:T(8,128)} fusion(bf16[2048,2560]{1,0:T(8,128)(2,1)S(1)} %constant_dynamic-update-slice_fusion.16, bf16[2560,768]{1,0:T(8,128)(2,1)} %bitcast.42), kind=kOutput, calls=%fused_computation.406 | convolution fusion | flops 5368709120 | bytes 17301504 | tf_op jit(solution)/shard_map/dot_general | solution.py:638
  398.2 6.4 shard_map.284
  429.9 12.6 %collective-permute-done.62 = bf16[128,2560]{1,0:T(8,128)(2,1)S(1)} collective-permute-done((bf16[128,2560]{1,0:T(8,128)(2,1)S(1)}, bf16[128,2560]{1,0:T(8,128)(2,1)S(1)}, u32[]{:S(2)}, u32[]{:S(2)}) %collective-permute-start.62) | collective-permute-done | bytes 655392 | tf_op jit(solution)/shard_map/ppermute | solution.py:30
  442.9 10.4 %collective-permute-done.60 = bf16[128,2560]{1,0:T(8,128)(2,1)S(1)} collective-permute-done((bf16[128,2560]{1,0:T(8,128)(2,1)S(1)}, bf16[128,2560]{1,0:T(8,128)(2,1)S(1)}, u32[]{:S(2)}, u32[]{:S(2)}) %collective-permute-start.60) | collective-permute-done | bytes 655392 | tf_op jit(solution)/shard_map/ppermute | solution.py:30
  455.6 5.0 collective-permute-start.67
  461.5 24.3 %collective-permute-done.67 = bf16[64,2560]{1,0:T(8,128)(2,1)S(1)} collective-permute-done((bf16[64,2560]{1,0:T(8,128)(2,1)S(1)}, bf16[64,2560]{1,0:T(8,128)(2,1)S(1)}, u32[]{:S(2)}, u32[]{:S(2)}) %collective-permute-start.67) | collective-permute-done | bytes 327712 | tf_op jit(solution)/shard_map/ppermute | solution.py:30
  495.6 10.7 %convolution_convert_fusion.1 = bf16[2560,512]{1,0:T(8,128)(2,1)} fusion(bf16[2048,2560]{1,0:T(8,128)(2,1)} %copy-done.57, bf16[2048,512]{1,0:T(8,128)(2,1)} %get-tuple-element.78), kind=kOutput, calls=%fused_computation.3 | convolution fusion | flops 5370019840 | bytes 15204352 | tf_op jit(solution)/shard_map/dot_general | solution.py:638
  508.8 4.2 convolution_convert_fusion.7
  513.0 4.7 all-to-all-start.3
  523.3 6.1 shard_map.285
  537.3 6.1 collective-permute-done.90
  545.2 4.8 collective-permute-done.89
  550.0 4.7 collective-permute-start.107
  555.3 5.0 shard_map.286
  571.7 4.0 shard_map.287
  587.9 4.5 convolution_convert_fusion
  619.9 4.7 collective-permute-done.76
  624.8 6.8 collective-permute-done.84
  635.1 15.1 %collective-permute-done.101 = bf16[4,192,768]{2,1,0:T(8,128)(2,1)S(1)} collective-permute-done((bf16[4,192,768]{2,1,0:T(8,128)(2,1)S(1)}, bf16[4,192,768]{2,1,0:T(8,128)(2,1)S(1)}, u32[]{:S(2)}, u32[]{:S(2)}) %collective-permute-start.101) | collective-permute-done | bytes 1179680 | tf_op jit(solution)/shard_map/ppermute | solution.py:41
  661.4 24.9 %collective-permute-start.103 = (bf16[4,192,768]{2,1,0:T(8,128)(2,1)}, bf16[4,192,768]{2,1,0:T(8,128)(2,1)}, u32[]{:S(2)}, u32[]{:S(2)}) collective-permute-start(bf16[4,192,768]{2,1,0:T(8,128)(2,1)} %fusion.14), channel_id=1, source_target_pairs={{0,8},{1,9},{2,10},{3,11},{4,12},{5,13},{6,14},{7,15},{8,0},{9,1},... | collective-permute-start | bytes 3538952 | tf_op jit(solution)/shard_map/ppermute | solution.py:41
  697.7 13.6 %collective-permute-done.103 = bf16[4,192,768]{2,1,0:T(8,128)(2,1)} collective-permute-done((bf16[4,192,768]{2,1,0:T(8,128)(2,1)}, bf16[4,192,768]{2,1,0:T(8,128)(2,1)}, u32[]{:S(2)}, u32[]{:S(2)}) %collective-permute-start.103) | collective-permute-done | bytes 1179680 | tf_op jit(solution)/shard_map/ppermute | solution.py:41
  726.2 7.2 all-to-all-done.4
  734.5 5.7 all-to-all-start.6
  750.5 42.7 %all-to-all-done.6.grads = bf16[16,160,512]{2,1,0:T(8,128)(2,1)S(1)} async-done(((bf16[16,160,512]{2,1,0:T(8,128)(2,1)}), bf16[16,160,512]{2,1,0:T(8,128)(2,1)S(1)}, u32[]{:S(2)}, u32[]{:S(2)}) %all-to-all-start.6) | async-done | bytes 2621472 | tf_op jit(solution)/shard_map/all_to_all | solution.py:171
  794.7 7.6 shard_map.290
  (594 shorter events, 335.5 us)
Async XLA Ops:
  26.4 28.1 %collective-permute-start.2 = (bf16[256,2560]{1,0:T(8,128)(2,1)}, bf16[256,2560]{1,0:T(8,128)(2,1)}, u32[]{:S(2)}, u32[]{:S(2)}) collective-permute-start(bf16[256,2560]{1,0:T(8,128)(2,1)} %pad_maximum_fusion.8), channel_id=1, source_target_pairs={{0,1},{1,0},{2,3},{3,2},{4,5},{5,4},{6,7},{7,6},{8,9},{9,8},{10,11... | collective-permute-start | bytes 3932168 | tf_op jit(solution)/shard_map/ppermute | solution.py:34
  48.1 110.9 %all-to-all-start.1 = ((bf16[4,160,384]{2,1,0:T(8,128)(2,1)}), bf16[4,160,384]{2,1,0:T(8,128)(2,1)}, u32[]{:S(2)}, u32[]{:S(2)}) async-start(bf16[4,160,384]{2,1,0:T(8,128)(2,1)} %pad_maximum_fusion.36), calls=%async_computation.1 | async-start | bytes 983040 | tf_op jit(solution)/shard_map/all_to_all | solution.py:134
  52.4 36.0 %collective-permute-start.4 = (bf16[4,192,768]{2,1,0:T(8,128)(2,1)S(1)}, bf16[4,192,768]{2,1,0:T(8,128)(2,1)S(1)}, u32[]{:S(2)}, u32[]{:S(2)}) collective-permute-start(bf16[4,192,768]{2,1,0:T(8,128)(2,1)S(1)} %all-to-all-done), channel_id=1, source_target_pairs={{0,8},{1,9},{2,10},{3,11},{4,12},{5,13},{6,14},{7,15},{8,0},{9,1},... | collective-permute-start | bytes 3538952 | tf_op jit(solution)/shard_map/ppermute | solution.py:41
  53.7 37.8 %collective-permute-start.6 = (bf16[4,192,768]{2,1,0:T(8,128)(2,1)S(1)}, bf16[4,192,768]{2,1,0:T(8,128)(2,1)S(1)}, u32[]{:S(2)}, u32[]{:S(2)}) collective-permute-start(bf16[4,192,768]{2,1,0:T(8,128)(2,1)S(1)} %all-to-all-done), channel_id=1, source_target_pairs={{8,16},{9,17},{10,18},{11,19},{12,20},{13,21},{14,22},{15,23},{16,... | collective-permute-start | bytes 3538952 | tf_op jit(solution)/shard_map/ppermute | solution.py:41
  59.9 25.9 %collective-permute-start.38 = (bf16[64,2560]{1,0:T(8,128)(2,1)S(1)}, bf16[64,2560]{1,0:T(8,128)(2,1)S(1)}, u32[]{:S(2)}, u32[]{:S(2)}) collective-permute-start(bf16[64,2560]{1,0:T(8,128)(2,1)S(1)} %constant_dynamic-slice_fusion.20), channel_id=1, source_target_pairs={{0,8},{1,9},{2,10},{3,11},{4,12},{5,13},{6,14},{7,15},{8,0},{9,1},... | collective-permute-start | bytes 983048 | tf_op jit(solution)/shard_map/ppermute | solution.py:41
  65.1 28.8 %collective-permute-start.37 = (bf16[128,2560]{1,0:T(8,128)(2,1)S(1)}, bf16[128,2560]{1,0:T(8,128)(2,1)S(1)}, u32[]{:S(2)}, u32[]{:S(2)}) collective-permute-start(bf16[128,2560]{1,0:T(8,128)(2,1)S(1)} %pad_maximum_fusion.27), channel_id=1, source_target_pairs={{0,2},{1,5},{2,0},{3,7},{4,6},{5,1},{6,4},{7,3},{8,10},{9,13},{10,... | collective-permute-start | bytes 1966088 | tf_op jit(solution)/shard_map/ppermute | solution.py:30
  92.2 34.1 %collective-permute-start.7 = (bf16[4,192,768]{2,1,0:T(8,128)(2,1)S(1)}, bf16[4,192,768]{2,1,0:T(8,128)(2,1)S(1)}, u32[]{:S(2)}, u32[]{:S(2)}) collective-permute-start(bf16[4,192,768]{2,1,0:T(8,128)(2,1)S(1)} %collective-permute-done.6), channel_id=1, source_target_pairs={{8,0},{9,1},{10,2},{11,3},{12,4},{13,5},{14,6},{15,7},{16,24},{17,... | collective-permute-start | bytes 3538952 | tf_op jit(solution)/shard_map/ppermute | solution.py:41
  93.9 39.4 %collective-permute-start.46 = (bf16[64,2560]{1,0:T(8,128)(2,1)S(1)}, bf16[64,2560]{1,0:T(8,128)(2,1)S(1)}, u32[]{:S(2)}, u32[]{:S(2)}) collective-permute-start(bf16[64,2560]{1,0:T(8,128)(2,1)S(1)} %collective-permute-done.41), channel_id=1, source_target_pairs={{8,0},{9,1},{10,2},{11,3},{12,4},{13,5},{14,6},{15,7},{16,24},{17,... | collective-permute-start | bytes 983048 | tf_op jit(solution)/shard_map/ppermute | solution.py:41
  126.7 32.0 %collective-permute-start.8 = (bf16[4,192,768]{2,1,0:T(8,128)(2,1)S(1)}, bf16[4,192,768]{2,1,0:T(8,128)(2,1)S(1)}, u32[]{:S(2)}, u32[]{:S(2)}) collective-permute-start(bf16[4,192,768]{2,1,0:T(8,128)(2,1)S(1)} %collective-permute-done.5), channel_id=1, source_target_pairs={{8,0},{9,1},{10,2},{11,3},{12,4},{13,5},{14,6},{15,7},{16,24},{17,... | collective-permute-start | bytes 3538952 | tf_op jit(solution)/shard_map/ppermute | solution.py:41
  141.3 90.1 %collective-permute-start.48 = (bf16[128,2560]{1,0:T(8,128)(2,1)}, bf16[128,2560]{1,0:T(8,128)(2,1)}, u32[]{:S(2)}, u32[]{:S(2)}) collective-permute-start(bf16[128,2560]{1,0:T(8,128)(2,1)} %pad_maximum_fusion.30), channel_id=1, source_target_pairs={{0,2},{1,5},{2,0},{3,7},{4,6},{5,1},{6,4},{7,3},{8,10},{9,13},{10,... | collective-permute-start | bytes 1966088 | tf_op jit(solution)/shard_map/ppermute | solution.py:30
  165.5 36.7 %collective-permute-start.9 = (f32[8,384]{1,0:T(8,128)}, f32[8,384]{1,0:T(8,128)}, u32[]{:S(2)}, u32[]{:S(2)}) collective-permute-start(f32[8,384]{1,0:T(8,128)} %constant_dynamic-slice_fusion.29), channel_id=1, source_target_pairs={{0,8},{1,9},{2,10},{3,11},{4,12},{5,13},{6,14},{7,15},{8,16},{9,17... | collective-permute-start | bytes 36872 | tf_op jit(solution)/shard_map/ppermute | solution.py:145
  198.1 37.2 %collective-permute-start.21 = (bf16[2560,384]{1,0:T(8,128)(2,1)S(1)}, bf16[2560,384]{1,0:T(8,128)(2,1)}, u32[]{:S(2)}, u32[]{:S(2)}) collective-permute-start(bf16[2560,384]{1,0:T(8,128)(2,1)S(1)} %pad_maximum_fusion.6), channel_id=1, source_target_pairs={{0,1},{1,0},{2,3},{3,2},{4,5},{5,4},{6,7},{7,6},{8,9},{9,8},{10,11... | collective-permute-start | bytes 5898248 | tf_op jit(solution)/shard_map/ppermute | solution.py:34
  219.8 141.3 %all-to-all-start.2 = ((bf16[16,160,768]{2,1,0:T(8,128)(2,1)}), bf16[16,160,768]{2,1,0:T(8,128)(2,1)}, u32[]{:S(2)}, u32[]{:S(2)}) async-start(bf16[16,160,768]{2,1,0:T(8,128)(2,1)} %shard_map.283), calls=%async_computation.2 | async-start | bytes 7864320 | tf_op jit(solution)/shard_map/all_to_all | solution.py:171
  226.4 39.2 %collective-permute-start.51 = (bf16[256,2560]{1,0:T(8,128)(2,1)}, bf16[256,2560]{1,0:T(8,128)(2,1)S(1)}, u32[]{:S(2)}, u32[]{:S(2)}) collective-permute-start(bf16[256,2560]{1,0:T(8,128)(2,1)} %pad_maximum_fusion.11), channel_id=1, source_target_pairs={{0,1},{1,0},{2,3},{3,2},{4,5},{5,4},{6,7},{7,6},{8,9},{9,8},{10,11... | collective-permute-start | bytes 3932168 | tf_op jit(solution)/shard_map/ppermute | solution.py:34
  234.8 47.5 %collective-permute-start.52 = (bf16[256,2560]{1,0:T(8,128)(2,1)S(1)}, bf16[256,2560]{1,0:T(8,128)(2,1)S(1)}, u32[]{:S(2)}, u32[]{:S(2)}) collective-permute-start(bf16[256,2560]{1,0:T(8,128)(2,1)S(1)} %pad_maximum_fusion.12), channel_id=1, source_target_pairs={{0,1},{1,0},{2,3},{3,2},{4,5},{5,4},{6,7},{7,6},{8,9},{9,8},{10,11... | collective-permute-start | bytes 3932168 | tf_op jit(solution)/shard_map/ppermute | solution.py:34
  294.6 41.1 %collective-permute-start.25 = (bf16[128,2560]{1,0:T(8,128)(2,1)S(1)}, bf16[128,2560]{1,0:T(8,128)(2,1)S(1)}, u32[]{:S(2)}, u32[]{:S(2)}) collective-permute-start(bf16[128,2560]{1,0:T(8,128)(2,1)S(1)} %pad_maximum_fusion.23), channel_id=1, source_target_pairs={{0,2},{1,5},{2,0},{3,7},{4,6},{5,1},{6,4},{7,3},{8,10},{9,13},{10,... | collective-permute-start | bytes 1966088 | tf_op jit(solution)/shard_map/ppermute | solution.py:30
  307.0 34.3 %collective-permute-start.31 = (bf16[64,2560]{1,0:T(8,128)(2,1)S(1)}, bf16[64,2560]{1,0:T(8,128)(2,1)S(1)}, u32[]{:S(2)}, u32[]{:S(2)}) collective-permute-start(bf16[64,2560]{1,0:T(8,128)(2,1)S(1)} %collective-permute-done.30), channel_id=1, source_target_pairs={{8,0},{9,1},{10,2},{11,3},{12,4},{13,5},{14,6},{15,7},{16,24},{17,... | collective-permute-start | bytes 983048 | tf_op jit(solution)/shard_map/ppermute | solution.py:41
  309.0 26.5 %collective-permute-start.34 = (bf16[64,2560]{1,0:T(8,128)(2,1)S(1)}, bf16[64,2560]{1,0:T(8,128)(2,1)S(1)}, u32[]{:S(2)}, u32[]{:S(2)}) collective-permute-start(bf16[64,2560]{1,0:T(8,128)(2,1)S(1)} %collective-permute-done.29), channel_id=1, source_target_pairs={{8,0},{9,1},{10,2},{11,3},{12,4},{13,5},{14,6},{15,7},{16,24},{17,... | collective-permute-start | bytes 983048 | tf_op jit(solution)/shard_map/ppermute | solution.py:41
  312.2 28.2 %collective-permute-start.28 = (bf16[128,2560]{1,0:T(8,128)(2,1)S(1)}, bf16[128,2560]{1,0:T(8,128)(2,1)S(1)}, u32[]{:S(2)}, u32[]{:S(2)}) collective-permute-start(bf16[128,2560]{1,0:T(8,128)(2,1)S(1)} %pad_maximum_fusion.24), channel_id=1, source_target_pairs={{0,2},{1,5},{2,0},{3,7},{4,6},{5,1},{6,4},{7,3},{8,10},{9,13},{10,... | collective-permute-start | bytes 1966088 | tf_op jit(solution)/shard_map/ppermute | solution.py:30
  335.8 44.7 %collective-permute-start.54 = (bf16[256,2560]{1,0:T(8,128)(2,1)S(1)}, bf16[256,2560]{1,0:T(8,128)(2,1)}, u32[]{:S(2)}, u32[]{:S(2)}) collective-permute-start(bf16[256,2560]{1,0:T(8,128)(2,1)S(1)} %pad_maximum_fusion.13), channel_id=1, source_target_pairs={{0,1},{1,0},{2,3},{3,2},{4,5},{5,4},{6,7},{7,6},{8,9},{9,8},{10,11... | collective-permute-start | bytes 3932168 | tf_op jit(solution)/shard_map/ppermute | solution.py:34
  343.7 38.2 %collective-permute-start.55 = (bf16[256,2560]{1,0:T(8,128)(2,1)}, bf16[256,2560]{1,0:T(8,128)(2,1)}, u32[]{:S(2)}, u32[]{:S(2)}) collective-permute-start(bf16[256,2560]{1,0:T(8,128)(2,1)} %pad_maximum_fusion.14), channel_id=1, source_target_pairs={{0,1},{1,0},{2,3},{3,2},{4,5},{5,4},{6,7},{7,6},{8,9},{9,8},{10,11... | collective-permute-start | bytes 3932168 | tf_op jit(solution)/shard_map/ppermute | solution.py:34
  373.4 33.0 %collective-permute-start.59 = (bf16[2560,512]{1,0:T(8,128)(2,1)S(1)}, bf16[2560,512]{1,0:T(8,128)(2,1)}, u32[]{:S(2)}, u32[]{:S(2)}) collective-permute-start(bf16[2560,512]{1,0:T(8,128)(2,1)S(1)} %slice.529), channel_id=1, source_target_pairs={{0,1},{1,0},{2,3},{3,2},{4,5},{5,4},{6,7},{7,6},{8,9},{9,8},{10,11... | collective-permute-start | bytes 7864328 | tf_op jit(solution)/shard_map/ppermute | solution.py:34
  425.8 27.5 %collective-permute-start.60 = (bf16[128,2560]{1,0:T(8,128)(2,1)S(1)}, bf16[128,2560]{1,0:T(8,128)(2,1)S(1)}, u32[]{:S(2)}, u32[]{:S(2)}) collective-permute-start(bf16[128,2560]{1,0:T(8,128)(2,1)S(1)} %slice.531), channel_id=1, source_target_pairs={{0,2},{1,5},{2,0},{3,7},{4,6},{5,1},{6,4},{7,3},{8,10},{9,13},{10,... | collective-permute-start | bytes 1966088 | tf_op jit(solution)/shard_map/ppermute | solution.py:30
  426.1 27.5 %collective-permute-start.69 = (bf16[64,2560]{1,0:T(8,128)(2,1)S(1)}, bf16[64,2560]{1,0:T(8,128)(2,1)S(1)}, u32[]{:S(2)}, u32[]{:S(2)}) collective-permute-start(bf16[64,2560]{1,0:T(8,128)(2,1)S(1)} %slice.697), channel_id=1, source_target_pairs={{0,4},{1,3},{2,6},{3,1},{4,0},{5,7},{6,2},{7,5},{8,12},{9,11},{10,... | collective-permute-start | bytes 983048 | tf_op jit(solution)/shard_map/ppermute | solution.py:30
  429.7 25.8 %collective-permute-start.66 = (bf16[64,2560]{1,0:T(8,128)(2,1)S(1)}, bf16[64,2560]{1,0:T(8,128)(2,1)S(1)}, u32[]{:S(2)}, u32[]{:S(2)}) collective-permute-start(bf16[64,2560]{1,0:T(8,128)(2,1)S(1)} %slice.698), channel_id=1, source_target_pairs={{0,4},{1,3},{2,6},{3,1},{4,0},{5,7},{6,2},{7,5},{8,12},{9,11},{10,... | collective-permute-start | bytes 983048 | tf_op jit(solution)/shard_map/ppermute | solution.py:30
  455.6 30.3 %collective-permute-start.67 = (bf16[64,2560]{1,0:T(8,128)(2,1)S(1)}, bf16[64,2560]{1,0:T(8,128)(2,1)S(1)}, u32[]{:S(2)}, u32[]{:S(2)}) collective-permute-start(bf16[64,2560]{1,0:T(8,128)(2,1)S(1)} %fusion.34), channel_id=1, source_target_pairs={{0,16},{1,17},{2,18},{3,19},{4,20},{5,21},{6,22},{7,23},{8,24},{9,... | collective-permute-start | bytes 983048 | tf_op jit(solution)/shard_map/ppermute | solution.py:30
  490.0 123.8 %collective-permute-start.95 = (bf16[2560,768]{1,0:T(8,128)(2,1)}, bf16[2560,768]{1,0:T(8,128)(2,1)}, u32[]{:S(2)}, u32[]{:S(2)}) collective-permute-start(bf16[2560,768]{1,0:T(8,128)(2,1)} %copy-done.1), channel_id=1, source_target_pairs={{0,1},{1,0},{2,3},{3,2},{4,5},{5,4},{6,7},{7,6},{8,9},{9,8},{10,11... | collective-permute-start | bytes 11796488 | tf_op jit(solution)/shard_map/ppermute | solution.py:34
  494.3 106.6 %collective-permute-start.75 = (bf16[2560,256]{1,0:T(8,128)(2,1)}, bf16[2560,256]{1,0:T(8,128)(2,1)}, u32[]{:S(2)}, u32[]{:S(2)}) collective-permute-start(bf16[2560,256]{1,0:T(8,128)(2,1)} %slice.528), channel_id=1, source_target_pairs={{0,1},{1,0},{2,3},{3,2},{4,5},{5,4},{6,7},{7,6},{8,9},{9,8},{10,11... | collective-permute-start | bytes 3932168 | tf_op jit(solution)/shard_map/ppermute | solution.py:34
  513.0 74.8 %all-to-all-start.3 = ((bf16[16,160,256]{2,1,0:T(8,128)(2,1)}), bf16[16,160,256]{2,1,0:T(8,128)(2,1)S(1)}, u32[]{:S(2)}, u32[]{:S(2)}) async-start(bf16[16,160,256]{2,1,0:T(8,128)(2,1)} %bitcast.206), calls=%async_computation.3 | async-start | bytes 2621440 | tf_op jit(solution)/shard_map/all_to_all | solution.py:171
  543.4 58.8 %collective-permute-start.74 = (bf16[1024,256]{1,0:T(8,128)(2,1)}, bf16[1024,256]{1,0:T(8,128)(2,1)}, u32[]{:S(2)}, u32[]{:S(2)}) collective-permute-start(bf16[1024,256]{1,0:T(8,128)(2,1)} %get-tuple-element.172), channel_id=1, source_target_pairs={{0,1},{1,0},{2,3},{3,2},{4,5},{5,4},{6,7},{7,6},{8,9},{9,8},{10,11... | collective-permute-start | bytes 1572872 | tf_op jit(solution)/shard_map/ppermute | solution.py:34
  550.0 46.0 %collective-permute-start.107 = (bf16[4,160,384]{2,1,0:T(8,128)(2,1)}, bf16[4,160,384]{2,1,0:T(8,128)(2,1)}, u32[]{:S(2)}, u32[]{:S(2)}) collective-permute-start(bf16[4,160,384]{2,1,0:T(8,128)(2,1)} %bitcast.66), channel_id=1, source_target_pairs={{0,8},{1,9},{2,10},{3,11},{4,12},{5,13},{6,14},{7,15},{24,16},{25,... | collective-permute-start | bytes 1474568 | tf_op jit(solution)/shard_map/ppermute | solution.py:41
  598.2 35.5 %collective-permute-start.99 = (bf16[4,192,768]{2,1,0:T(8,128)(2,1)S(1)}, bf16[4,192,768]{2,1,0:T(8,128)(2,1)S(1)}, u32[]{:S(2)}, u32[]{:S(2)}) collective-permute-start(bf16[4,192,768]{2,1,0:T(8,128)(2,1)S(1)} %get-tuple-element.158), channel_id=1, source_target_pairs={{0,8},{1,9},{2,10},{3,11},{4,12},{5,13},{6,14},{7,15},{24,16},{25,... | collective-permute-start | bytes 3538952 | tf_op jit(solution)/shard_map/ppermute | solution.py:41
  600.8 49.3 %collective-permute-start.101 = (bf16[4,192,768]{2,1,0:T(8,128)(2,1)S(1)}, bf16[4,192,768]{2,1,0:T(8,128)(2,1)S(1)}, u32[]{:S(2)}, u32[]{:S(2)}) collective-permute-start(bf16[4,192,768]{2,1,0:T(8,128)(2,1)S(1)} %get-tuple-element.159), channel_id=1, source_target_pairs={{0,8},{1,9},{2,10},{3,11},{4,12},{5,13},{6,14},{7,15},{24,16},{25,... | collective-permute-start | bytes 3538952 | tf_op jit(solution)/shard_map/ppermute | solution.py:41
  613.9 74.4 %collective-permute-start.106 = (bf16[4,160,384]{2,1,0:T(8,128)(2,1)S(1)}, bf16[4,160,384]{2,1,0:T(8,128)(2,1)S(1)}, u32[]{:S(2)}, u32[]{:S(2)}) collective-permute-start(bf16[4,160,384]{2,1,0:T(8,128)(2,1)S(1)} %add_convert_fusion.3), channel_id=1, source_target_pairs={{8,16},{9,17},{10,18},{11,19},{12,20},{13,21},{14,22},{15,23},{16,... | collective-permute-start | bytes 1474568 | tf_op jit(solution)/shard_map/ppermute | solution.py:41
  624.6 29.3 %collective-permute-start.81 = (bf16[128,2560]{1,0:T(8,128)(2,1)S(1)}, bf16[128,2560]{1,0:T(8,128)(2,1)S(1)}, u32[]{:S(2)}, u32[]{:S(2)}) collective-permute-start(bf16[128,2560]{1,0:T(8,128)(2,1)S(1)} %slice.555), channel_id=1, source_target_pairs={{0,2},{1,5},{2,0},{3,7},{4,6},{5,1},{6,4},{7,3},{8,10},{9,13},{10,... | collective-permute-start | bytes 1966088 | tf_op jit(solution)/shard_map/ppermute | solution.py:30
  633.6 27.8 %collective-permute-start.96 = (bf16[128,2560]{1,0:T(8,128)(2,1)S(1)}, bf16[128,2560]{1,0:T(8,128)(2,1)S(1)}, u32[]{:S(2)}, u32[]{:S(2)}) collective-permute-start(bf16[128,2560]{1,0:T(8,128)(2,1)S(1)} %slice.563), channel_id=1, source_target_pairs={{0,2},{1,5},{2,0},{3,7},{4,6},{5,1},{6,4},{7,3},{8,10},{9,13},{10,... | collective-permute-start | bytes 1966088 | tf_op jit(solution)/shard_map/ppermute | solution.py:30
  650.2 39.0 %collective-permute-start.109 = (bf16[4,160,384]{2,1,0:T(8,128)(2,1)S(1)}, bf16[4,160,384]{2,1,0:T(8,128)(2,1)S(1)}, u32[]{:S(2)}, u32[]{:S(2)}) collective-permute-start(bf16[4,160,384]{2,1,0:T(8,128)(2,1)S(1)} %fusion.17), channel_id=1, source_target_pairs={{0,8},{1,9},{2,10},{3,11},{4,12},{5,13},{6,14},{7,15},{8,0},{9,1},... | collective-permute-start | bytes 1474568 | tf_op jit(solution)/shard_map/ppermute | solution.py:41
  654.9 39.4 %collective-permute-start.85 = (bf16[64,2560]{1,0:T(8,128)(2,1)}, bf16[64,2560]{1,0:T(8,128)(2,1)}, u32[]{:S(2)}, u32[]{:S(2)}) collective-permute-start(bf16[64,2560]{1,0:T(8,128)(2,1)} %slice.693), channel_id=1, source_target_pairs={{0,4},{1,3},{2,6},{3,1},{4,0},{5,7},{6,2},{7,5},{8,12},{9,11},{10,... | collective-permute-start | bytes 983048 | tf_op jit(solution)/shard_map/ppermute | solution.py:30
  658.2 38.9 %collective-permute-start.100 = (bf16[4,192,768]{2,1,0:T(8,128)(2,1)}, bf16[4,192,768]{2,1,0:T(8,128)(2,1)}, u32[]{:S(2)}, u32[]{:S(2)}) collective-permute-start(bf16[4,192,768]{2,1,0:T(8,128)(2,1)} %get-tuple-element.156), channel_id=1, source_target_pairs={{8,16},{9,17},{10,18},{11,19},{12,20},{13,21},{14,22},{15,23},{16,... | collective-permute-start | bytes 3538952 | tf_op jit(solution)/shard_map/ppermute | solution.py:41
  661.4 49.9 %collective-permute-start.103 = (bf16[4,192,768]{2,1,0:T(8,128)(2,1)}, bf16[4,192,768]{2,1,0:T(8,128)(2,1)}, u32[]{:S(2)}, u32[]{:S(2)}) collective-permute-start(bf16[4,192,768]{2,1,0:T(8,128)(2,1)} %fusion.14), channel_id=1, source_target_pairs={{0,8},{1,9},{2,10},{3,11},{4,12},{5,13},{6,14},{7,15},{8,0},{9,1},... | collective-permute-start | bytes 3538952 | tf_op jit(solution)/shard_map/ppermute | solution.py:41
  688.3 32.5 %collective-permute-start.82 = (bf16[64,2560]{1,0:T(8,128)(2,1)}, bf16[64,2560]{1,0:T(8,128)(2,1)}, u32[]{:S(2)}, u32[]{:S(2)}) collective-permute-start(bf16[64,2560]{1,0:T(8,128)(2,1)} %slice.694), channel_id=1, source_target_pairs={{0,4},{1,3},{2,6},{3,1},{4,0},{5,7},{6,2},{7,5},{8,12},{9,11},{10,... | collective-permute-start | bytes 983048 | tf_op jit(solution)/shard_map/ppermute | solution.py:30
  689.1 34.1 %collective-permute-start.79 = (bf16[64,2560]{1,0:T(8,128)(2,1)}, bf16[64,2560]{1,0:T(8,128)(2,1)S(1)}, u32[]{:S(2)}, u32[]{:S(2)}) collective-permute-start(bf16[64,2560]{1,0:T(8,128)(2,1)} %slice.695), channel_id=1, source_target_pairs={{0,4},{1,3},{2,6},{3,1},{4,0},{5,7},{6,2},{7,5},{8,12},{9,11},{10,... | collective-permute-start | bytes 983048 | tf_op jit(solution)/shard_map/ppermute | solution.py:30
  690.7 25.7 %all-to-all-start.5 = ((bf16[4,160,384]{2,1,0:T(8,128)(2,1)}), bf16[4,160,384]{2,1,0:T(8,128)(2,1)S(1)}, u32[]{:S(2)}, u32[]{:S(2)}) async-start(bf16[4,160,384]{2,1,0:T(8,128)(2,1)} %fusion.19), calls=%async_computation.5 | async-start | bytes 983040 | tf_op jit(solution)/shard_map/all_to_all | solution.py:134
  694.2 49.8 %collective-permute-start.77 = (bf16[64,2560]{1,0:T(8,128)(2,1)}, bf16[64,2560]{1,0:T(8,128)(2,1)}, u32[]{:S(2)}, u32[]{:S(2)}) collective-permute-start(bf16[64,2560]{1,0:T(8,128)(2,1)} %slice.696), channel_id=1, source_target_pairs={{0,4},{1,3},{2,6},{3,1},{4,0},{5,7},{6,2},{7,5},{8,12},{9,11},{10,... | collective-permute-start | bytes 983048 | tf_op jit(solution)/shard_map/ppermute | solution.py:30
  697.1 43.1 %collective-permute-start.97 = (bf16[64,2560]{1,0:T(8,128)(2,1)}, bf16[64,2560]{1,0:T(8,128)(2,1)}, u32[]{:S(2)}, u32[]{:S(2)}) collective-permute-start(bf16[64,2560]{1,0:T(8,128)(2,1)} %slice.692), channel_id=1, source_target_pairs={{0,4},{1,3},{2,6},{3,1},{4,0},{5,7},{6,2},{7,5},{8,12},{9,11},{10,... | collective-permute-start | bytes 983048 | tf_op jit(solution)/shard_map/ppermute | solution.py:30
  711.3 33.3 %collective-permute-start.86 = (bf16[64,2560]{1,0:T(8,128)(2,1)}, bf16[64,2560]{1,0:T(8,128)(2,1)}, u32[]{:S(2)}, u32[]{:S(2)}) collective-permute-start(bf16[64,2560]{1,0:T(8,128)(2,1)} %fusion.25), channel_id=1, source_target_pairs={{0,24},{1,25},{2,26},{3,27},{4,28},{5,29},{6,30},{7,31},{8,16},{9,... | collective-permute-start | bytes 983048 | tf_op jit(solution)/shard_map/ppermute | solution.py:30
  734.5 58.7 %all-to-all-start.6 = ((bf16[16,160,512]{2,1,0:T(8,128)(2,1)}), bf16[16,160,512]{2,1,0:T(8,128)(2,1)S(1)}, u32[]{:S(2)}, u32[]{:S(2)}) async-start(bf16[16,160,512]{2,1,0:T(8,128)(2,1)} %bitcast.195), calls=%async_computation.6 | async-start | bytes 5242880 | tf_op jit(solution)/shard_map/all_to_all | solution.py:171
  748.8 54.5 %collective-permute-start.104 = (bf16[2,192,768]{2,1,0:T(8,128)(2,1)S(1)}, bf16[2,192,768]{2,1,0:T(8,128)(2,1)}, u32[]{:S(2)}, u32[]{:S(2)}) collective-permute-start(bf16[2,192,768]{2,1,0:T(8,128)(2,1)S(1)} %constant_dynamic-slice_fusion.7), channel_id=1, source_target_pairs={{0,1},{1,0},{2,3},{3,2},{4,5},{5,4},{6,7},{7,6},{8,9},{9,8},{10,11... | collective-permute-start | bytes 1769480 | tf_op jit(solution)/shard_map/ppermute | solution.py:34
  (138 other events, 1499.1 us)
